TPU v7x, 128 devices: a whole 4x4x4 slice. The times are simulated.
128 devices in a mesh: ctx: 32 (over y, z, core), exp: 4 (over x).
Axes of the slice: x: 4, y: 4, z: 4, core: 2. Of those that a mesh axis runs over, the one named last changes fastest.
Arguments:
- inputs: bfloat16 [4096, 4096], P('ctx', 'exp'), may hold values from -6 to 6
- gate_input: bfloat16 [4096, 4096], P('ctx', 'exp')
- b_proj: bfloat16 [4096, 128], P('ctx'), may hold values from -0.5 to 0.5
- c_proj: bfloat16 [4096, 128], P('ctx'), may hold values from -6 to 6
- step_size: float32 [64, 4096], P('exp', 'ctx'), may hold values from 0.03 to 0.3
- decay_rate: float32 [64, 4096], P('exp', 'ctx'), as said below
- skip_gain: float32 [64], P('exp'), may hold values from 0.5 to 2
- start_state: float32 [64, 64, 128], P('exp'), may hold values from -3 to 3
- norm_gain: float32 [4096], P('exp'), may hold values from 0.5 to 1.5
- out_proj: bfloat16 [4096, 4096], P('exp', 'ctx'), may hold values from -0.09375 to 0.09375
- residual: bfloat16 [4096, 4096], P('ctx'), may hold values from -6 to 6
- moe_gain: float32 [4096], replicated, may hold values from 0.5 to 1.5
- w_gate: bfloat16 [32, 4096, 3584], P('ctx', None, 'exp'), may hold values from -0.09375 to 0.09375
- w_up: bfloat16 [32, 4096, 3584], P('ctx', None, 'exp'), may hold values from -0.09375 to 0.09375
- w_down: bfloat16 [32, 3584, 4096], P('ctx', 'exp'), may hold values from -0.0625 to 0.0625
- route_ids: int32 [4096, 2], P('ctx'), may hold values from 0 to 15, all different within a row; in each aligned block of 32 rows (0 to 31, 32 to 63, ...) at most 8 rows name the same one
- route_gates: float32 [4096, 2], P('ctx'), may hold values from 0.3 to 1
Outputs:
- output: bfloat16 [4096, 4096], P(('ctx', 'exp'))
Inputs may be any that keep to these rules, and one draw needn't show every extreme that they name: `route_ids`: each row names two different experts. In each aligned block of 32 rows no expert is named more than 8 times, a bound that some block reaches. `decay_rate`: Non-negative.
All inputs are finite; a program needn't handle non-finite values.
Results may differ from a plain program's by a relative error of at most 0.02.
Values may be sent and summed in bfloat16 or wider, within the bound.
A program may use at most 128 MiB of HBM per device.

v0:
```python
import jax
import jax.numpy as jnp
from jax import lax
from jax.sharding import PartitionSpec as P

PAIR = 2


eps_norm = 1e-05
top_precision = lax.Precision.HIGHEST


def entering(x, axis, join, neutral):
    place = lax.axis_index(axis)
    gathered = jax.tree.map(
        lambda a, kind: lax.all_gather(a.astype(kind), axis), x, (jnp.bfloat16, jnp.bfloat16)
    )
    state = jax.tree.map(lambda a, e: jnp.zeros_like(a) + jnp.asarray(e, a.dtype), x, neutral)

    def one(hop, state):
        return join(
            state,
            jax.tree.map(
                lambda a, own: lax.dynamic_index_in_dim(a, hop, 0, False).astype(own.dtype),
                gathered,
                x,
            ),
        )

    return lax.fori_loop(0, place, one, state)


def later_state(earlier, later):
    first_decay, first_state = earlier
    second_decay, second_state = later
    return (first_decay * second_decay, second_decay[:, None, None] * first_state + second_state)


def route_ranks(quarter_ids, experts):
    flattened = quarter_ids.reshape(-1)
    onehot = (flattened[:, None] == jnp.arange(experts, dtype=jnp.int32)[None, :]).astype(jnp.int32)
    running = jnp.cumsum(onehot, axis=0)
    rank_ids = jnp.sum(onehot * running, axis=1) - 1
    return (flattened, rank_ids)


def place_rows(normed, quarter_ids, experts, capacity):
    flattened, rank_ids = route_ranks(quarter_ids, experts)
    slot_ids = rank_ids * experts + flattened
    matches = (
        jnp.arange(capacity * experts, dtype=jnp.int32)[:, None] == slot_ids[None, :]
    ).astype(jnp.bfloat16)
    doubled = jnp.repeat(normed, quarter_ids.shape[1], axis=0)
    placed = jnp.dot(matches, doubled, preferred_element_type=jnp.float32).astype(jnp.bfloat16)
    return placed.reshape(capacity, experts, normed.shape[1])


def rms_rows(values, gain_vec):
    scaling = lax.rsqrt(jnp.mean(values * values, axis=1, keepdims=True) + eps_norm)
    return (values * scaling * gain_vec[None, :]).astype(jnp.bfloat16)


def local(
    inputs,
    gate_input,
    b_proj,
    c_proj,
    step_size,
    decay_rate,
    skip_gain,
    start_state,
    norm_gain,
    out_proj,
    residual,
    moe_gain,
    w_gate,
    w_up,
    w_down,
    route_ids,
    route_gates,
):
    tok_ctx = inputs.shape[0]
    head_count = step_size.shape[0]
    head_dim = inputs.shape[1] // head_count
    model_width = residual.shape[1]
    n_ctx = lax.axis_size("ctx")
    n_exp = lax.axis_size("exp")
    experts = n_ctx // PAIR
    tok_quarter = tok_ctx // n_exp
    capacity = 4 * tok_quarter // experts
    x_local = inputs.astype(jnp.float32).reshape(tok_ctx, head_count, head_dim)
    b_local = b_proj.astype(jnp.float32)
    c_local = c_proj.astype(jnp.float32)
    cumulative = jnp.cumsum(decay_rate, axis=1)
    span_total = cumulative[:, -1]
    sequence_indices = jnp.arange(tok_ctx, dtype=jnp.int32)
    causal = sequence_indices[:, None] >= sequence_indices[None, :]
    spread = jnp.where(causal[None], cumulative[:, :, None] - cumulative[:, None, :], 0.0)
    scores = jnp.dot(c_local, b_local.T, precision=top_precision)
    mixing = jnp.where(causal[None], jnp.exp(-spread), 0.0) * scores[None] * step_size[:, None, :]
    inside_part = jnp.einsum("hts,shp->thp", mixing, x_local, precision=top_precision)
    ending = jnp.exp(-(span_total[:, None] - cumulative)) * step_size
    local_state = jnp.einsum("hs,shp,sn->hpn", ending, x_local, b_local, precision=top_precision)
    prior_decay, prior_state = entering(
        (jnp.exp(-span_total), local_state),
        "ctx",
        later_state,
        (jnp.ones_like(span_total), jnp.zeros_like(local_state)),
    )
    incoming = prior_state + prior_decay[:, None, None] * start_state
    carried = (
        jnp.einsum("hpn,tn->thp", incoming, c_local, precision=top_precision)
        * jnp.exp(-cumulative).T[:, :, None]
    )
    ssm_out = inside_part + carried + skip_gain[None, :, None] * x_local
    gated_out = ssm_out.reshape(tok_ctx, head_count * head_dim) * jax.nn.silu(
        gate_input.astype(jnp.float32)
    )
    squares = lax.psum(jnp.sum(gated_out * gated_out, axis=1), "exp")
    scaling = lax.rsqrt(squares / (head_count * head_dim * n_exp) + eps_norm)
    normed_mix = (gated_out * scaling[:, None] * norm_gain[None, :]).astype(jnp.bfloat16)
    partial_value = jnp.dot(
        normed_mix,
        lax.all_gather(out_proj, "ctx", axis=1, tiled=True),
        preferred_element_type=jnp.float32,
    )
    gate_rows = w_gate[0]
    up_rows = w_up[0]
    down_rows = w_down[0]
    piece_width = gate_rows.shape[1]
    first_row = lax.axis_index("exp") * tok_quarter
    own_ids = lax.dynamic_slice_in_dim(route_ids, first_row, tok_quarter, 0)
    own_gates = lax.dynamic_slice_in_dim(route_gates, first_row, tok_quarter, 0)
    mixed_all = lax.psum(partial_value.astype(jnp.bfloat16), "exp").astype(jnp.float32)
    hidden_all = residual.astype(jnp.float32) + mixed_all
    moe_all = rms_rows(hidden_all, moe_gain)

    def place_quarter(quarter_rows, quarter_ids):
        return place_rows(quarter_rows, quarter_ids, experts, capacity)

    placed = jax.vmap(place_quarter)(
        moe_all.reshape(n_exp, tok_quarter, model_width),
        route_ids.reshape(n_exp, tok_quarter, route_ids.shape[1]),
    )
    placed = placed.reshape(n_exp * capacity, experts, model_width)
    outgoing = jnp.repeat(placed, PAIR, axis=1)
    arrived = lax.all_to_all(outgoing, "ctx", split_axis=1, concat_axis=1, tiled=True)
    flattened = arrived.reshape(-1, model_width)
    gate_val = jnp.dot(flattened, gate_rows, preferred_element_type=jnp.float32)
    up_val = jnp.dot(flattened, up_rows, preferred_element_type=jnp.float32)
    activated = (jax.nn.silu(gate_val) * up_val).astype(jnp.bfloat16)
    hidden = activated.reshape(arrived.shape[0], arrived.shape[1], piece_width)
    hidden_own = lax.dynamic_slice_in_dim(hidden_all, first_row, tok_quarter, 0)
    product = jnp.dot(
        hidden.reshape(-1, piece_width), down_rows, preferred_element_type=jnp.float32
    )
    rounded = lax.optimization_barrier(product.astype(jnp.bfloat16)).astype(jnp.float32)
    summed = lax.psum_scatter(
        rounded.reshape(lax.axis_size("exp") * capacity, hidden.shape[1], model_width).astype(
            jnp.bfloat16
        ),
        "exp",
        scatter_dimension=0,
        tiled=True,
    )
    halves = lax.all_to_all(summed, "ctx", split_axis=1, concat_axis=1, tiled=True)
    flattened, rank_ids = route_ranks(own_ids, experts)
    base_rows = rank_ids * n_ctx + flattened * PAIR
    fetch_rows = base_rows[:, None] + jnp.arange(PAIR, dtype=jnp.int32)[None, :]
    fetched = halves.reshape(capacity * n_ctx, model_width)[fetch_rows]
    expert_out = jnp.sum(fetched.astype(jnp.float32), axis=1)
    weighted = expert_out * own_gates.reshape(-1)[:, None]
    moe_out = jnp.sum(weighted.reshape(tok_quarter, -1, model_width), axis=1)
    return (hidden_own + moe_out).astype(jnp.bfloat16)


def solution(mesh):
    in_specs = (
        P("ctx", "exp"),
        P("ctx", "exp"),
        P("ctx", None),
        P("ctx", None),
        P("exp", "ctx"),
        P("exp", "ctx"),
        P("exp"),
        P("exp", None, None),
        P("exp"),
        P("exp", "ctx"),
        P("ctx", None),
        P(),
        P("ctx", None, "exp"),
        P("ctx", None, "exp"),
        P("ctx", "exp", None),
        P("ctx", None),
        P("ctx", None),
    )
    out_specs = P(("ctx", "exp"), None)
    return jax.shard_map(local, mesh=mesh, in_specs=in_specs, out_specs=out_specs, check_vma=False)
```

profile of v0, /device:TPU:1, one launch (start us, length us, event | category | flops | bytes accessed | tf_op | source)
XLA Modules:
  0.0 490.3 jit_solution(6920894452097007620)
XLA Ops:
  6.5 1.0 reduce_window_sum.33
  7.5 0.2 slice_reduce_fusion
  7.7 1.1 copy.61
  8.8 0.8 exponential_bitcast_fusion
  9.6 1.1 convolution_convert_fusion.3
  10.8 0.7 all-gather.5.cloned.1.call-update
  11.6 1.2 dynamic-slice
  13.4 0.2 fusion.38
  13.6 0.2 dynamic-update-slice
  13.8 65.5 %all-reduce = bf16[512]{0:T(512)(128)(2,1)S(1)} all-reduce(bf16[512]{0:T(512)(128)(2,1)S(1)} %dynamic-update-slice), channel_id=2, replica_groups=mesh['ctx'=32,'exp'=4] {'ctx'}, use_global_device_ids=true, to_apply=%add | all-reduce | flops 512 | bytes 2048
  79.5 0.9 fusion.42
  80.5 1.2 while.12
  80.5 1.1 convert_add_fusion.3
  81.7 0.5 fusion.9
  82.2 1.4 fusion.8
  83.6 0.2 copy.62
  83.8 0.2 multiply_reduce_fusion.2
  84.1 8.4 %psum.14 = f32[128]{0:T(128)S(1)} all-reduce(f32[128]{0:T(128)S(1)} %multiply_reduce_fusion.2), channel_id=1, replica_groups=mesh['ctx'=32,'exp'=4] {'exp'}, use_global_device_ids=true, to_apply=%region_4.5 | all-reduce | flops 128 | bytes 1024 | tf_op jit(solution)/shard_map/psum | solution.py:119
  92.5 36.7 %all-gather.5.cloned.1.call-done = bf16[1024,4096]{1,0:T(8,128)(2,1)} async-done(((bf16[1024,128]{1,0:T(8,128)(2,1)}), bf16[1024,4096]{1,0:T(8,128)(2,1)}) %all-gather.5.cloned.1.call-update) | async-done | bytes 8388624 | tf_op jit(solution)/shard_map/all_gather | solution.py:124
  129.2 5.8 %convolution_convert_fusion.2 = bf16[128,4096]{1,0:T(8,128)(2,1)} fusion(bf16[1024,4096]{1,0:T(8,128)(2,1)} %all-gather.5.cloned.1.call-done, f32[1024]{0:T(1024)S(1)} %copy-done.12, f32[128]{0:T(128)S(1)} %add_rsqrt_fusion.1, f32[128,1024]{1,0:T(8,128)S(1)} %copy.62, bf16[128,1024]{1,0:T(8,128)(2,1)S(1)} %copy-done.6), kind=kOutput, calls=%fused_computation.10 | convolution fusion | flops 1075445760 | bytes 10228224 | tf_op jit(solution)/shard_map/dot_general | solution.py:122
  135.5 0.1 reduce_window_sum.34
  135.6 0.2 select_reduce_fusion
  135.8 42.9 %all-reduce.3.cloned.1.call-done = bf16[128,4096]{1,0:T(8,128)(2,1)} async-done(((bf16[128,4096]{1,0:T(8,128)(2,1)}), bf16[128,4096]{1,0:T(8,128)(2,1)}) %all-reduce.3.cloned.1.call-update) | async-done | bytes 1048592 | tf_op jit(solution)/shard_map/psum | solution.py:134
  178.8 3.0 convert_add_fusion.1
  181.8 0.4 multiply_convert_fusion.1
  182.2 3.4 broadcast_in_dim.28
  185.7 2.7 reshape.157
  188.4 1.4 convolution_convert_fusion.1
  189.8 2.3 copy.64
  192.1 4.3 broadcast_in_dim.29
  196.3 105.0 %all_to_all.10 = bf16[32,32,4096]{2,0,1:T(8,128)(2,1)} all-to-all(bf16[32,32,4096]{2,0,1:T(8,128)(2,1)} %bitcast.66), channel_id=1, replica_groups=mesh['ctx'=32,'exp'=4] {'ctx'}, dimensions={1} | all-to-all | bytes 16777216 | tf_op jit(solution)/shard_map/all_to_all | solution.py:147
  301.4 11.3 %copy.65 = bf16[32,32,4096]{2,1,0:T(8,128)(2,1)} copy(bf16[32,32,4096]{2,0,1:T(8,128)(2,1)} %all_to_all.10) | data formatting | bytes 16777216 | tf_op jit(solution)/shard_map/all_to_all | solution.py:147
  312.7 13.0 %fusion.1 = f32[1024,896]{1,0:T(8,128)S(1)} fusion(bf16[1024,4096]{1,0:T(8,128)(2,1)} %bitcast.68, bf16[1,4096,896]{2,1,0:T(8,128)(2,1)} %param.32), kind=kOutput, calls=%fused_computation.5 | convolution fusion | flops 7516192768 | bytes 19398656 | tf_op jit(solution)/shard_map/dot_general | solution.py:150
  325.8 9.2 %multiply_convert_fusion = bf16[1024,896]{1,0:T(8,128)(2,1)S(1)} fusion(f32[1024,896]{1,0:T(8,128)S(1)} %fusion.1, bf16[1024,4096]{1,0:T(8,128)(2,1)S(1)} %bitcast.69, bf16[1,4096,896]{2,1,0:T(8,128)(2,1)S(1)} %bitcast.78), kind=kOutput, calls=%fused_computation.11 | convolution fusion | flops 7521697792 | bytes 21233664 | tf_op jit(solution)/shard_map/dot_general | solution.py:149
  335.0 11.2 %convolution_convert_fusion = bf16[1024,4096]{1,0:T(8,128)(2,1)} fusion(bf16[1024,896]{1,0:T(8,128)(2,1)S(1)} %multiply_convert_fusion, bf16[1,896,4096]{2,1,0:T(8,128)(2,1)S(1)} %bitcast.80), kind=kOutput, calls=%fused_computation.3 | convolution fusion | flops 7520387072 | bytes 17563648 | tf_op jit(solution)/shard_map/dot_general | solution.py:154
  346.2 11.3 %copy.74 = bf16[4,8,32,4096]{3,1,2,0:T(8,128)(2,1)} copy(bf16[4,8,32,4096]{3,2,1,0:T(8,128)(2,1)} %bitcast.70) | data formatting | bytes 16777216
  357.5 77.8 %reduce-scatter.4.cloned.1.call-done = bf16[8,131072]{1,0:T(8,128)(2,1)} async-done(((bf16[32,131072]{1,0:T(8,128)(2,1)}), bf16[8,131072]{1,0:T(8,128)(2,1)}) %reduce-scatter.4.cloned.1.call-update) | async-done | bytes 2097168
  435.3 8.1 %all-to-all-start.1 = ((bf16[8,32,4096]{2,0,1:T(8,128)(2,1)}), bf16[8,32,4096]{2,0,1:T(8,128)(2,1)}, u32[]{:S(2)}, u32[]{:S(2)}) async-start(bf16[8,32,4096]{2,0,1:T(8,128)(2,1)} %bitcast.72), calls=%async_computation.1 | async-start | bytes 4194304 | tf_op jit(solution)/shard_map/all_to_all | solution.py:166
  443.9 0.2 select_reduce_fusion.1
  444.2 0.1 reshape.166
  444.5 27.1 %all-to-all-done.1 = bf16[8,32,4096]{2,0,1:T(8,128)(2,1)} async-done(((bf16[8,32,4096]{2,0,1:T(8,128)(2,1)}), bf16[8,32,4096]{2,0,1:T(8,128)(2,1)}, u32[]{:S(2)}, u32[]{:S(2)}) %all-to-all-start.1) | async-done | bytes 2097184 | tf_op jit(solution)/shard_map/all_to_all | solution.py:166
  471.6 2.7 copy.67
  474.3 1.2 gather_fusion
  475.5 1.3 reshape.175
  476.9 2.7 reduce_sum.60
  479.6 0.6 reduce_sum.61
  480.2 1.4 multiply_reduce_fusion.1
  481.7 1.8 add_convert_fusion
  (68 shorter events, 1.5 us)
Async XLA Ops:
  6.5 3.1 copy-start
  6.5 73.9 %all-gather.7.cloned.1.call-start = ((), (), s32[]{:S(2)}) async-start(), calls=%async_computation.5 | async-start | bytes 8650752 | tf_op jit(solution)/shard_map/all_gather | solution.py:16
  10.7 118.4 %all-gather.5.cloned.1.call-start = ((), (), s32[]{:S(2)}) async-start(), calls=%async_computation.3 | async-start | bytes 8650752 | tf_op jit(solution)/shard_map/all_gather | solution.py:124
  11.5 167.3 %all-reduce.3.cloned.1.call-start = ((), (), s32[]{:S(2)}) async-start(), calls=%async_computation.4 | async-start | bytes 2097152 | tf_op jit(solution)/shard_map/psum | solution.py:134
  80.3 1.4 copy-start.5
  80.3 1.4 copy-start.7
  80.5 1.7 copy-start.9
  80.5 1.7 copy-start.13
  81.7 2.1 copy-start.6
  81.7 47.5 %copy-start.12 = (f32[1024]{0:T(1024)S(1)}, f32[1024]{0:T(1024)}, u32[]{:S(2)}) copy-start(f32[1024]{0:T(1024)} %param.27) | copy-start | bytes 12292
  92.5 42.6 %copy-start.10 = (s32[128,2]{0,1:T(2,128)S(1)}, s32[128,2]{0,1:T(2,128)}, u32[]{:S(2)}) copy-start(s32[128,2]{0,1:T(2,128)} %param.34) | copy-start | bytes 3076
  92.5 86.3 %copy-start.3 = (bf16[128,4096]{1,0:T(8,128)(2,1)S(1)}, bf16[128,4096]{1,0:T(8,128)(2,1)}, u32[]{:S(2)}) copy-start(bf16[128,4096]{1,0:T(8,128)(2,1)} %param.29) | copy-start | bytes 3145732
  135.0 46.8 %copy-start.8 = (f32[4096]{0:T(1024)S(1)}, f32[4096]{0:T(1024)}, u32[]{:S(2)}) copy-start(f32[4096]{0:T(1024)} %param.30) | copy-start | bytes 49156
  135.1 300.3 %reduce-scatter.4.cloned.1.call-start = ((), (), s32[]{:S(2)}) async-start(), calls=%async_computation.6 | async-start | bytes 10485760
  178.8 3.0 copy-start.4
  301.4 24.4 %slice-start = ((s8[7340032]{0:T(1024)(128)(4,1)}), s8[3145728]{0:T(1024)(128)(4,1)S(1)}, s32[]{:S(2)}) async-start(s8[7340032]{0:T(1024)(128)(4,1)} %bitcast.77), calls=%async_computation.7 | async-start | bytes 6291456
  312.7 13.0 %copy-start.2 = (bf16[32,32,4096]{2,1,0:T(8,128)(2,1)S(1)}, bf16[32,32,4096]{2,1,0:T(8,128)(2,1)}, u32[]{:S(2)}) copy-start(bf16[32,32,4096]{2,1,0:T(8,128)(2,1)} %copy.65) | copy-start | bytes 25165828
  312.7 13.0 %slice-start.1 = ((s8[7340032]{0:T(1024)(128)(4,1)}), s8[4194304]{0:T(1024)(128)(4,1)S(1)}, s32[]{:S(2)}) async-start(s8[7340032]{0:T(1024)(128)(4,1)} %bitcast.77), calls=%async_computation.8 | async-start | bytes 8388608
  312.7 22.2 %slice-start.2 = ((s8[7340032]{0:T(1024)(128)(4,1)}), s8[4194304]{0:T(1024)(128)(4,1)S(1)}, s32[]{:S(2)}) async-start(s8[7340032]{0:T(1024)(128)(4,1)} %bitcast.79), calls=%async_computation.9 | async-start | bytes 8388608
  325.8 9.2 %slice-start.3 = ((s8[7340032]{0:T(1024)(128)(4,1)}), s8[3145728]{0:T(1024)(128)(4,1)S(1)}, s32[]{:S(2)}) async-start(s8[7340032]{0:T(1024)(128)(4,1)} %bitcast.79), calls=%async_computation.10 | async-start | bytes 6291456
  357.5 86.8 %copy-start.11 = (f32[128,2]{0,1:T(2,128)S(1)}, f32[128,2]{0,1:T(2,128)}, u32[]{:S(2)}) copy-start(f32[128,2]{0,1:T(2,128)} %param.35) | copy-start | bytes 3076
  435.3 36.3 %all-to-all-start.1 = ((bf16[8,32,4096]{2,0,1:T(8,128)(2,1)}), bf16[8,32,4096]{2,0,1:T(8,128)(2,1)}, u32[]{:S(2)}, u32[]{:S(2)}) async-start(bf16[8,32,4096]{2,0,1:T(8,128)(2,1)} %bitcast.72), calls=%async_computation.1 | async-start | bytes 4194304 | tf_op jit(solution)/shard_map/all_to_all | solution.py:166
  475.5 8.0 %copy-start.1 = (bf16[128,128]{1,0:T(8,128)(2,1)S(1)}, bf16[128,128]{1,0:T(8,128)(2,1)}, u32[]{:S(2)}) copy-start(bf16[128,128]{1,0:T(8,128)(2,1)} %param.21) | copy-start | bytes 98308
Sparse Core Ops, SparseCore 0:
  10.9 56.8 all-gather.6
  69.9 59.2 all-gather.4
  135.2 43.5 all-reduce.2
  357.7 77.6 reduce-scatter.3
where the time goes:
time: 500 us; the launch traced here: 490 us
  waiting for transfers between devices  185 us (37%)
  blocking collectives  179 us (36%)
  local copies, waits for them, and re-layouts  45.3 us (9%)
  matrix products  44.4 us (9%)
  between operations  14.4 us (3%)
  other arithmetic  13.7 us (3%)
  starting transfers between devices  8.24 us (2%)
    all_to_all x1, blocking collectives, local(): lax.all_to_all(outgoing, 'ctx', split_axis=1, concat_axis=1, tiled=True)  105 us
    unnamed x5, waiting for transfers between devices  78.5 us
    unnamed x1, blocking collectives  65.5 us
    psum x1, waiting for transfers between devices, local(): lax.psum(partial_value.astype(jnp.bfloat16), 'exp').astype(jnp.float32)  42.9 us
    all_gather x1, waiting for transfers between devices, local(): lax.all_gather(out_proj, 'ctx', axis=1, tiled=True)  36.7 us
    all_to_all x1, waiting for transfers between devices, local(): lax.all_to_all(summed, 'ctx', split_axis=1, concat_axis=1, tiled=True)  27.1 us
    unnamed x42, local copies, waits for them, and re-layouts  14.1 us
    dot_general x1, matrix products, local(): up_val = jnp.dot(flattened, up_rows, preferred_element_type=jnp.float32)  13 us
  transfers between devices with their start and end apart: 5, of which 4 were waited for; matrix products, arithmetic and copies ran while one was open for 2% of the time, Pallas kernels for 0%

commit v1 on v0

--- a/solution.py
+++ b/solution.py
@@ -12,22 +12,18 @@
 
 def entering(x, axis, join, neutral):
     place = lax.axis_index(axis)
-    gathered = jax.tree.map(
-        lambda a, kind: lax.all_gather(a.astype(kind), axis), x, (jnp.bfloat16, jnp.bfloat16)
+    decay, state = x
+    packed = jnp.concatenate(
+        [state, jnp.broadcast_to(decay[:, None, None], (state.shape[0], 1, state.shape[2]))], axis=1
     )
-    state = jax.tree.map(lambda a, e: jnp.zeros_like(a) + jnp.asarray(e, a.dtype), x, neutral)
+    gathered = lax.all_gather(packed.astype(jnp.bfloat16), axis)
+    start = jax.tree.map(lambda a, e: jnp.zeros_like(a) + jnp.asarray(e, a.dtype), x, neutral)
 
-    def one(hop, state):
-        return join(
-            state,
-            jax.tree.map(
-                lambda a, own: lax.dynamic_index_in_dim(a, hop, 0, False).astype(own.dtype),
-                gathered,
-                x,
-            ),
-        )
+    def one(hop, carry):
+        block = lax.dynamic_index_in_dim(gathered, hop, 0, False).astype(jnp.float32)
+        return join(carry, (block[:, -1, 0], block[:, :-1, :]))
 
-    return lax.fori_loop(0, place, one, state)
+    return lax.fori_loop(0, place, one, start)
 
 
 def later_state(earlier, later):

time: 500 us -> 696 us (1.39)
  the two profiles are of different devices: /device:TPU:1 before, /device:TPU:0 now
where the time goes in v1:
time: 696 us; the launch traced here: 688 us
  waiting for transfers between devices  446 us (64%)
  blocking collectives  114 us (16%)
  local copies, waits for them, and re-layouts  49.8 us (7%)
  matrix products  43.4 us (6%)
  between operations  13.8 us (2%)
  other arithmetic  12.4 us (2%)
  starting transfers between devices  8.07 us (1%)
    psum x1, waiting for transfers between devices, local(): lax.psum(partial_value.astype(jnp.bfloat16), 'exp').astype(jnp.float32)  242 us
    all_to_all x1, blocking collectives, local(): lax.all_to_all(outgoing, 'ctx', split_axis=1, concat_axis=1, tiled=True)  103 us
    unnamed x5, waiting for transfers between devices  78.9 us
    all_gather x1, waiting for transfers between devices, entering(): gathered = lax.all_gather(packed.astype(jnp.bfloat16), axis)  54.2 us
    all_gather x1, waiting for transfers between devices, local(): lax.all_gather(out_proj, 'ctx', axis=1, tiled=True)  43.2 us
    all_to_all x1, waiting for transfers between devices, local(): lax.all_to_all(summed, 'ctx', split_axis=1, concat_axis=1, tiled=True)  27.8 us
  transfers between devices with their start and end apart: 5, of which 5 were waited for; matrix products, arithmetic and copies ran while one was open for 1% of the time, Pallas kernels for 0%

profile of v1, /device:TPU:0, one launch (start us, length us, event | category | flops | bytes accessed | tf_op | source)
XLA Modules:
  0.0 687.7 jit_solution(15999288479080339872)
XLA Ops:
  6.5 1.0 reduce_window_sum.33
  7.5 0.2 slice_reduce_fusion
  7.7 0.8 exponential_bitcast_fusion
  8.5 1.1 copy.109
  9.6 0.4 fusion.11
  10.2 0.7 copy.110
  11.0 0.7 all-gather.5.cloned.1.call-update
  11.8 0.9 fusion.42
  12.6 54.2 %all-gather.3.cloned.1.call-done = bf16[32,16,65,128]{3,1,2,0:T(8,128)(2,1)} async-done(((bf16[1,16,65,128]{3,1,2,0:T(8,128)(2,1)}), bf16[32,16,65,128]{3,1,2,0:T(8,128)(2,1)}) %all-gather.3.cloned.1.call-update) | async-done | bytes 8519696 | tf_op jit(solution)/shard_map/all_gather | solution.py:19
  66.9 2.4 broadcast_in_dim.28
  69.4 2.9 copy.112
  72.3 0.5 fusion.10
  72.8 1.4 fusion.9
  74.2 0.2 copy.115
  74.4 0.2 multiply_reduce_fusion.2
  74.7 10.4 %psum.14 = f32[128]{0:T(128)S(1)} all-reduce(f32[128]{0:T(128)S(1)} %multiply_reduce_fusion.2), channel_id=1, replica_groups=mesh['ctx'=32,'exp'=4] {'exp'}, use_global_device_ids=true, to_apply=%region_4.5 | all-reduce | flops 128 | bytes 1024 | tf_op jit(solution)/shard_map/psum | solution.py:115
  85.1 43.2 %all-gather.5.cloned.1.call-done = bf16[1024,4096]{1,0:T(8,128)(2,1)} async-done(((bf16[1024,128]{1,0:T(8,128)(2,1)}), bf16[1024,4096]{1,0:T(8,128)(2,1)}) %all-gather.5.cloned.1.call-update) | async-done | bytes 8388624 | tf_op jit(solution)/shard_map/all_gather | solution.py:120
  128.3 5.8 convolution_convert_fusion.2
  134.1 0.3 reduce-scatter.4.cloned.1.call-start
  134.5 0.1 copy.116
  134.8 0.1 reduce_window_sum.34
  134.9 0.2 select_reduce_fusion
  135.2 242.2 %all-reduce.2.cloned.1.call-done = bf16[128,4096]{1,0:T(8,128)(2,1)} async-done(((bf16[128,4096]{1,0:T(8,128)(2,1)}), bf16[128,4096]{1,0:T(8,128)(2,1)}) %all-reduce.2.cloned.1.call-update) | async-done | bytes 1048592 | tf_op jit(solution)/shard_map/psum | solution.py:130
  377.4 3.0 convert_add_fusion
  380.4 0.4 multiply_convert_fusion.1
  380.8 3.4 broadcast_in_dim.30
  384.3 2.7 reshape.163
  387.0 1.4 convolution_convert_fusion.1
  388.4 2.3 copy.117
  390.7 4.3 broadcast_in_dim.31
  395.0 103.4 %all_to_all.10 = bf16[32,32,4096]{2,0,1:T(8,128)(2,1)} all-to-all(bf16[32,32,4096]{2,0,1:T(8,128)(2,1)} %bitcast.70), channel_id=1, replica_groups=mesh['ctx'=32,'exp'=4] {'ctx'}, dimensions={1} | all-to-all | bytes 16777216 | tf_op jit(solution)/shard_map/all_to_all | solution.py:143
  498.4 11.3 %copy.118 = bf16[32,32,4096]{2,1,0:T(8,128)(2,1)} copy(bf16[32,32,4096]{2,0,1:T(8,128)(2,1)} %all_to_all.10) | data formatting | bytes 16777216 | tf_op jit(solution)/shard_map/all_to_all | solution.py:143
  509.7 12.7 %fusion.2 = f32[1024,896]{1,0:T(8,128)S(1)} fusion(bf16[1024,4096]{1,0:T(8,128)(2,1)} %bitcast.72, bf16[1,4096,896]{2,1,0:T(8,128)(2,1)} %param.32), kind=kOutput, calls=%fused_computation.8 | convolution fusion | flops 7516192768 | bytes 19398656 | tf_op jit(solution)/shard_map/dot_general | solution.py:146
  522.4 9.2 %multiply_convert_fusion = bf16[1024,896]{1,0:T(8,128)(2,1)S(1)} fusion(f32[1024,896]{1,0:T(8,128)S(1)} %fusion.2, bf16[1024,4096]{1,0:T(8,128)(2,1)S(1)} %bitcast.73, bf16[1,4096,896]{2,1,0:T(8,128)(2,1)S(1)} %bitcast.81), kind=kOutput, calls=%fused_computation.14 | convolution fusion | flops 7521697792 | bytes 21233664 | tf_op jit(solution)/shard_map/dot_general | solution.py:145
  531.6 11.3 %convolution_convert_fusion = bf16[1024,4096]{1,0:T(8,128)(2,1)} fusion(bf16[1024,896]{1,0:T(8,128)(2,1)S(1)} %multiply_convert_fusion, bf16[1,896,4096]{2,1,0:T(8,128)(2,1)S(1)} %bitcast.83), kind=kOutput, calls=%fused_computation.6 | convolution fusion | flops 7520387072 | bytes 17563648 | tf_op jit(solution)/shard_map/dot_general | solution.py:150
  542.9 11.3 %copy.130 = bf16[4,8,32,4096]{3,1,2,0:T(8,128)(2,1)} copy(bf16[4,8,32,4096]{3,2,1,0:T(8,128)(2,1)} %bitcast.74) | data formatting | bytes 16777216
  554.2 78.2 %reduce-scatter.4.cloned.1.call-done = bf16[8,131072]{1,0:T(8,128)(2,1)} async-done(((bf16[32,131072]{1,0:T(8,128)(2,1)}), bf16[8,131072]{1,0:T(8,128)(2,1)}) %reduce-scatter.4.cloned.1.call-update) | async-done | bytes 2097168
  632.4 7.7 %all-to-all-start.1 = ((bf16[8,32,4096]{2,0,1:T(8,128)(2,1)}), bf16[8,32,4096]{2,0,1:T(8,128)(2,1)}, u32[]{:S(2)}, u32[]{:S(2)}) async-start(bf16[8,32,4096]{2,0,1:T(8,128)(2,1)} %bitcast.76), calls=%async_computation.1 | async-start | bytes 4194304 | tf_op jit(solution)/shard_map/all_to_all | solution.py:162
  640.5 0.2 select_reduce_fusion.1
  640.8 0.1 reshape.171
  641.1 27.8 %all-to-all-done.1 = bf16[8,32,4096]{2,0,1:T(8,128)(2,1)} async-done(((bf16[8,32,4096]{2,0,1:T(8,128)(2,1)}), bf16[8,32,4096]{2,0,1:T(8,128)(2,1)}, u32[]{:S(2)}, u32[]{:S(2)}) %all-to-all-start.1) | async-done | bytes 2097184 | tf_op jit(solution)/shard_map/all_to_all | solution.py:162
  669.0 2.7 copy.120
  671.7 1.2 gather_fusion
  672.9 1.3 reshape.178
  674.3 2.7 reduce_sum.60
  677.0 0.6 reduce_sum.61
  677.6 1.4 multiply_reduce_fusion.1
  679.1 1.8 add_convert_fusion
  (65 shorter events, 1.3 us)
Async XLA Ops:
  6.5 3.1 copy-start
  6.5 60.3 %all-gather.3.cloned.1.call-start = ((), (), s32[]{:S(2)}) async-start(), calls=%async_computation.3 | async-start | bytes 8785920 | tf_op jit(solution)/shard_map/all_gather | solution.py:19
  10.9 117.4 %all-gather.5.cloned.1.call-start = ((), (), s32[]{:S(2)}) async-start(), calls=%async_computation.4 | async-start | bytes 8650752 | tf_op jit(solution)/shard_map/all_gather | solution.py:120
  11.7 365.7 %all-reduce.2.cloned.1.call-start = ((), (), s32[]{:S(2)}) async-start(), calls=%async_computation.5 | async-start | bytes 2097152 | tf_op jit(solution)/shard_map/psum | solution.py:130
  69.3 3.0 copy-start.5
  69.3 3.0 copy-start.7
  69.3 3.5 copy-start.9
  69.3 3.5 copy-start.13
  69.4 5.1 copy-start.6
  72.3 56.0 %copy-start.12 = (f32[1024]{0:T(1024)S(1)}, f32[1024]{0:T(1024)}, u32[]{:S(2)}) copy-start(f32[1024]{0:T(1024)} %param.27) | copy-start | bytes 12292
  85.1 49.4 %copy-start.10 = (s32[128,2]{0,1:T(2,128)S(1)}, s32[128,2]{0,1:T(2,128)}, u32[]{:S(2)}) copy-start(s32[128,2]{0,1:T(2,128)} %param.34) | copy-start | bytes 3076
  85.1 292.3 %copy-start.3 = (bf16[128,4096]{1,0:T(8,128)(2,1)S(1)}, bf16[128,4096]{1,0:T(8,128)(2,1)}, u32[]{:S(2)}) copy-start(bf16[128,4096]{1,0:T(8,128)(2,1)} %param.29) | copy-start | bytes 3145732
  134.1 246.3 %copy-start.8 = (f32[4096]{0:T(1024)S(1)}, f32[4096]{0:T(1024)}, u32[]{:S(2)}) copy-start(f32[4096]{0:T(1024)} %param.30) | copy-start | bytes 49156
  134.1 498.3 %reduce-scatter.4.cloned.1.call-start = ((), (), s32[]{:S(2)}) async-start(), calls=%async_computation.6 | async-start | bytes 10485760
  377.4 3.0 copy-start.4
  498.4 24.0 %slice-start = ((s8[7340032]{0:T(1024)(128)(4,1)}), s8[3145728]{0:T(1024)(128)(4,1)S(1)}, s32[]{:S(2)}) async-start(s8[7340032]{0:T(1024)(128)(4,1)} %bitcast.80), calls=%async_computation.7 | async-start | bytes 6291456
  509.7 12.7 %copy-start.2 = (bf16[32,32,4096]{2,1,0:T(8,128)(2,1)S(1)}, bf16[32,32,4096]{2,1,0:T(8,128)(2,1)}, u32[]{:S(2)}) copy-start(bf16[32,32,4096]{2,1,0:T(8,128)(2,1)} %copy.118) | copy-start | bytes 25165828
  509.7 12.7 %slice-start.1 = ((s8[7340032]{0:T(1024)(128)(4,1)}), s8[4194304]{0:T(1024)(128)(4,1)S(1)}, s32[]{:S(2)}) async-start(s8[7340032]{0:T(1024)(128)(4,1)} %bitcast.80), calls=%async_computation.8 | async-start | bytes 8388608
  509.7 21.9 %slice-start.2 = ((s8[7340032]{0:T(1024)(128)(4,1)}), s8[4194304]{0:T(1024)(128)(4,1)S(1)}, s32[]{:S(2)}) async-start(s8[7340032]{0:T(1024)(128)(4,1)} %bitcast.82), calls=%async_computation.9 | async-start | bytes 8388608
  522.4 9.2 %slice-start.3 = ((s8[7340032]{0:T(1024)(128)(4,1)}), s8[3145728]{0:T(1024)(128)(4,1)S(1)}, s32[]{:S(2)}) async-start(s8[7340032]{0:T(1024)(128)(4,1)} %bitcast.82), calls=%async_computation.10 | async-start | bytes 6291456
  554.2 86.7 %copy-start.11 = (f32[128,2]{0,1:T(2,128)S(1)}, f32[128,2]{0,1:T(2,128)}, u32[]{:S(2)}) copy-start(f32[128,2]{0,1:T(2,128)} %param.35) | copy-start | bytes 3076
  632.4 36.6 %all-to-all-start.1 = ((bf16[8,32,4096]{2,0,1:T(8,128)(2,1)}), bf16[8,32,4096]{2,0,1:T(8,128)(2,1)}, u32[]{:S(2)}, u32[]{:S(2)}) async-start(bf16[8,32,4096]{2,0,1:T(8,128)(2,1)} %bitcast.76), calls=%async_computation.1 | async-start | bytes 4194304 | tf_op jit(solution)/shard_map/all_to_all | solution.py:162
  672.9 8.0 %copy-start.1 = (bf16[128,128]{1,0:T(8,128)(2,1)S(1)}, bf16[128,128]{1,0:T(8,128)(2,1)}, u32[]{:S(2)}) copy-start(bf16[128,128]{1,0:T(8,128)(2,1)} %param.21) | copy-start | bytes 98308
Sparse Core Ops, SparseCore 0:
  11.0 55.7 all-gather.2
  69.1 59.1 all-gather.4
  134.2 243.1 all-reduce.1
  554.3 78.0 reduce-scatter.3

commit v2 on v1

--- a/solution.py
+++ b/solution.py
@@ -10,26 +10,23 @@
 top_precision = lax.Precision.HIGHEST
 
 
-def entering(x, axis, join, neutral):
+def entering(decay, state, axis):
     place = lax.axis_index(axis)
-    decay, state = x
+    heads, rows, width = state.shape
     packed = jnp.concatenate(
-        [state, jnp.broadcast_to(decay[:, None, None], (state.shape[0], 1, state.shape[2]))], axis=1
+        [state.reshape(heads, rows * width), jnp.broadcast_to(decay[:, None], (heads, width))], axis=1
     )
     gathered = lax.all_gather(packed.astype(jnp.bfloat16), axis)
-    start = jax.tree.map(lambda a, e: jnp.zeros_like(a) + jnp.asarray(e, a.dtype), x, neutral)
-
-    def one(hop, carry):
-        block = lax.dynamic_index_in_dim(gathered, hop, 0, False).astype(jnp.float32)
-        return join(carry, (block[:, -1, 0], block[:, :-1, :]))
-
-    return lax.fori_loop(0, place, one, start)
-
-
-def later_state(earlier, later):
-    first_decay, first_state = earlier
-    second_decay, second_state = later
-    return (first_decay * second_decay, second_decay[:, None, None] * first_state + second_state)
+    decays = gathered[:, :, rows * width].astype(jnp.float32)
+    states = gathered[:, :, : rows * width]
+    order = jnp.arange(gathered.shape[0], dtype=jnp.int32)
+    earlier = order < place
+    between = (order[None, :] > order[:, None]) & earlier[None, :]
+    weights = jnp.prod(jnp.where(between[:, :, None], decays[None, :, :], 1.0), axis=1)
+    weights = jnp.where(earlier[:, None], weights, 0.0)
+    prior_decay = jnp.prod(jnp.where(earlier[:, None], decays, 1.0), axis=0)
+    prior_state = jnp.sum(weights[:, :, None] * states.astype(jnp.float32), axis=0)
+    return prior_decay, prior_state.reshape(heads, rows, width)
 
 
 def route_ranks(quarter_ids, experts):
@@ -97,12 +94,7 @@
     inside_part = jnp.einsum("hts,shp->thp", mixing, x_local, precision=top_precision)
     ending = jnp.exp(-(span_total[:, None] - cumulative)) * step_size
     local_state = jnp.einsum("hs,shp,sn->hpn", ending, x_local, b_local, precision=top_precision)
-    prior_decay, prior_state = entering(
-        (jnp.exp(-span_total), local_state),
-        "ctx",
-        later_state,
-        (jnp.ones_like(span_total), jnp.zeros_like(local_state)),
-    )
+    prior_decay, prior_state = entering(jnp.exp(-span_total), local_state, "ctx")
     incoming = prior_state + prior_decay[:, None, None] * start_state
     carried = (
         jnp.einsum("hpn,tn->thp", incoming, c_local, precision=top_precision)

time: 696 us -> 498 us (0.72)
  waiting for transfers between devices: 446 us -> 240 us
  other arithmetic: 12.4 us -> 19.7 us
    psum x1, waiting for transfers between devices: 242 us -> 44.2 us  [local(): lax.psum(partial_value.astype(jnp.bfloat16), 'exp').astype(jnp.float32)]
    all_gather x1, waiting for transfers between devices: 43.2 us -> 35.3 us  [local(): lax.all_gather(out_proj, 'ctx', axis=1, tiled=True)]
    unnamed x39 -> x41, local copies, waits for them, and re-layouts: 12.6 us -> 15.4 us
  transfers between devices with their start and end apart: 5 -> 5, of which waited for: 5 -> 5; matrix products, arithmetic and copies ran while one was open for 1% -> 4% of each run, Pallas kernels for 0% -> 0%
where the time goes in v2:
time: 498 us; the launch traced here: 490 us
  waiting for transfers between devices  240 us (48%)
  blocking collectives  114 us (23%)
  local copies, waits for them, and re-layouts  50.7 us (10%)
  matrix products  43.4 us (9%)
  other arithmetic  19.7 us (4%)
  between operations  14 us (3%)
  starting transfers between devices  8.34 us (2%)
    all_to_all x1, blocking collectives, local(): lax.all_to_all(outgoing, 'ctx', split_axis=1, concat_axis=1, tiled=True)  103 us
    unnamed x5, waiting for transfers between devices  78.9 us
    all_gather x1, waiting for transfers between devices, entering(): gathered = lax.all_gather(packed.astype(jnp.bfloat16), axis)  54.2 us
    psum x1, waiting for transfers between devices, local(): lax.psum(partial_value.astype(jnp.bfloat16), 'exp').astype(jnp.float32)  44.2 us
    all_gather x1, waiting for transfers between devices, local(): lax.all_gather(out_proj, 'ctx', axis=1, tiled=True)  35.3 us
    all_to_all x1, waiting for transfers between devices, local(): lax.all_to_all(summed, 'ctx', split_axis=1, concat_axis=1, tiled=True)  27.8 us
    unnamed x41, local copies, waits for them, and re-layouts  15.4 us
    dot_general x1, matrix products, local(): up_val = jnp.dot(flattened, up_rows, preferred_element_type=jnp.float32)  12.7 us
  transfers between devices with their start and end apart: 5, of which 5 were waited for; matrix products, arithmetic and copies ran while one was open for 4% of the time, Pallas kernels for 0%

profile of v2, /device:TPU:0, one launch (start us, length us, event | category | flops | bytes accessed | tf_op | source)
XLA Modules:
  0.0 490.2 jit_solution(4317544862249127260)
XLA Ops:
  6.5 1.0 reduce_window_sum.33
  7.7 0.2 fusion.39
  7.9 1.1 copy.82
  9.0 0.8 exponential_bitcast_fusion
  9.8 0.4 convolution_convert_fusion.3
  10.4 0.7 pad_maximum_fusion
  11.2 0.7 all-gather.5.cloned.1.call-update
  12.0 0.9 fusion.42
  12.9 54.2 %all-gather.3.cloned.1.call-done = bf16[32,16,8320]{2,1,0:T(8,128)(2,1)} async-done(((bf16[1,16,8320]{2,1,0:T(8,128)(2,1)}), bf16[32,16,8320]{2,1,0:T(8,128)(2,1)}) %all-gather.3.cloned.1.call-update) | async-done | bytes 8519696 | tf_op jit(solution)/shard_map/all_gather | solution.py:19
  67.1 0.9 slice.15
  68.0 0.2 copy.100
  68.3 0.6 select_reduce_fusion
  69.0 5.7 %multiply_reduce_fusion = f32[16,8192]{1,0:T(8,128)S(1)} fusion(bf16[32,16,8320]{2,1,0:T(8,128)(2,1)} %all-gather.3.cloned.1.call-done, f32[32,16]{1,0:T(8,128)S(1)} %get-tuple-element.10), kind=kLoop, calls=%fused_computation.1 | loop fusion | flops 12451840 | bytes 8914944 | tf_op jit(solution)/shard_map/reduce_sum | solution.py:28
  74.8 2.6 copy.98
  77.4 3.0 copy.86
  80.5 0.5 fusion.9
  80.9 1.4 fusion.8
  82.3 0.2 copy.87
  82.6 0.2 multiply_reduce_fusion.3
  82.8 10.4 %psum.14 = f32[128]{0:T(128)S(1)} all-reduce(f32[128]{0:T(128)S(1)} %multiply_reduce_fusion.3), channel_id=1, replica_groups=mesh['ctx'=32,'exp'=4] {'exp'}, use_global_device_ids=true, to_apply=%region_5.6 | all-reduce | flops 128 | bytes 1024 | tf_op jit(solution)/shard_map/psum | solution.py:107
  93.2 35.3 %all-gather.5.cloned.1.call-done = bf16[1024,4096]{1,0:T(8,128)(2,1)} async-done(((bf16[1024,128]{1,0:T(8,128)(2,1)}), bf16[1024,4096]{1,0:T(8,128)(2,1)}) %all-gather.5.cloned.1.call-update) | async-done | bytes 8388624 | tf_op jit(solution)/shard_map/all_gather | solution.py:112
  128.5 5.8 %convolution_convert_fusion.2 = bf16[128,4096]{1,0:T(8,128)(2,1)} fusion(bf16[1024,4096]{1,0:T(8,128)(2,1)} %all-gather.5.cloned.1.call-done, f32[1024]{0:T(1024)S(1)} %copy-done.12, f32[128]{0:T(128)S(1)} %add_rsqrt_fusion.1, f32[128,1024]{1,0:T(8,128)S(1)} %copy.87, bf16[128,1024]{1,0:T(8,128)(2,1)S(1)} %copy-done.6), kind=kOutput, calls=%fused_computation.9 | convolution fusion | flops 1075445760 | bytes 10228224 | tf_op jit(solution)/shard_map/dot_general | solution.py:110
  134.3 0.6 reduce-scatter.4.cloned.1.call-start
  135.4 0.2 select_reduce_fusion.1
  135.6 44.2 %all-reduce.2.cloned.1.call-done = bf16[128,4096]{1,0:T(8,128)(2,1)} async-done(((bf16[128,4096]{1,0:T(8,128)(2,1)}), bf16[128,4096]{1,0:T(8,128)(2,1)}) %all-reduce.2.cloned.1.call-update) | async-done | bytes 1048592 | tf_op jit(solution)/shard_map/psum | solution.py:122
  179.8 3.0 convert_add_fusion
  182.9 0.4 multiply_convert_fusion.1
  183.3 3.4 broadcast_in_dim.107
  186.7 2.7 reshape.232
  189.5 1.4 convolution_convert_fusion.1
  190.8 2.3 copy.89
  193.1 4.3 broadcast_in_dim.108
  197.4 103.1 %all_to_all.10 = bf16[32,32,4096]{2,0,1:T(8,128)(2,1)} all-to-all(bf16[32,32,4096]{2,0,1:T(8,128)(2,1)} %bitcast.59), channel_id=1, replica_groups=mesh['ctx'=32,'exp'=4] {'ctx'}, dimensions={1} | all-to-all | bytes 16777216 | tf_op jit(solution)/shard_map/all_to_all | solution.py:135
  300.5 11.3 %copy.90 = bf16[32,32,4096]{2,1,0:T(8,128)(2,1)} copy(bf16[32,32,4096]{2,0,1:T(8,128)(2,1)} %all_to_all.10) | data formatting | bytes 16777216 | tf_op jit(solution)/shard_map/all_to_all | solution.py:135
  311.8 12.7 %fusion.1 = f32[1024,896]{1,0:T(8,128)S(1)} fusion(bf16[1024,4096]{1,0:T(8,128)(2,1)} %bitcast.62, bf16[1,4096,896]{2,1,0:T(8,128)(2,1)} %param.30), kind=kOutput, calls=%fused_computation.4 | convolution fusion | flops 7516192768 | bytes 19398656 | tf_op jit(solution)/shard_map/dot_general | solution.py:138
  324.6 9.2 %multiply_convert_fusion = bf16[1024,896]{1,0:T(8,128)(2,1)S(1)} fusion(f32[1024,896]{1,0:T(8,128)S(1)} %fusion.1, bf16[1024,4096]{1,0:T(8,128)(2,1)S(1)} %bitcast.63, bf16[1,4096,896]{2,1,0:T(8,128)(2,1)S(1)} %bitcast.71), kind=kOutput, calls=%fused_computation.10 | convolution fusion | flops 7521697792 | bytes 21233664 | tf_op jit(solution)/shard_map/dot_general | solution.py:137
  333.8 11.3 %convolution_convert_fusion = bf16[1024,4096]{1,0:T(8,128)(2,1)} fusion(bf16[1024,896]{1,0:T(8,128)(2,1)S(1)} %multiply_convert_fusion, bf16[1,896,4096]{2,1,0:T(8,128)(2,1)S(1)} %bitcast.73), kind=kOutput, calls=%fused_computation.2 | convolution fusion | flops 7520387072 | bytes 17563648 | tf_op jit(solution)/shard_map/dot_general | solution.py:142
  345.1 11.3 %copy.101 = bf16[4,8,32,4096]{3,1,2,0:T(8,128)(2,1)} copy(bf16[4,8,32,4096]{3,2,1,0:T(8,128)(2,1)} %bitcast.64) | data formatting | bytes 16777216
  356.4 78.2 %reduce-scatter.4.cloned.1.call-done = bf16[8,131072]{1,0:T(8,128)(2,1)} async-done(((bf16[32,131072]{1,0:T(8,128)(2,1)}), bf16[8,131072]{1,0:T(8,128)(2,1)}) %reduce-scatter.4.cloned.1.call-update) | async-done | bytes 2097168
  434.6 7.7 %all-to-all-start.1 = ((bf16[8,32,4096]{2,0,1:T(8,128)(2,1)}), bf16[8,32,4096]{2,0,1:T(8,128)(2,1)}, u32[]{:S(2)}, u32[]{:S(2)}) async-start(bf16[8,32,4096]{2,0,1:T(8,128)(2,1)} %bitcast.66), calls=%async_computation.1 | async-start | bytes 4194304 | tf_op jit(solution)/shard_map/all_to_all | solution.py:154
  443.4 27.8 %all-to-all-done.1 = bf16[8,32,4096]{2,0,1:T(8,128)(2,1)} async-done(((bf16[8,32,4096]{2,0,1:T(8,128)(2,1)}), bf16[8,32,4096]{2,0,1:T(8,128)(2,1)}, u32[]{:S(2)}, u32[]{:S(2)}) %all-to-all-start.1) | async-done | bytes 2097184 | tf_op jit(solution)/shard_map/all_to_all | solution.py:154
  471.2 2.7 copy.92
  473.9 1.2 gather_fusion
  475.2 1.3 reshape.248
  476.5 2.7 reduce_sum.70
  479.2 0.6 reduce_sum.71
  479.8 1.4 multiply_reduce_fusion.2
  481.3 1.8 add_convert_fusion
  (72 shorter events, 2.3 us)
Async XLA Ops:
  6.5 3.3 copy-start
  6.5 60.6 %all-gather.3.cloned.1.call-start = ((), (), s32[]{:S(2)}) async-start(), calls=%async_computation.3 | async-start | bytes 8785920 | tf_op jit(solution)/shard_map/all_gather | solution.py:19
  11.2 117.3 %all-gather.5.cloned.1.call-start = ((), (), s32[]{:S(2)}) async-start(), calls=%async_computation.4 | async-start | bytes 8650752 | tf_op jit(solution)/shard_map/all_gather | solution.py:112
  11.9 167.9 %all-reduce.2.cloned.1.call-start = ((), (), s32[]{:S(2)}) async-start(), calls=%async_computation.5 | async-start | bytes 2097152 | tf_op jit(solution)/shard_map/psum | solution.py:122
  74.8 5.7 %copy-start.5 = (f32[16,64,128]{2,1,0:T(8,128)S(1)}, f32[16,64,128]{2,1,0:T(8,128)}, u32[]{:S(2)}) copy-start(f32[16,64,128]{2,1,0:T(8,128)} %param.24) | copy-start | bytes 1572868
  74.8 5.7 %copy-start.7 = (bf16[128,128]{1,0:T(8,128)(2,1)S(1)}, bf16[128,128]{1,0:T(8,128)(2,1)}, u32[]{:S(2)}) copy-start(bf16[128,128]{1,0:T(8,128)(2,1)} %param.20) | copy-start | bytes 98308
  77.4 3.6 copy-start.9
  77.4 3.6 copy-start.13
  77.4 5.2 %copy-start.6 = (bf16[128,1024]{1,0:T(8,128)(2,1)S(1)}, bf16[128,1024]{1,0:T(8,128)(2,1)}, u32[]{:S(2)}) copy-start(bf16[128,1024]{1,0:T(8,128)(2,1)} %param.18) | copy-start | bytes 786436
  80.4 48.1 %copy-start.12 = (f32[1024]{0:T(1024)S(1)}, f32[1024]{0:T(1024)}, u32[]{:S(2)}) copy-start(f32[1024]{0:T(1024)} %param.25) | copy-start | bytes 12292
  93.2 41.7 %copy-start.10 = (s32[128,2]{0,1:T(2,128)S(1)}, s32[128,2]{0,1:T(2,128)}, u32[]{:S(2)}) copy-start(s32[128,2]{0,1:T(2,128)} %param.32) | copy-start | bytes 3076
  93.2 86.6 %copy-start.3 = (bf16[128,4096]{1,0:T(8,128)(2,1)S(1)}, bf16[128,4096]{1,0:T(8,128)(2,1)}, u32[]{:S(2)}) copy-start(bf16[128,4096]{1,0:T(8,128)(2,1)} %param.27) | copy-start | bytes 3145732
  134.3 48.5 %copy-start.8 = (f32[4096]{0:T(1024)S(1)}, f32[4096]{0:T(1024)}, u32[]{:S(2)}) copy-start(f32[4096]{0:T(1024)} %param.28) | copy-start | bytes 49156
  134.3 300.3 %reduce-scatter.4.cloned.1.call-start = ((), (), s32[]{:S(2)}) async-start(), calls=%async_computation.6 | async-start | bytes 10485760
  179.8 3.0 copy-start.4
  300.5 24.0 %slice-start = ((s8[7340032]{0:T(1024)(128)(4,1)}), s8[3145728]{0:T(1024)(128)(4,1)S(1)}, s32[]{:S(2)}) async-start(s8[7340032]{0:T(1024)(128)(4,1)} %bitcast.70), calls=%async_computation.7 | async-start | bytes 6291456
  311.8 12.7 %copy-start.2 = (bf16[32,32,4096]{2,1,0:T(8,128)(2,1)S(1)}, bf16[32,32,4096]{2,1,0:T(8,128)(2,1)}, u32[]{:S(2)}) copy-start(bf16[32,32,4096]{2,1,0:T(8,128)(2,1)} %copy.90) | copy-start | bytes 25165828
  311.8 12.7 %slice-start.1 = ((s8[7340032]{0:T(1024)(128)(4,1)}), s8[4194304]{0:T(1024)(128)(4,1)S(1)}, s32[]{:S(2)}) async-start(s8[7340032]{0:T(1024)(128)(4,1)} %bitcast.70), calls=%async_computation.8 | async-start | bytes 8388608
  311.8 21.9 %slice-start.2 = ((s8[7340032]{0:T(1024)(128)(4,1)}), s8[4194304]{0:T(1024)(128)(4,1)S(1)}, s32[]{:S(2)}) async-start(s8[7340032]{0:T(1024)(128)(4,1)} %bitcast.72), calls=%async_computation.9 | async-start | bytes 8388608
  324.6 9.2 %slice-start.3 = ((s8[7340032]{0:T(1024)(128)(4,1)}), s8[3145728]{0:T(1024)(128)(4,1)S(1)}, s32[]{:S(2)}) async-start(s8[7340032]{0:T(1024)(128)(4,1)} %bitcast.72), calls=%async_computation.10 | async-start | bytes 6291456
  356.4 86.8 %copy-start.11 = (f32[128,2]{0,1:T(2,128)S(1)}, f32[128,2]{0,1:T(2,128)}, u32[]{:S(2)}) copy-start(f32[128,2]{0,1:T(2,128)} %param.33) | copy-start | bytes 3076
  434.6 36.6 %all-to-all-start.1 = ((bf16[8,32,4096]{2,0,1:T(8,128)(2,1)}), bf16[8,32,4096]{2,0,1:T(8,128)(2,1)}, u32[]{:S(2)}, u32[]{:S(2)}) async-start(bf16[8,32,4096]{2,0,1:T(8,128)(2,1)} %bitcast.66), calls=%async_computation.1 | async-start | bytes 4194304 | tf_op jit(solution)/shard_map/all_to_all | solution.py:154
  475.1 8.0 %copy-start.1 = (bf16[128,128]{1,0:T(8,128)(2,1)S(1)}, bf16[128,128]{1,0:T(8,128)(2,1)}, u32[]{:S(2)}) copy-start(bf16[128,128]{1,0:T(8,128)(2,1)} %param.19) | copy-start | bytes 98308
Sparse Core Ops, SparseCore 0:
  11.3 55.7 all-gather.2
  69.3 59.1 all-gather.4
  134.5 45.3 all-reduce.1
  356.5 78.0 reduce-scatter.3

commit v3 on v2

--- a/solution.py
+++ b/solution.py
@@ -10,23 +10,34 @@
 top_precision = lax.Precision.HIGHEST
 
 
+def combine(earlier, later):
+    first_decay, first_state = earlier
+    second_decay, second_state = later
+    return (first_decay * second_decay, second_decay[:, None, None] * first_state + second_state)
+
+
 def entering(decay, state, axis):
     place = lax.axis_index(axis)
+    count = lax.axis_size(axis)
     heads, rows, width = state.shape
-    packed = jnp.concatenate(
-        [state.reshape(heads, rows * width), jnp.broadcast_to(decay[:, None], (heads, width))], axis=1
-    )
-    gathered = lax.all_gather(packed.astype(jnp.bfloat16), axis)
-    decays = gathered[:, :, rows * width].astype(jnp.float32)
-    states = gathered[:, :, : rows * width]
-    order = jnp.arange(gathered.shape[0], dtype=jnp.int32)
-    earlier = order < place
-    between = (order[None, :] > order[:, None]) & earlier[None, :]
-    weights = jnp.prod(jnp.where(between[:, :, None], decays[None, :, :], 1.0), axis=1)
-    weights = jnp.where(earlier[:, None], weights, 0.0)
-    prior_decay = jnp.prod(jnp.where(earlier[:, None], decays, 1.0), axis=0)
-    prior_state = jnp.sum(weights[:, :, None] * states.astype(jnp.float32), axis=0)
-    return prior_decay, prior_state.reshape(heads, rows, width)
+    inclusive = (decay, state)
+    exclusive = (jnp.ones_like(decay), jnp.zeros_like(state))
+    hop = 1
+    while hop < count:
+        packed = jnp.concatenate(
+            [inclusive[1].reshape(heads, rows * width), jnp.broadcast_to(inclusive[0][:, None], (heads, width))],
+            axis=1,
+        ).astype(jnp.bfloat16)
+        got = lax.ppermute(packed, axis, [(i, i + hop) for i in range(count - hop)]).astype(jnp.float32)
+        valid = place >= hop
+        arrived = (
+            jnp.where(valid, got[:, rows * width], 1.0),
+            jnp.where(valid, got[:, : rows * width], 0.0).reshape(heads, rows, width),
+        )
+        inclusive = combine(arrived, inclusive)
+        exclusive = combine(arrived, exclusive)
+        hop *= 2
+    return exclusive
 
 
 def route_ranks(quarter_ids, experts):
@@ -104,14 +115,22 @@
     gated_out = ssm_out.reshape(tok_ctx, head_count * head_dim) * jax.nn.silu(
         gate_input.astype(jnp.float32)
     )
-    squares = lax.psum(jnp.sum(gated_out * gated_out, axis=1), "exp")
-    scaling = lax.rsqrt(squares / (head_count * head_dim * n_exp) + eps_norm)
-    normed_mix = (gated_out * scaling[:, None] * norm_gain[None, :]).astype(jnp.bfloat16)
+    squares = jnp.sum(gated_out * gated_out, axis=1)
+    unscaled_mix = (gated_out * norm_gain[None, :]).astype(jnp.bfloat16)
     partial_value = jnp.dot(
-        normed_mix,
+        unscaled_mix,
         lax.all_gather(out_proj, "ctx", axis=1, tiled=True),
         preferred_element_type=jnp.float32,
     )
+    width_out = partial_value.shape[1]
+    summed_parts = lax.psum(
+        jnp.concatenate(
+            [partial_value, jnp.broadcast_to(squares[:, None], (tok_ctx, 128))], axis=1
+        ).astype(jnp.bfloat16),
+        "exp",
+    ).astype(jnp.float32)
+    scaling = lax.rsqrt(summed_parts[:, width_out] / (head_count * head_dim * n_exp) + eps_norm)
+    mixed_all = summed_parts[:, :width_out] * scaling[:, None]
     gate_rows = w_gate[0]
     up_rows = w_up[0]
     down_rows = w_down[0]
@@ -119,7 +138,6 @@
     first_row = lax.axis_index("exp") * tok_quarter
     own_ids = lax.dynamic_slice_in_dim(route_ids, first_row, tok_quarter, 0)
     own_gates = lax.dynamic_slice_in_dim(route_gates, first_row, tok_quarter, 0)
-    mixed_all = lax.psum(partial_value.astype(jnp.bfloat16), "exp").astype(jnp.float32)
     hidden_all = residual.astype(jnp.float32) + mixed_all
     moe_all = rms_rows(hidden_all, moe_gain)
 

time: 498 us -> 452 us (0.908)
  waiting for transfers between devices: 240 us -> 177 us
  starting transfers between devices: 8.34 us -> 40.5 us
  blocking collectives: 114 us -> 103 us
    all_gather x1 -> x0, waiting for transfers between devices: 54.2 us -> none  [entering(): gathered = lax.all_gather(packed.astype(jnp.bfloat16), axis)]
    all_gather x1, waiting for transfers between devices: 35.3 us -> 0.38 us  [local(): lax.all_gather(out_proj, 'ctx', axis=1, tiled=True)]
    ppermute x0 -> x5, starting transfers between devices: none -> 32.5 us  [entering(): lax.ppermute(packed, axis, [(i, i + hop) for i in range(count - hop)])]
    ppermute x0 -> x5, waiting for transfers between devices: none -> 22.8 us  [entering(): lax.ppermute(packed, axis, [(i, i + hop) for i in range(count - hop)])]
    psum x1 -> x0, blocking collectives: 10.4 us -> none  [local(): squares = lax.psum(jnp.sum(gated_out * gated_out, axis=1), 'exp')]
    reduce_sum x2, other arithmetic: 5.97 us -> 0.84 us  [the longest x1 0.59 us: rms_rows(): jnp.mean(values * values, axis=1, keepdims=True) + eps_norm]
    unnamed x41 -> x57, local copies, waits for them, and re-layouts: 15.4 us -> 16.7 us
    unnamed x5 -> x4, waiting for transfers between devices: 78.9 us -> 78.9 us
  transfers between devices with their start and end apart: 5 -> 9, of which waited for: 5 -> 9; matrix products, arithmetic and copies ran while one was open for 4% -> 4% of each run, Pallas kernels for 0% -> 0%
where the time goes in v3:
time: 452 us; the launch traced here: 445 us
  waiting for transfers between devices  177 us (39%)
  blocking collectives  103 us (23%)
  local copies, waits for them, and re-layouts  48.2 us (11%)
  matrix products  42.1 us (9%)
  starting transfers between devices  40.5 us (9%)
  other arithmetic  19.8 us (4%)
  between operations  14.1 us (3%)
    all_to_all x1, blocking collectives, local(): lax.all_to_all(outgoing, 'ctx', split_axis=1, concat_axis=1, tiled=True)  103 us
    unnamed x4, waiting for transfers between devices  78.9 us
    psum x1, waiting for transfers between devices, local(): lax.psum(jnp.concatenate([partial_value, jnp.broadcast_to(squares[:, None...  46.8 us
    ppermute x5, starting transfers between devices, entering(): lax.ppermute(packed, axis, [(i, i + hop) for i in range(count - hop)])  32.5 us
    all_to_all x1, waiting for transfers between devices, local(): lax.all_to_all(summed, 'ctx', split_axis=1, concat_axis=1, tiled=True)  27.8 us
    ppermute x5, waiting for transfers between devices, entering(): lax.ppermute(packed, axis, [(i, i + hop) for i in range(count - hop)])  22.8 us
    unnamed x57, local copies, waits for them, and re-layouts  16.7 us
    dot_general x1, matrix products, local(): up_val = jnp.dot(flattened, up_rows, preferred_element_type=jnp.float32)  12.7 us
  transfers between devices with their start and end apart: 9, of which 9 were waited for; matrix products, arithmetic and copies ran while one was open for 4% of the time, Pallas kernels for 0%

profile of v3, /device:TPU:0, one launch (start us, length us, event | category | flops | bytes accessed | tf_op | source)
XLA Modules:
  0.0 444.8 jit_solution(16321302196685559610)
XLA Ops:
  6.5 0.7 all-gather.2.cloned.1.call-update
  7.3 1.1 copy.61
  8.4 1.0 reduce_window_sum.33
  9.6 1.3 exponential_bitcast_fusion
  11.8 1.3 collective-permute-start
  13.1 1.1 collective-permute-done
  15.7 9.2 %collective-permute-start.1 = (bf16[16,8320]{1,0:T(8,128)(2,1)S(1)}, bf16[16,8320]{1,0:T(8,128)(2,1)S(1)}, u32[]{:S(2)}, u32[]{:S(2)}) collective-permute-start(bf16[16,8320]{1,0:T(8,128)(2,1)S(1)} %pad_maximum_fusion.2), channel_id=1, source_target_pairs={{0,8},{4,12},{8,16},{12,20},{16,24},{20,28},{24,32},{28,36},{32,40... | collective-permute-start | bytes 798728 | tf_op jit(solution)/shard_map/ppermute | solution.py:31
  24.9 6.7 %collective-permute-done.1 = bf16[16,8320]{1,0:T(8,128)(2,1)S(1)} collective-permute-done((bf16[16,8320]{1,0:T(8,128)(2,1)S(1)}, bf16[16,8320]{1,0:T(8,128)(2,1)S(1)}, u32[]{:S(2)}, u32[]{:S(2)}) %collective-permute-start.1) | collective-permute-done | bytes 266272 | tf_op jit(solution)/shard_map/ppermute | solution.py:31
  32.7 6.1 %collective-permute-start.2 = (bf16[16,8320]{1,0:T(8,128)(2,1)S(1)}, bf16[16,8320]{1,0:T(8,128)(2,1)S(1)}, u32[]{:S(2)}, u32[]{:S(2)}) collective-permute-start(bf16[16,8320]{1,0:T(8,128)(2,1)S(1)} %pad_maximum_fusion.3), channel_id=1, source_target_pairs={{0,16},{4,20},{8,24},{12,28},{16,32},{20,36},{24,40},{28,44},{32,4... | collective-permute-start | bytes 798728 | tf_op jit(solution)/shard_map/ppermute | solution.py:31
  38.7 0.8 fusion.60
  39.6 3.1 collective-permute-done.2
  44.0 0.7 pad_maximum_fusion.4
  44.7 8.3 %collective-permute-start.3 = (bf16[16,8320]{1,0:T(8,128)(2,1)}, bf16[16,8320]{1,0:T(8,128)(2,1)S(1)}, u32[]{:S(2)}, u32[]{:S(2)}) collective-permute-start(bf16[16,8320]{1,0:T(8,128)(2,1)} %pad_maximum_fusion.4), channel_id=1, source_target_pairs={{0,32},{4,36},{8,40},{12,44},{16,48},{20,52},{24,56},{28,60},{32,6... | collective-permute-start | bytes 798728 | tf_op jit(solution)/shard_map/ppermute | solution.py:31
  53.0 6.3 %collective-permute-done.3 = bf16[16,8320]{1,0:T(8,128)(2,1)S(1)} collective-permute-done((bf16[16,8320]{1,0:T(8,128)(2,1)}, bf16[16,8320]{1,0:T(8,128)(2,1)S(1)}, u32[]{:S(2)}, u32[]{:S(2)}) %collective-permute-start.3) | collective-permute-done | bytes 266272 | tf_op jit(solution)/shard_map/ppermute | solution.py:31
  60.3 7.6 %collective-permute-start.4 = (bf16[16,8320]{1,0:T(8,128)(2,1)S(1)}, bf16[16,8320]{1,0:T(8,128)(2,1)S(1)}, u32[]{:S(2)}, u32[]{:S(2)}) collective-permute-start(bf16[16,8320]{1,0:T(8,128)(2,1)S(1)} %pad_maximum_fusion.5), channel_id=1, source_target_pairs={{0,64},{4,68},{8,72},{12,76},{16,80},{20,84},{24,88},{28,92},{32,9... | collective-permute-start | bytes 798728 | tf_op jit(solution)/shard_map/ppermute | solution.py:31
  68.1 0.8 fusion.63
  69.0 5.5 %collective-permute-done.4 = bf16[16,8320]{1,0:T(8,128)(2,1)S(1)} collective-permute-done((bf16[16,8320]{1,0:T(8,128)(2,1)S(1)}, bf16[16,8320]{1,0:T(8,128)(2,1)S(1)}, u32[]{:S(2)}, u32[]{:S(2)}) %collective-permute-start.4) | collective-permute-done | bytes 266272 | tf_op jit(solution)/shard_map/ppermute | solution.py:31
  74.8 0.7 fusion.71
  75.5 1.5 fusion.24
  77.1 1.1 fusion.10
  78.2 1.4 fusion.9
  80.4 4.7 %convolution_convert_fusion.2 = bf16[128,4096]{1,0:T(8,128)(2,1)S(1)} fusion(bf16[1024,4096]{1,0:T(8,128)(2,1)} %all-gather.2.cloned.1.call-done, f32[1024]{0:T(1024)S(1)} %copy-done.16, f32[128,1024]{1,0:T(8,128)S(1)} %copy.62, bf16[128,1024]{1,0:T(8,128)(2,1)S(1)} %copy-done.7), kind=kOutput, calls=%fused_computation.8 | convolution fusion | flops 1075314688 | bytes 10227712 | tf_op jit(solution)/shard_map/dot_general | solution.py:120
  85.2 1.1 pad_maximum_fusion
  87.4 46.8 %all-reduce.2.cloned.1.call-done = bf16[128,4224]{1,0:T(8,128)(2,1)} async-done(((bf16[128,4224]{1,0:T(8,128)(2,1)}), bf16[128,4224]{1,0:T(8,128)(2,1)}) %all-reduce.2.cloned.1.call-update) | async-done | bytes 1081360 | tf_op jit(solution)/shard_map/psum | solution.py:126
  134.2 1.4 convert_element_type.74
  135.7 0.6 multiply_reduce_fusion
  136.3 1.3 copy-done.2
  137.9 3.4 broadcast_in_dim.131
  141.4 2.7 reshape.283
  144.1 1.4 convolution_convert_fusion.1
  145.5 2.3 copy.64
  147.8 4.3 broadcast_in_dim.132
  152.1 103.4 %all_to_all.10 = bf16[32,32,4096]{2,0,1:T(8,128)(2,1)} all-to-all(bf16[32,32,4096]{2,0,1:T(8,128)(2,1)} %bitcast.138), channel_id=1, replica_groups=mesh['ctx'=32,'exp'=4] {'ctx'}, dimensions={1} | all-to-all | bytes 16777216 | tf_op jit(solution)/shard_map/all_to_all | solution.py:153
  255.5 11.3 %copy.65 = bf16[32,32,4096]{2,1,0:T(8,128)(2,1)} copy(bf16[32,32,4096]{2,0,1:T(8,128)(2,1)} %all_to_all.10) | data formatting | bytes 16777216 | tf_op jit(solution)/shard_map/all_to_all | solution.py:153
  266.8 12.7 %fusion.1 = f32[1024,896]{1,0:T(8,128)S(1)} fusion(bf16[1024,4096]{1,0:T(8,128)(2,1)} %bitcast.140, bf16[1,4096,896]{2,1,0:T(8,128)(2,1)} %param.30), kind=kOutput, calls=%fused_computation.3 | convolution fusion | flops 7516192768 | bytes 19398656 | tf_op jit(solution)/shard_map/dot_general | solution.py:156
  279.5 9.2 %multiply_convert_fusion = bf16[1024,896]{1,0:T(8,128)(2,1)S(1)} fusion(f32[1024,896]{1,0:T(8,128)S(1)} %fusion.1, bf16[1024,4096]{1,0:T(8,128)(2,1)S(1)} %bitcast.141, bf16[1,4096,896]{2,1,0:T(8,128)(2,1)S(1)} %bitcast.159), kind=kOutput, calls=%fused_computation.9 | convolution fusion | flops 7521697792 | bytes 21233664 | tf_op jit(solution)/shard_map/dot_general | solution.py:155
  288.7 11.3 %convolution_convert_fusion = bf16[1024,4096]{1,0:T(8,128)(2,1)} fusion(bf16[1024,896]{1,0:T(8,128)(2,1)S(1)} %multiply_convert_fusion, bf16[1,896,4096]{2,1,0:T(8,128)(2,1)S(1)} %bitcast.161), kind=kOutput, calls=%fused_computation.1 | convolution fusion | flops 7520387072 | bytes 17563648 | tf_op jit(solution)/shard_map/dot_general | solution.py:160
  300.0 11.3 %copy.84 = bf16[4,8,32,4096]{3,1,2,0:T(8,128)(2,1)} copy(bf16[4,8,32,4096]{3,2,1,0:T(8,128)(2,1)} %bitcast.142) | data formatting | bytes 16777216
  311.3 78.2 %reduce-scatter.4.cloned.1.call-done = bf16[8,131072]{1,0:T(8,128)(2,1)} async-done(((bf16[32,131072]{1,0:T(8,128)(2,1)}), bf16[8,131072]{1,0:T(8,128)(2,1)}) %reduce-scatter.4.cloned.1.call-update) | async-done | bytes 2097168
  389.5 7.7 %all-to-all-start.1 = ((bf16[8,32,4096]{2,0,1:T(8,128)(2,1)}), bf16[8,32,4096]{2,0,1:T(8,128)(2,1)}, u32[]{:S(2)}, u32[]{:S(2)}) async-start(bf16[8,32,4096]{2,0,1:T(8,128)(2,1)} %bitcast.144), calls=%async_computation.1 | async-start | bytes 4194304 | tf_op jit(solution)/shard_map/all_to_all | solution.py:172
  398.3 27.8 %all-to-all-done.1 = bf16[8,32,4096]{2,0,1:T(8,128)(2,1)} async-done(((bf16[8,32,4096]{2,0,1:T(8,128)(2,1)}), bf16[8,32,4096]{2,0,1:T(8,128)(2,1)}, u32[]{:S(2)}, u32[]{:S(2)}) %all-to-all-start.1) | async-done | bytes 2097184 | tf_op jit(solution)/shard_map/all_to_all | solution.py:172
  426.1 2.7 copy.67
  428.8 1.2 gather_fusion
  430.0 1.3 reshape.302
  431.4 2.7 reduce_sum.60
  434.1 0.6 reduce_sum.61
  434.7 1.4 multiply_reduce_fusion.1
  436.2 1.8 add_convert_fusion
  (122 shorter events, 9.6 us)
Async XLA Ops:
  6.5 4.4 copy-start
  6.5 73.9 %all-gather.2.cloned.1.call-start = ((), (), s32[]{:S(2)}) async-start(), calls=%async_computation.3 | async-start | bytes 8650752 | tf_op jit(solution)/shard_map/all_gather | solution.py:122
  7.3 126.9 %all-reduce.2.cloned.1.call-start = ((), (), s32[]{:S(2)}) async-start(), calls=%async_computation.4 | async-start | bytes 2162688 | tf_op jit(solution)/shard_map/psum | solution.py:126
  11.8 2.4 collective-permute-start
  14.5 0.6 copy-start.10
  15.7 16.0 %collective-permute-start.1 = (bf16[16,8320]{1,0:T(8,128)(2,1)S(1)}, bf16[16,8320]{1,0:T(8,128)(2,1)S(1)}, u32[]{:S(2)}, u32[]{:S(2)}) collective-permute-start(bf16[16,8320]{1,0:T(8,128)(2,1)S(1)} %pad_maximum_fusion.2), channel_id=1, source_target_pairs={{0,8},{4,12},{8,16},{12,20},{16,24},{20,28},{24,32},{28,36},{32,40... | collective-permute-start | bytes 798728 | tf_op jit(solution)/shard_map/ppermute | solution.py:31
  31.7 0.8 copy-start.5
  32.7 10.0 %collective-permute-start.2 = (bf16[16,8320]{1,0:T(8,128)(2,1)S(1)}, bf16[16,8320]{1,0:T(8,128)(2,1)S(1)}, u32[]{:S(2)}, u32[]{:S(2)}) collective-permute-start(bf16[16,8320]{1,0:T(8,128)(2,1)S(1)} %pad_maximum_fusion.3), channel_id=1, source_target_pairs={{0,16},{4,20},{8,24},{12,28},{16,32},{20,36},{24,40},{28,44},{32,4... | collective-permute-start | bytes 798728 | tf_op jit(solution)/shard_map/ppermute | solution.py:31
  39.5 3.4 copy-start.12
  42.9 0.5 copy-start.13
  43.6 24.3 %copy-start.8 = (bf16[128,128]{1,0:T(8,128)(2,1)S(1)}, bf16[128,128]{1,0:T(8,128)(2,1)}, u32[]{:S(2)}) copy-start(bf16[128,128]{1,0:T(8,128)(2,1)} %param.20) | copy-start | bytes 98308
  44.7 14.6 %collective-permute-start.3 = (bf16[16,8320]{1,0:T(8,128)(2,1)}, bf16[16,8320]{1,0:T(8,128)(2,1)S(1)}, u32[]{:S(2)}, u32[]{:S(2)}) collective-permute-start(bf16[16,8320]{1,0:T(8,128)(2,1)} %pad_maximum_fusion.4), channel_id=1, source_target_pairs={{0,32},{4,36},{8,40},{12,44},{16,48},{20,52},{24,56},{28,60},{32,6... | collective-permute-start | bytes 798728 | tf_op jit(solution)/shard_map/ppermute | solution.py:31
  59.4 0.8 copy-start.4
  60.3 14.2 %collective-permute-start.4 = (bf16[16,8320]{1,0:T(8,128)(2,1)S(1)}, bf16[16,8320]{1,0:T(8,128)(2,1)S(1)}, u32[]{:S(2)}, u32[]{:S(2)}) collective-permute-start(bf16[16,8320]{1,0:T(8,128)(2,1)S(1)} %pad_maximum_fusion.5), channel_id=1, source_target_pairs={{0,64},{4,68},{8,72},{12,76},{16,80},{20,84},{24,88},{28,92},{32,9... | collective-permute-start | bytes 798728 | tf_op jit(solution)/shard_map/ppermute | solution.py:31
  68.9 9.2 %copy-start.11 = (f32[16,128]{1,0:T(8,128)S(1)}, f32[16,128]{1,0:T(8,128)}, u32[]{:S(2)}) copy-start(f32[16,128]{1,0:T(8,128)} %param.21) | copy-start | bytes 24580
  68.9 9.2 %copy-start.17 = (f32[16]{0:T(128)S(1)}, f32[16]{0:T(128)}, u32[]{:S(2)}) copy-start(f32[16]{0:T(128)} %param.23) | copy-start | bytes 196
  75.5 4.3 copy-start.7
  77.0 3.4 copy-start.16
  80.0 6.7 %copy-start.14 = (s32[128,2]{0,1:T(2,128)S(1)}, s32[128,2]{0,1:T(2,128)}, u32[]{:S(2)}) copy-start(s32[128,2]{0,1:T(2,128)} %param.32) | copy-start | bytes 3076
  85.1 50.6 %copy-start.6 = (bf16[128,4096]{1,0:T(8,128)(2,1)S(1)}, bf16[128,4096]{1,0:T(8,128)(2,1)}, u32[]{:S(2)}) copy-start(bf16[128,4096]{1,0:T(8,128)(2,1)} %param.27) | copy-start | bytes 3145732
  86.4 303.2 %reduce-scatter.4.cloned.1.call-start = ((), (), s32[]{:S(2)}) async-start(), calls=%async_computation.5 | async-start | bytes 10485760
  87.4 50.2 %copy-start.9 = (f32[4096]{0:T(1024)S(1)}, f32[4096]{0:T(1024)}, u32[]{:S(2)}) copy-start(f32[4096]{0:T(1024)} %param.28) | copy-start | bytes 49156
  136.3 1.4 copy-start.2
  255.5 24.0 %slice-start = ((s8[7340032]{0:T(1024)(128)(4,1)}), s8[3145728]{0:T(1024)(128)(4,1)S(1)}, s32[]{:S(2)}) async-start(s8[7340032]{0:T(1024)(128)(4,1)} %bitcast.158), calls=%async_computation.6 | async-start | bytes 6291456
  266.8 12.7 %copy-start.3 = (bf16[32,32,4096]{2,1,0:T(8,128)(2,1)S(1)}, bf16[32,32,4096]{2,1,0:T(8,128)(2,1)}, u32[]{:S(2)}) copy-start(bf16[32,32,4096]{2,1,0:T(8,128)(2,1)} %copy.65) | copy-start | bytes 25165828
  266.8 12.7 %slice-start.1 = ((s8[7340032]{0:T(1024)(128)(4,1)}), s8[4194304]{0:T(1024)(128)(4,1)S(1)}, s32[]{:S(2)}) async-start(s8[7340032]{0:T(1024)(128)(4,1)} %bitcast.158), calls=%async_computation.7 | async-start | bytes 8388608
  266.8 21.9 %slice-start.2 = ((s8[7340032]{0:T(1024)(128)(4,1)}), s8[4194304]{0:T(1024)(128)(4,1)S(1)}, s32[]{:S(2)}) async-start(s8[7340032]{0:T(1024)(128)(4,1)} %bitcast.160), calls=%async_computation.8 | async-start | bytes 8388608
  279.5 9.2 %slice-start.3 = ((s8[7340032]{0:T(1024)(128)(4,1)}), s8[3145728]{0:T(1024)(128)(4,1)S(1)}, s32[]{:S(2)}) async-start(s8[7340032]{0:T(1024)(128)(4,1)} %bitcast.160), calls=%async_computation.9 | async-start | bytes 6291456
  311.3 86.7 %copy-start.15 = (f32[128,2]{0,1:T(2,128)S(1)}, f32[128,2]{0,1:T(2,128)}, u32[]{:S(2)}) copy-start(f32[128,2]{0,1:T(2,128)} %param.33) | copy-start | bytes 3076
  389.5 36.6 %all-to-all-start.1 = ((bf16[8,32,4096]{2,0,1:T(8,128)(2,1)}), bf16[8,32,4096]{2,0,1:T(8,128)(2,1)}, u32[]{:S(2)}, u32[]{:S(2)}) async-start(bf16[8,32,4096]{2,0,1:T(8,128)(2,1)} %bitcast.144), calls=%async_computation.1 | async-start | bytes 4194304 | tf_op jit(solution)/shard_map/all_to_all | solution.py:172
  430.0 8.0 %copy-start.1 = (bf16[128,128]{1,0:T(8,128)(2,1)S(1)}, bf16[128,128]{1,0:T(8,128)(2,1)}, u32[]{:S(2)}) copy-start(bf16[128,128]{1,0:T(8,128)(2,1)} %param.19) | copy-start | bytes 98308
Sparse Core Ops, SparseCore 0:
  9.5 70.8 all-gather.1
  86.5 47.6 all-reduce.1
  311.4 78.0 reduce-scatter.3

commit v4 on v3

--- a/solution.py
+++ b/solution.py
@@ -1,9 +1,10 @@
 import jax
 import jax.numpy as jnp
 from jax import lax
-from jax.sharding import PartitionSpec as P
+from jax.sharding import Mesh, PartitionSpec as P
 
 PAIR = 2
+CTX = ("chip", "core")
 
 
 eps_norm = 1e-05
@@ -17,8 +18,8 @@
 
 
 def entering(decay, state, axis):
-    place = lax.axis_index(axis)
-    count = lax.axis_size(axis)
+    place = lax.axis_index("chip") * lax.axis_size("core") + lax.axis_index("core")
+    count = lax.axis_size("chip") * lax.axis_size("core")
     heads, rows, width = state.shape
     inclusive = (decay, state)
     exclusive = (jnp.ones_like(decay), jnp.zeros_like(state))
@@ -87,7 +88,7 @@
     head_count = step_size.shape[0]
     head_dim = inputs.shape[1] // head_count
     model_width = residual.shape[1]
-    n_ctx = lax.axis_size("ctx")
+    n_ctx = lax.axis_size("chip") * lax.axis_size("core")
     n_exp = lax.axis_size("exp")
     experts = n_ctx // PAIR
     tok_quarter = tok_ctx // n_exp
@@ -105,7 +106,7 @@
     inside_part = jnp.einsum("hts,shp->thp", mixing, x_local, precision=top_precision)
     ending = jnp.exp(-(span_total[:, None] - cumulative)) * step_size
     local_state = jnp.einsum("hs,shp,sn->hpn", ending, x_local, b_local, precision=top_precision)
-    prior_decay, prior_state = entering(jnp.exp(-span_total), local_state, "ctx")
+    prior_decay, prior_state = entering(jnp.exp(-span_total), local_state, CTX)
     incoming = prior_state + prior_decay[:, None, None] * start_state
     carried = (
         jnp.einsum("hpn,tn->thp", incoming, c_local, precision=top_precision)
@@ -119,7 +120,7 @@
     unscaled_mix = (gated_out * norm_gain[None, :]).astype(jnp.bfloat16)
     partial_value = jnp.dot(
         unscaled_mix,
-        lax.all_gather(out_proj, "ctx", axis=1, tiled=True),
+        lax.all_gather(out_proj, CTX, axis=1, tiled=True),
         preferred_element_type=jnp.float32,
     )
     width_out = partial_value.shape[1]
@@ -149,56 +150,52 @@
         route_ids.reshape(n_exp, tok_quarter, route_ids.shape[1]),
     )
     placed = placed.reshape(n_exp * capacity, experts, model_width)
-    outgoing = jnp.repeat(placed, PAIR, axis=1)
-    arrived = lax.all_to_all(outgoing, "ctx", split_axis=1, concat_axis=1, tiled=True)
+    swap = [(0, 1), (1, 0)]
+    mine = lax.all_to_all(placed, "chip", split_axis=1, concat_axis=1, tiled=True)
+    other = lax.ppermute(mine, "core", swap)
+    arrived = jnp.stack([mine, other], axis=1)
     flattened = arrived.reshape(-1, model_width)
     gate_val = jnp.dot(flattened, gate_rows, preferred_element_type=jnp.float32)
     up_val = jnp.dot(flattened, up_rows, preferred_element_type=jnp.float32)
     activated = (jax.nn.silu(gate_val) * up_val).astype(jnp.bfloat16)
-    hidden = activated.reshape(arrived.shape[0], arrived.shape[1], piece_width)
     hidden_own = lax.dynamic_slice_in_dim(hidden_all, first_row, tok_quarter, 0)
-    product = jnp.dot(
-        hidden.reshape(-1, piece_width), down_rows, preferred_element_type=jnp.float32
-    )
-    rounded = lax.optimization_barrier(product.astype(jnp.bfloat16)).astype(jnp.float32)
+    product = jnp.dot(activated, down_rows, preferred_element_type=jnp.float32)
+    rounded = lax.optimization_barrier(product.astype(jnp.bfloat16))
     summed = lax.psum_scatter(
-        rounded.reshape(lax.axis_size("exp") * capacity, hidden.shape[1], model_width).astype(
-            jnp.bfloat16
-        ),
-        "exp",
-        scatter_dimension=0,
-        tiled=True,
-    )
-    halves = lax.all_to_all(summed, "ctx", split_axis=1, concat_axis=1, tiled=True)
+        rounded.reshape(arrived.shape), "exp", scatter_dimension=0, tiled=True
+    )
+    partner_half = lax.ppermute(summed[:, 1], "core", swap)
+    both_halves = (summed[:, 0].astype(jnp.float32) + partner_half.astype(jnp.float32)).astype(jnp.bfloat16)
+    returned = lax.all_to_all(both_halves, "chip", split_axis=1, concat_axis=1, tiled=True)
     flattened, rank_ids = route_ranks(own_ids, experts)
-    base_rows = rank_ids * n_ctx + flattened * PAIR
-    fetch_rows = base_rows[:, None] + jnp.arange(PAIR, dtype=jnp.int32)[None, :]
-    fetched = halves.reshape(capacity * n_ctx, model_width)[fetch_rows]
-    expert_out = jnp.sum(fetched.astype(jnp.float32), axis=1)
-    weighted = expert_out * own_gates.reshape(-1)[:, None]
+    fetched = returned.reshape(capacity * experts, model_width)[rank_ids * experts + flattened]
+    weighted = fetched.astype(jnp.float32) * own_gates.reshape(-1)[:, None]
     moe_out = jnp.sum(weighted.reshape(tok_quarter, -1, model_width), axis=1)
     return (hidden_own + moe_out).astype(jnp.bfloat16)
 
 
 def solution(mesh):
     in_specs = (
-        P("ctx", "exp"),
-        P("ctx", "exp"),
-        P("ctx", None),
-        P("ctx", None),
-        P("exp", "ctx"),
-        P("exp", "ctx"),
+        P(CTX, "exp"),
+        P(CTX, "exp"),
+        P(CTX, None),
+        P(CTX, None),
+        P("exp", CTX),
+        P("exp", CTX),
         P("exp"),
         P("exp", None, None),
         P("exp"),
-        P("exp", "ctx"),
-        P("ctx", None),
+        P("exp", CTX),
+        P(CTX, None),
         P(),
-        P("ctx", None, "exp"),
-        P("ctx", None, "exp"),
-        P("ctx", "exp", None),
-        P("ctx", None),
-        P("ctx", None),
-    )
-    out_specs = P(("ctx", "exp"), None)
-    return jax.shard_map(local, mesh=mesh, in_specs=in_specs, out_specs=out_specs, check_vma=False)
+        P(CTX, None, "exp"),
+        P(CTX, None, "exp"),
+        P(CTX, "exp", None),
+        P(CTX, None),
+        P(CTX, None),
+    )
+    out_specs = P(("chip", "core", "exp"), None)
+    split_mesh = Mesh(
+        mesh.devices.reshape(mesh.devices.shape[0] // 2, 2, mesh.devices.shape[1]), ("chip", "core", "exp")
+    )
+    return jax.shard_map(local, mesh=split_mesh, in_specs=in_specs, out_specs=out_specs, check_vma=False)

time: 452 us -> 404 us (0.89)
  blocking collectives: 103 us -> 56.2 us
  local copies, waits for them, and re-layouts: 48.2 us -> 37.4 us
  matrix products: 42.1 us -> 49.7 us
  other arithmetic: 19.8 us -> 24.6 us
    all_to_all x1, blocking collectives: 103 us -> 56.2 us  [local(): lax.all_to_all(placed, 'chip', split_axis=1, concat_axis=1, tiled=True)]
    all_to_all x1, waiting for transfers between devices: 27.8 us -> 17.2 us  [local(): lax.all_to_all(both_halves, 'chip', split_axis=1, concat_axis=1, tiled=True)]
    all_to_all x2, local copies, waits for them, and re-layouts: 14.1 us -> 4.11 us  [the longest x1 2.3 us: local(): lax.all_to_all(placed, 'chip', split_axis=1, concat_axis=1, tiled=True)]
    ppermute x0 -> x2, waiting for transfers between devices: none -> 9.79 us  [the longest x1 7.15 us: local(): other = lax.ppermute(mine, 'core', swap)]
    another operation x9 -> x10, other arithmetic: 1.42 us -> 7.62 us  [the longest x1 6.2 us: local(): arrived = jnp.stack([mine, other], axis=1)]
    dot_general x1, matrix products: 9.16 us -> 15.1 us  [local(): gate_val = jnp.dot(flattened, gate_rows, preferred_element_type=jnp.float32)]
    unnamed x57 -> x53, local copies, waits for them, and re-layouts: 16.7 us -> 17.3 us
  transfers between devices with their start and end apart: 9 -> 11, of which waited for: 9 -> 11; matrix products, arithmetic and copies ran while one was open for 4% -> 4% of each run, Pallas kernels for 0% -> 0%
where the time goes in v4:
time: 404 us; the launch traced here: 398 us
  waiting for transfers between devices  175 us (43%)
  blocking collectives  56.2 us (14%)
  matrix products  49.7 us (12%)
  starting transfers between devices  40.4 us (10%)
  local copies, waits for them, and re-layouts  37.4 us (9%)
  other arithmetic  24.6 us (6%)
  between operations  14 us (3%)
    unnamed x4, waiting for transfers between devices  78.4 us
    all_to_all x1, blocking collectives, local(): lax.all_to_all(placed, 'chip', split_axis=1, concat_axis=1, tiled=True)  56.2 us
    psum x1, waiting for transfers between devices, local(): lax.psum(jnp.concatenate([partial_value, jnp.broadcast_to(squares[:, None...  46.6 us
    ppermute x5, starting transfers between devices, entering(): lax.ppermute(packed, axis, [(i, i + hop) for i in range(count - hop)])  32.5 us
    ppermute x5, waiting for transfers between devices, entering(): lax.ppermute(packed, axis, [(i, i + hop) for i in range(count - hop)])  22.8 us
    unnamed x53, local copies, waits for them, and re-layouts  17.3 us
    all_to_all x1, waiting for transfers between devices, local(): lax.all_to_all(both_halves, 'chip', split_axis=1, concat_axis=1, tiled=True)  17.2 us
    dot_general x1, matrix products, local(): gate_val = jnp.dot(flattened, gate_rows, preferred_element_type=jnp.float32)  15.1 us
  transfers between devices with their start and end apart: 11, of which 11 were waited for; matrix products, arithmetic and copies ran while one was open for 4% of the time, Pallas kernels for 0%

profile of v4, /device:TPU:0, one launch (start us, length us, event | category | flops | bytes accessed | tf_op | source)
XLA Modules:
  0.0 397.6 jit_solution(12349760757154850888)
XLA Ops:
  6.5 0.7 all-gather.2.cloned.1.call-update
  7.3 1.1 copy.43
  8.4 1.0 reduce_window_sum.33
  9.6 1.3 exponential_bitcast_fusion
  11.8 1.3 collective-permute-start
  13.1 1.1 collective-permute-done
  15.7 9.2 %collective-permute-start.1 = (bf16[16,8320]{1,0:T(8,128)(2,1)S(1)}, bf16[16,8320]{1,0:T(8,128)(2,1)S(1)}, u32[]{:S(2)}, u32[]{:S(2)}) collective-permute-start(bf16[16,8320]{1,0:T(8,128)(2,1)S(1)} %pad_maximum_fusion.3), channel_id=1, source_target_pairs={{0,8},{4,12},{8,16},{12,20},{16,24},{20,28},{24,32},{28,36},{32,40... | collective-permute-start | bytes 798728 | tf_op jit(solution)/shard_map/ppermute | solution.py:32
  24.9 6.7 %collective-permute-done.1 = bf16[16,8320]{1,0:T(8,128)(2,1)S(1)} collective-permute-done((bf16[16,8320]{1,0:T(8,128)(2,1)S(1)}, bf16[16,8320]{1,0:T(8,128)(2,1)S(1)}, u32[]{:S(2)}, u32[]{:S(2)}) %collective-permute-start.1) | collective-permute-done | bytes 266272 | tf_op jit(solution)/shard_map/ppermute | solution.py:32
  32.7 6.1 %collective-permute-start.2 = (bf16[16,8320]{1,0:T(8,128)(2,1)S(1)}, bf16[16,8320]{1,0:T(8,128)(2,1)S(1)}, u32[]{:S(2)}, u32[]{:S(2)}) collective-permute-start(bf16[16,8320]{1,0:T(8,128)(2,1)S(1)} %pad_maximum_fusion.4), channel_id=1, source_target_pairs={{0,16},{4,20},{8,24},{12,28},{16,32},{20,36},{24,40},{28,44},{32,4... | collective-permute-start | bytes 798728 | tf_op jit(solution)/shard_map/ppermute | solution.py:32
  38.7 0.8 fusion.60
  39.6 3.1 collective-permute-done.2
  44.0 0.7 pad_maximum_fusion.5
  44.7 8.3 %collective-permute-start.3 = (bf16[16,8320]{1,0:T(8,128)(2,1)}, bf16[16,8320]{1,0:T(8,128)(2,1)S(1)}, u32[]{:S(2)}, u32[]{:S(2)}) collective-permute-start(bf16[16,8320]{1,0:T(8,128)(2,1)} %pad_maximum_fusion.5), channel_id=1, source_target_pairs={{0,32},{4,36},{8,40},{12,44},{16,48},{20,52},{24,56},{28,60},{32,6... | collective-permute-start | bytes 798728 | tf_op jit(solution)/shard_map/ppermute | solution.py:32
  53.0 6.3 %collective-permute-done.3 = bf16[16,8320]{1,0:T(8,128)(2,1)S(1)} collective-permute-done((bf16[16,8320]{1,0:T(8,128)(2,1)}, bf16[16,8320]{1,0:T(8,128)(2,1)S(1)}, u32[]{:S(2)}, u32[]{:S(2)}) %collective-permute-start.3) | collective-permute-done | bytes 266272 | tf_op jit(solution)/shard_map/ppermute | solution.py:32
  60.3 7.6 %collective-permute-start.4 = (bf16[16,8320]{1,0:T(8,128)(2,1)S(1)}, bf16[16,8320]{1,0:T(8,128)(2,1)S(1)}, u32[]{:S(2)}, u32[]{:S(2)}) collective-permute-start(bf16[16,8320]{1,0:T(8,128)(2,1)S(1)} %pad_maximum_fusion.6), channel_id=1, source_target_pairs={{0,64},{4,68},{8,72},{12,76},{16,80},{20,84},{24,88},{28,92},{32,9... | collective-permute-start | bytes 798728 | tf_op jit(solution)/shard_map/ppermute | solution.py:32
  68.1 0.8 fusion.63
  69.0 5.5 %collective-permute-done.4 = bf16[16,8320]{1,0:T(8,128)(2,1)S(1)} collective-permute-done((bf16[16,8320]{1,0:T(8,128)(2,1)S(1)}, bf16[16,8320]{1,0:T(8,128)(2,1)S(1)}, u32[]{:S(2)}, u32[]{:S(2)}) %collective-permute-start.4) | collective-permute-done | bytes 266272 | tf_op jit(solution)/shard_map/ppermute | solution.py:32
  75.5 1.5 fusion.24
  77.1 1.1 fusion.10
  78.2 1.4 fusion.9
  80.4 4.7 %convolution_convert_fusion.2 = bf16[128,4096]{1,0:T(8,128)(2,1)S(1)} fusion(bf16[1024,4096]{1,0:T(8,128)(2,1)} %all-gather.2.cloned.1.call-done, f32[1024]{0:T(1024)S(1)} %copy-done.16, f32[128,1024]{1,0:T(8,128)S(1)} %copy.44, bf16[128,1024]{1,0:T(8,128)(2,1)S(1)} %copy-done.7), kind=kOutput, calls=%fused_computation.9 | convolution fusion | flops 1075314688 | bytes 10227712 | tf_op jit(solution)/shard_map/dot_general | solution.py:121
  85.2 1.1 pad_maximum_fusion.1
  87.6 46.6 %all-reduce.2.cloned.1.call-done = bf16[128,4224]{1,0:T(8,128)(2,1)} async-done(((bf16[128,4224]{1,0:T(8,128)(2,1)}), bf16[128,4224]{1,0:T(8,128)(2,1)}) %all-reduce.2.cloned.1.call-update) | async-done | bytes 1081360 | tf_op jit(solution)/shard_map/psum | solution.py:127
  134.2 1.4 convert_element_type.85
  136.6 3.4 broadcast_in_dim.126
  140.0 4.1 %reshape.271 = bf16[4,64,4096]{2,1,0:T(8,128)(2,1)} reshape(bf16[4,32,2,4096]{3,2,1,0:T(2,128)(2,1)} %broadcast_in_dim.126) | data formatting | bytes 4194304 | tf_op jit(solution)/shard_map/vmap()/reshape | solution.py:58
  144.2 2.9 convolution_convert_fusion.1
  147.1 2.3 copy.46
  149.4 56.2 %all_to_all.10 = bf16[32,16,4096]{2,0,1:T(8,128)(2,1)S(1)} all-to-all(bf16[32,16,4096]{2,0,1:T(8,128)(2,1)S(1)} %copy.46), channel_id=1, replica_groups=mesh['chip'=16,'core'=2,'exp'=4] {'chip'}, dimensions={1} | all-to-all | bytes 8388608 | tf_op jit(solution)/shard_map/all_to_all | solution.py:154
  205.6 2.3 copy.79
  208.2 7.1 %collective-permute-done.5 = bf16[32,16,4096]{2,1,0:T(8,128)(2,1)S(1)} collective-permute-done((bf16[32,16,4096]{2,1,0:T(8,128)(2,1)S(1)}, bf16[32,16,4096]{2,1,0:T(8,128)(2,1)S(1)}, u32[]{:S(2)}, u32[]{:S(2)}) %collective-permute-start.5) | collective-permute-done | bytes 4194336 | tf_op jit(solution)/shard_map/ppermute | solution.py:155
  215.3 2.0 copy-done.3
  217.3 6.2 %pad_maximum_fusion = bf16[32,2,16,4096]{3,2,1,0:T(8,128)(2,1)} fusion(bf16[32,1,16,4096]{3,2,1,0:T(8,128)(2,1)} %bitcast.156, bf16[32,1,16,4096]{3,2,1,0:T(8,128)(2,1)S(1)} %bitcast.151), kind=kLoop, calls=%fused_computation.1 | loop fusion | flops 4194304 | bytes 16777216 | tf_op jit(solution)/shard_map/stack | solution.py:156
  223.5 12.5 %fusion.1 = f32[1024,896]{1,0:T(8,128)S(1)} fusion(bf16[1024,4096]{1,0:T(8,128)(2,1)} %bitcast.152, bf16[1,4096,896]{2,1,0:T(8,128)(2,1)} %param.30), kind=kOutput, calls=%fused_computation.4 | convolution fusion | flops 7516192768 | bytes 19398656 | tf_op jit(solution)/shard_map/dot_general | solution.py:159
  236.0 15.1 %fusion.3 = f32[1024,896]{1,0:T(8,128)S(1)} fusion(bf16[1024,4096]{1,0:T(8,128)(2,1)S(1)} %bitcast.153, bf16[1,4096,896]{2,1,0:T(8,128)(2,1)} %param.29), kind=kOutput, calls=%fused_computation.6 | convolution fusion | flops 7516192768 | bytes 19398656 | tf_op jit(solution)/shard_map/dot_general | solution.py:158
  251.1 11.5 %convolution_convert_fusion = bf16[1024,4096]{1,0:T(8,128)(2,1)} fusion(bf16[1,896,4096]{2,1,0:T(8,128)(2,1)S(1)} %bitcast.173, f32[1024,896]{1,0:T(8,128)S(1)} %fusion.1, f32[1024,896]{1,0:T(8,128)S(1)} %fusion.3), kind=kOutput, calls=%fused_computation.2 | convolution fusion | flops 7525892096 | bytes 23068672 | tf_op jit(solution)/shard_map/dot_general | solution.py:162
  262.6 11.3 %copy.66 = bf16[4,8,32,4096]{3,1,2,0:T(8,128)(2,1)} copy(bf16[4,8,32,4096]{3,2,1,0:T(8,128)(2,1)} %bitcast.154) | data formatting | bytes 16777216
  274.0 77.7 %reduce-scatter.4.cloned.1.call-done = bf16[8,131072]{1,0:T(8,128)(2,1)} async-done(((bf16[32,131072]{1,0:T(8,128)(2,1)}), bf16[8,131072]{1,0:T(8,128)(2,1)}) %reduce-scatter.4.cloned.1.call-update) | async-done | bytes 2097168
  351.7 1.3 slice_bitcast_fusion
  353.1 2.6 collective-permute-done.6
  355.7 2.5 fusion.6
  358.2 7.0 %all-to-all-start.1 = ((bf16[8,16,4096]{2,0,1:T(8,128)(2,1)}), bf16[8,16,4096]{2,0,1:T(8,128)(2,1)}, u32[]{:S(2)}, u32[]{:S(2)}) async-start(bf16[8,16,4096]{2,0,1:T(8,128)(2,1)} %fusion.6), calls=%async_computation.1 | async-start | bytes 2097152 | tf_op jit(solution)/shard_map/all_to_all | solution.py:169
  366.2 17.2 %all-to-all-done.1 = bf16[8,16,4096]{2,0,1:T(8,128)(2,1)} async-done(((bf16[8,16,4096]{2,0,1:T(8,128)(2,1)}), bf16[8,16,4096]{2,0,1:T(8,128)(2,1)}, u32[]{:S(2)}, u32[]{:S(2)}) %all-to-all-start.1) | async-done | bytes 1048608 | tf_op jit(solution)/shard_map/all_to_all | solution.py:169
  383.4 1.8 copy.50
  385.2 1.7 gather_fusion
  386.9 1.7 reshape.283
  388.6 1.4 multiply_reduce_fusion.1
  390.0 0.8 add_convert_fusion
  (120 shorter events, 11.3 us)
Async XLA Ops:
  6.5 4.4 %copy-start = (bf16[128,128]{1,0:T(8,128)(2,1)S(1)}, bf16[128,128]{1,0:T(8,128)(2,1)}, u32[]{:S(2)}) copy-start(bf16[128,128]{1,0:T(8,128)(2,1)} %param.19) | copy-start | bytes 98308
  6.5 73.9 %all-gather.2.cloned.1.call-start = ((), (), s32[]{:S(2)}) async-start(), calls=%async_computation.3 | async-start | bytes 8650752 | tf_op jit(solution)/shard_map/all_gather | solution.py:123
  7.3 126.9 %all-reduce.2.cloned.1.call-start = ((), (), s32[]{:S(2)}) async-start(), calls=%async_computation.4 | async-start | bytes 2162688 | tf_op jit(solution)/shard_map/psum | solution.py:127
  11.8 2.4 collective-permute-start
  14.5 0.6 copy-start.10
  15.7 16.0 %collective-permute-start.1 = (bf16[16,8320]{1,0:T(8,128)(2,1)S(1)}, bf16[16,8320]{1,0:T(8,128)(2,1)S(1)}, u32[]{:S(2)}, u32[]{:S(2)}) collective-permute-start(bf16[16,8320]{1,0:T(8,128)(2,1)S(1)} %pad_maximum_fusion.3), channel_id=1, source_target_pairs={{0,8},{4,12},{8,16},{12,20},{16,24},{20,28},{24,32},{28,36},{32,40... | collective-permute-start | bytes 798728 | tf_op jit(solution)/shard_map/ppermute | solution.py:32
  31.7 0.8 copy-start.5
  32.7 10.0 %collective-permute-start.2 = (bf16[16,8320]{1,0:T(8,128)(2,1)S(1)}, bf16[16,8320]{1,0:T(8,128)(2,1)S(1)}, u32[]{:S(2)}, u32[]{:S(2)}) collective-permute-start(bf16[16,8320]{1,0:T(8,128)(2,1)S(1)} %pad_maximum_fusion.4), channel_id=1, source_target_pairs={{0,16},{4,20},{8,24},{12,28},{16,32},{20,36},{24,40},{28,44},{32,4... | collective-permute-start | bytes 798728 | tf_op jit(solution)/shard_map/ppermute | solution.py:32
  39.5 3.4 copy-start.12
  42.9 0.5 copy-start.13
  43.6 24.3 %copy-start.8 = (bf16[128,128]{1,0:T(8,128)(2,1)S(1)}, bf16[128,128]{1,0:T(8,128)(2,1)}, u32[]{:S(2)}) copy-start(bf16[128,128]{1,0:T(8,128)(2,1)} %param.20) | copy-start | bytes 98308
  44.7 14.6 %collective-permute-start.3 = (bf16[16,8320]{1,0:T(8,128)(2,1)}, bf16[16,8320]{1,0:T(8,128)(2,1)S(1)}, u32[]{:S(2)}, u32[]{:S(2)}) collective-permute-start(bf16[16,8320]{1,0:T(8,128)(2,1)} %pad_maximum_fusion.5), channel_id=1, source_target_pairs={{0,32},{4,36},{8,40},{12,44},{16,48},{20,52},{24,56},{28,60},{32,6... | collective-permute-start | bytes 798728 | tf_op jit(solution)/shard_map/ppermute | solution.py:32
  59.4 0.8 copy-start.4
  60.3 14.2 %collective-permute-start.4 = (bf16[16,8320]{1,0:T(8,128)(2,1)S(1)}, bf16[16,8320]{1,0:T(8,128)(2,1)S(1)}, u32[]{:S(2)}, u32[]{:S(2)}) collective-permute-start(bf16[16,8320]{1,0:T(8,128)(2,1)S(1)} %pad_maximum_fusion.6), channel_id=1, source_target_pairs={{0,64},{4,68},{8,72},{12,76},{16,80},{20,84},{24,88},{28,92},{32,9... | collective-permute-start | bytes 798728 | tf_op jit(solution)/shard_map/ppermute | solution.py:32
  68.9 9.2 %copy-start.11 = (f32[16,128]{1,0:T(8,128)S(1)}, f32[16,128]{1,0:T(8,128)}, u32[]{:S(2)}) copy-start(f32[16,128]{1,0:T(8,128)} %param.21) | copy-start | bytes 24580
  68.9 9.2 %copy-start.17 = (f32[16]{0:T(128)S(1)}, f32[16]{0:T(128)}, u32[]{:S(2)}) copy-start(f32[16]{0:T(128)} %param.23) | copy-start | bytes 196
  75.5 4.3 %copy-start.7 = (bf16[128,1024]{1,0:T(8,128)(2,1)S(1)}, bf16[128,1024]{1,0:T(8,128)(2,1)}, u32[]{:S(2)}) copy-start(bf16[128,1024]{1,0:T(8,128)(2,1)} %param.18) | copy-start | bytes 786436
  77.0 3.4 copy-start.16
  80.0 6.8 %copy-start.14 = (s32[128,2]{0,1:T(2,128)S(1)}, s32[128,2]{0,1:T(2,128)}, u32[]{:S(2)}) copy-start(s32[128,2]{0,1:T(2,128)} %param.32) | copy-start | bytes 3076
  85.1 50.6 %copy-start.6 = (bf16[128,4096]{1,0:T(8,128)(2,1)S(1)}, bf16[128,4096]{1,0:T(8,128)(2,1)}, u32[]{:S(2)}) copy-start(bf16[128,4096]{1,0:T(8,128)(2,1)} %param.27) | copy-start | bytes 3145732
  86.4 265.3 %reduce-scatter.4.cloned.1.call-start = ((), (), s32[]{:S(2)}) async-start(), calls=%async_computation.5 | async-start | bytes 10485760
  87.6 48.7 %copy-start.9 = (f32[4096]{0:T(1024)S(1)}, f32[4096]{0:T(1024)}, u32[]{:S(2)}) copy-start(f32[4096]{0:T(1024)} %param.28) | copy-start | bytes 49156
  207.9 7.4 %collective-permute-start.5 = (bf16[32,16,4096]{2,1,0:T(8,128)(2,1)S(1)}, bf16[32,16,4096]{2,1,0:T(8,128)(2,1)S(1)}, u32[]{:S(2)}, u32[]{:S(2)}) collective-permute-start(bf16[32,16,4096]{2,1,0:T(8,128)(2,1)S(1)} %copy.79), channel_id=1, source_target_pairs={{0,4},{4,0},{1,5},{5,1},{2,6},{6,2},{3,7},{7,3},{8,12},{12,8},{9,1... | collective-permute-start | bytes 12582920 | tf_op jit(solution)/shard_map/ppermute | solution.py:155
  215.3 2.0 copy-start.3
  223.5 12.5 %copy-start.2 = (bf16[32,2,16,4096]{3,2,1,0:T(8,128)(2,1)S(1)}, bf16[32,2,16,4096]{3,2,1,0:T(8,128)(2,1)}, u32[]{:S(2)}) copy-start(bf16[32,2,16,4096]{3,2,1,0:T(8,128)(2,1)} %pad_maximum_fusion) | copy-start | bytes 25165828
  223.5 27.6 %slice-start = ((s8[7340032]{0:T(1024)(128)(4,1)}), s8[4194304]{0:T(1024)(128)(4,1)S(1)}, s32[]{:S(2)}) async-start(s8[7340032]{0:T(1024)(128)(4,1)} %bitcast.172), calls=%async_computation.6 | async-start | bytes 8388608
  236.0 15.1 %slice-start.1 = ((s8[7340032]{0:T(1024)(128)(4,1)}), s8[3145728]{0:T(1024)(128)(4,1)S(1)}, s32[]{:S(2)}) async-start(s8[7340032]{0:T(1024)(128)(4,1)} %bitcast.172), calls=%async_computation.7 | async-start | bytes 6291456
  351.7 14.1 %copy-start.15 = (f32[128,2]{0,1:T(2,128)S(1)}, f32[128,2]{0,1:T(2,128)}, u32[]{:S(2)}) copy-start(f32[128,2]{0,1:T(2,128)} %param.33) | copy-start | bytes 3076
  353.0 2.7 collective-permute-start.6
  358.2 25.2 %all-to-all-start.1 = ((bf16[8,16,4096]{2,0,1:T(8,128)(2,1)}), bf16[8,16,4096]{2,0,1:T(8,128)(2,1)}, u32[]{:S(2)}, u32[]{:S(2)}) async-start(bf16[8,16,4096]{2,0,1:T(8,128)(2,1)} %fusion.6), calls=%async_computation.1 | async-start | bytes 2097152 | tf_op jit(solution)/shard_map/all_to_all | solution.py:169
  385.2 5.6 %copy-start.1 = (bf16[128,128]{1,0:T(8,128)(2,1)S(1)}, bf16[128,128]{1,0:T(8,128)(2,1)}, u32[]{:S(2)}) copy-start(bf16[128,128]{1,0:T(8,128)(2,1)} %param.19) | copy-start | bytes 98308
Sparse Core Ops, SparseCore 0:
  9.5 70.8 all-gather.1
  86.5 47.6 all-reduce.1
  274.1 77.5 reduce-scatter.3

commit v5 on v4

--- a/solution.py
+++ b/solution.py
@@ -153,19 +153,22 @@
     swap = [(0, 1), (1, 0)]
     mine = lax.all_to_all(placed, "chip", split_axis=1, concat_axis=1, tiled=True)
     other = lax.ppermute(mine, "core", swap)
-    arrived = jnp.stack([mine, other], axis=1)
-    flattened = arrived.reshape(-1, model_width)
-    gate_val = jnp.dot(flattened, gate_rows, preferred_element_type=jnp.float32)
-    up_val = jnp.dot(flattened, up_rows, preferred_element_type=jnp.float32)
-    activated = (jax.nn.silu(gate_val) * up_val).astype(jnp.bfloat16)
     hidden_own = lax.dynamic_slice_in_dim(hidden_all, first_row, tok_quarter, 0)
-    product = jnp.dot(activated, down_rows, preferred_element_type=jnp.float32)
-    rounded = lax.optimization_barrier(product.astype(jnp.bfloat16))
-    summed = lax.psum_scatter(
-        rounded.reshape(arrived.shape), "exp", scatter_dimension=0, tiled=True
-    )
-    partner_half = lax.ppermute(summed[:, 1], "core", swap)
-    both_halves = (summed[:, 0].astype(jnp.float32) + partner_half.astype(jnp.float32)).astype(jnp.bfloat16)
+
+    def expert_rows(rows):
+        flat = rows.reshape(-1, model_width)
+        gate_val = jnp.dot(flat, gate_rows, preferred_element_type=jnp.float32)
+        up_val = jnp.dot(flat, up_rows, preferred_element_type=jnp.float32)
+        activated = (jax.nn.silu(gate_val) * up_val).astype(jnp.bfloat16)
+        product = jnp.dot(activated, down_rows, preferred_element_type=jnp.float32)
+        return lax.psum_scatter(
+            product.astype(jnp.bfloat16).reshape(rows.shape), "exp", scatter_dimension=0, tiled=True
+        )
+
+    own_sum = expert_rows(mine)
+    partner_sum = expert_rows(other)
+    partner_half = lax.ppermute(partner_sum, "core", swap)
+    both_halves = (own_sum.astype(jnp.float32) + partner_half.astype(jnp.float32)).astype(jnp.bfloat16)
     returned = lax.all_to_all(both_halves, "chip", split_axis=1, concat_axis=1, tiled=True)
     flattened, rank_ids = route_ranks(own_ids, experts)
     fetched = returned.reshape(capacity * experts, model_width)[rank_ids * experts + flattened]

time: 404 us -> 390 us (0.965)
  waiting for transfers between devices: 175 us -> 161 us
  matrix products: 49.7 us -> 59.6 us
  other arithmetic: 24.6 us -> 16.5 us
    unnamed x4 -> x6, waiting for transfers between devices: 78.4 us -> 60.2 us
    dot_general x3 -> x4, matrix products: 39.1 us -> 49 us  [the longest x2 33.1 us: expert_rows(): product = jnp.dot(activated, down_rows, preferred_element_type=jnp.float32)]
    another operation x10 -> x9, other arithmetic: 7.62 us -> 1.42 us  [the longest x1 6.2 us: local(): arrived = jnp.stack([mine, other], axis=1)]
    all_gather x1, waiting for transfers between devices: 0.37 us -> 5.83 us  [local(): lax.all_gather(out_proj, CTX, axis=1, tiled=True)]
    unnamed x53 -> x48, local copies, waits for them, and re-layouts: 17.3 us -> 20 us
  transfers between devices with their start and end apart: 11 -> 12, of which waited for: 11 -> 11; matrix products, arithmetic and copies ran while one was open for 4% -> 13% of each run, Pallas kernels for 0% -> 0%
where the time goes in v5:
time: 390 us; the launch traced here: 384 us
  waiting for transfers between devices  161 us (41%)
  matrix products  59.6 us (15%)
  blocking collectives  56.4 us (14%)
  local copies, waits for them, and re-layouts  38.8 us (10%)
  starting transfers between devices  37.6 us (10%)
  other arithmetic  16.5 us (4%)
  between operations  14 us (4%)
    unnamed x6, waiting for transfers between devices  60.2 us
    all_to_all x1, blocking collectives, local(): lax.all_to_all(placed, 'chip', split_axis=1, concat_axis=1, tiled=True)  56.4 us
    psum x1, waiting for transfers between devices, local(): lax.psum(jnp.concatenate([partial_value, jnp.broadcast_to(squares[:, None...  45 us
    dot_general x2, matrix products, expert_rows(): product = jnp.dot(activated, down_rows, preferred_element_type=jnp.float32)  33.1 us
    ppermute x5, starting transfers between devices, entering(): lax.ppermute(packed, axis, [(i, i + hop) for i in range(count - hop)])  29.2 us
    ppermute x5, waiting for transfers between devices, entering(): lax.ppermute(packed, axis, [(i, i + hop) for i in range(count - hop)])  25.7 us
    unnamed x48, local copies, waits for them, and re-layouts  20 us
    all_to_all x1, waiting for transfers between devices, local(): lax.all_to_all(both_halves, 'chip', split_axis=1, concat_axis=1, tiled=True)  16.9 us
  transfers between devices with their start and end apart: 12, of which 11 were waited for; matrix products, arithmetic and copies ran while one was open for 13% of the time, Pallas kernels for 0%

profile of v5, /device:TPU:0, one launch (start us, length us, event | category | flops | bytes accessed | tf_op | source)
XLA Modules:
  0.0 383.7 jit_solution(13033365871746023165)
XLA Ops:
  7.3 1.1 copy.51
  8.4 1.0 reduce_window_sum.33
  9.6 0.8 exponential_bitcast_fusion
  11.2 1.3 collective-permute-start
  12.6 1.1 collective-permute-done
  14.6 9.2 %collective-permute-start.1 = (bf16[16,8320]{1,0:T(8,128)(2,1)S(1)}, bf16[16,8320]{1,0:T(8,128)(2,1)S(1)}, u32[]{:S(2)}, u32[]{:S(2)}) collective-permute-start(bf16[16,8320]{1,0:T(8,128)(2,1)S(1)} %pad_maximum_fusion.2), channel_id=1, source_target_pairs={{0,8},{4,12},{8,16},{12,20},{16,24},{20,28},{24,32},{28,36},{32,40... | collective-permute-start | bytes 798728 | tf_op jit(solution)/shard_map/ppermute | solution.py:32
  23.9 7.3 %collective-permute-done.1 = bf16[16,8320]{1,0:T(8,128)(2,1)S(1)} collective-permute-done((bf16[16,8320]{1,0:T(8,128)(2,1)S(1)}, bf16[16,8320]{1,0:T(8,128)(2,1)S(1)}, u32[]{:S(2)}, u32[]{:S(2)}) %collective-permute-start.1) | collective-permute-done | bytes 266272 | tf_op jit(solution)/shard_map/ppermute | solution.py:32
  32.0 6.2 %collective-permute-start.2 = (bf16[16,8320]{1,0:T(8,128)(2,1)S(1)}, bf16[16,8320]{1,0:T(8,128)(2,1)S(1)}, u32[]{:S(2)}, u32[]{:S(2)}) collective-permute-start(bf16[16,8320]{1,0:T(8,128)(2,1)S(1)} %pad_maximum_fusion.3), channel_id=1, source_target_pairs={{0,16},{4,20},{8,24},{12,28},{16,32},{20,36},{24,40},{28,44},{32,4... | collective-permute-start | bytes 798728 | tf_op jit(solution)/shard_map/ppermute | solution.py:32
  38.3 4.1 %collective-permute-done.2 = bf16[16,8320]{1,0:T(8,128)(2,1)S(1)} collective-permute-done((bf16[16,8320]{1,0:T(8,128)(2,1)S(1)}, bf16[16,8320]{1,0:T(8,128)(2,1)S(1)}, u32[]{:S(2)}, u32[]{:S(2)}) %collective-permute-start.2) | collective-permute-done | bytes 266272 | tf_op jit(solution)/shard_map/ppermute | solution.py:32
  43.3 0.7 pad_maximum_fusion.4
  44.0 7.2 %collective-permute-start.3 = (bf16[16,8320]{1,0:T(8,128)(2,1)}, bf16[16,8320]{1,0:T(8,128)(2,1)S(1)}, u32[]{:S(2)}, u32[]{:S(2)}) collective-permute-start(bf16[16,8320]{1,0:T(8,128)(2,1)} %pad_maximum_fusion.4), channel_id=1, source_target_pairs={{0,32},{4,36},{8,40},{12,44},{16,48},{20,52},{24,56},{28,60},{32,6... | collective-permute-start | bytes 798728 | tf_op jit(solution)/shard_map/ppermute | solution.py:32
  51.2 10.9 %collective-permute-done.3 = bf16[16,8320]{1,0:T(8,128)(2,1)S(1)} collective-permute-done((bf16[16,8320]{1,0:T(8,128)(2,1)}, bf16[16,8320]{1,0:T(8,128)(2,1)S(1)}, u32[]{:S(2)}, u32[]{:S(2)}) %collective-permute-start.3) | collective-permute-done | bytes 266272 | tf_op jit(solution)/shard_map/ppermute | solution.py:32
  63.2 5.3 %collective-permute-start.4 = (bf16[16,8320]{1,0:T(8,128)(2,1)S(1)}, bf16[16,8320]{1,0:T(8,128)(2,1)S(1)}, u32[]{:S(2)}, u32[]{:S(2)}) collective-permute-start(bf16[16,8320]{1,0:T(8,128)(2,1)S(1)} %pad_maximum_fusion.5), channel_id=1, source_target_pairs={{0,64},{4,68},{8,72},{12,76},{16,80},{20,84},{24,88},{28,92},{32,9... | collective-permute-start | bytes 798728 | tf_op jit(solution)/shard_map/ppermute | solution.py:32
  68.5 0.8 fusion.100
  69.3 0.8 fusion.83
  70.1 2.3 collective-permute-done.4
  72.8 1.6 fusion.44
  74.8 1.4 fusion.22
  76.7 5.8 %all-gather.2.cloned.1.call-done = bf16[1024,4096]{1,0:T(8,128)(2,1)} async-done(((bf16[1024,128]{1,0:T(8,128)(2,1)}), bf16[1024,4096]{1,0:T(8,128)(2,1)}) %all-gather.2.cloned.1.call-update) | async-done | bytes 8388624 | tf_op jit(solution)/shard_map/all_gather | solution.py:123
  82.5 4.7 %convolution_convert_fusion.1 = bf16[128,4096]{1,0:T(8,128)(2,1)S(1)} fusion(bf16[1024,4096]{1,0:T(8,128)(2,1)} %all-gather.2.cloned.1.call-done, f32[1024]{0:T(1024)S(1)} %copy-done.13, f32[128,1024]{1,0:T(8,128)S(1)} %copy.52, bf16[128,1024]{1,0:T(8,128)(2,1)S(1)} %copy-done.5), kind=kOutput, calls=%fused_computation.16 | convolution fusion | flops 1075314688 | bytes 10227712 | tf_op jit(solution)/shard_map/dot_general | solution.py:121
  87.3 1.1 pad_maximum_fusion
  89.5 45.0 %all-reduce.2.cloned.1.call-done = bf16[128,4224]{1,0:T(8,128)(2,1)} async-done(((bf16[128,4224]{1,0:T(8,128)(2,1)}), bf16[128,4224]{1,0:T(8,128)(2,1)}) %all-reduce.2.cloned.1.call-update) | async-done | bytes 1081360 | tf_op jit(solution)/shard_map/psum | solution.py:127
  134.5 1.4 convert_element_type.88
  137.1 3.4 broadcast_in_dim.126
  140.5 4.1 %reshape.275 = bf16[4,64,4096]{2,1,0:T(8,128)(2,1)} reshape(bf16[4,32,2,4096]{3,2,1,0:T(2,128)(2,1)} %broadcast_in_dim.126) | data formatting | bytes 4194304 | tf_op jit(solution)/shard_map/vmap()/reshape | solution.py:58
  144.6 2.9 convolution_convert_fusion
  147.6 2.3 copy.54
  149.9 56.4 %all_to_all.10 = bf16[32,16,4096]{2,0,1:T(8,128)(2,1)S(1)} all-to-all(bf16[32,16,4096]{2,0,1:T(8,128)(2,1)S(1)} %copy.54), channel_id=1, replica_groups=mesh['chip'=16,'core'=2,'exp'=4] {'chip'}, dimensions={1} | all-to-all | bytes 8388608 | tf_op jit(solution)/shard_map/all_to_all | solution.py:154
  206.3 2.3 copy.55
  208.6 1.9 copy-done.2
  211.1 7.1 %collective-permute-done.5 = bf16[32,16,4096]{2,1,0:T(8,128)(2,1)S(1)} collective-permute-done((bf16[32,16,4096]{2,1,0:T(8,128)(2,1)S(1)}, bf16[32,16,4096]{2,1,0:T(8,128)(2,1)S(1)}, u32[]{:S(2)}, u32[]{:S(2)}) %collective-permute-start.5) | collective-permute-done | bytes 4194336 | tf_op jit(solution)/shard_map/ppermute | solution.py:155
  218.2 2.0 copy-done.12
  220.2 5.8 %fusion.4 = f32[512,896]{1,0:T(8,128)} fusion(bf16[512,4096]{1,0:T(8,128)(2,1)S(1)} %bitcast.187, bf16[1,4096,896]{2,1,0:T(8,128)(2,1)S(1)} %bitcast.186), kind=kOutput, calls=%fused_computation.5 | convolution fusion | flops 3758096384 | bytes 13369344 | tf_op jit(solution)/shard_map/dot_general | solution.py:161
  226.0 16.5 %fusion.15 = bf16[512,4096]{1,0:T(8,128)(2,1)} fusion(bf16[1,896,4096]{2,1,0:T(8,128)(2,1)} %param.31, f32[512,896]{1,0:T(8,128)} %fusion.4, bf16[512,4096]{1,0:T(8,128)(2,1)} %bitcast.188, bf16[1,4096,896]{2,1,0:T(8,128)(2,1)} %param.29), kind=kOutput, calls=%fused_computation.15 | convolution fusion | flops 7521042432 | bytes 24903680 | tf_op jit(solution)/shard_map/dot_general | solution.py:163
  242.5 6.5 %copy.78 = bf16[4,8,16,4096]{3,1,2,0:T(8,128)(2,1)} copy(bf16[4,8,16,4096]{3,2,1,0:T(8,128)(2,1)} %bitcast.169) | data formatting | bytes 8388608
  249.2 10.1 %fusion.10 = f32[512,896]{1,0:T(8,128)} fusion(bf16[512,4096]{1,0:T(8,128)(2,1)} %bitcast.167, bf16[1,4096,896]{2,1,0:T(8,128)(2,1)} %param.29), kind=kOutput, calls=%fused_computation.11 | convolution fusion | flops 3758096384 | bytes 13369344 | tf_op jit(solution)/shard_map/dot_general | solution.py:160
  259.3 16.6 %fusion.12 = bf16[512,4096]{1,0:T(8,128)(2,1)} fusion(bf16[1,896,4096]{2,1,0:T(8,128)(2,1)} %param.31, f32[512,896]{1,0:T(8,128)} %fusion.10, bf16[512,4096]{1,0:T(8,128)(2,1)} %bitcast.168, bf16[1,4096,896]{2,1,0:T(8,128)(2,1)} %param.30), kind=kOutput, calls=%fused_computation.14 | convolution fusion | flops 7521042432 | bytes 24903680 | tf_op jit(solution)/shard_map/dot_general | solution.py:163
  276.0 6.5 %copy.77 = bf16[4,8,16,4096]{3,1,2,0:T(8,128)(2,1)} copy(bf16[4,8,16,4096]{3,2,1,0:T(8,128)(2,1)} %bitcast.170) | data formatting | bytes 8388608
  282.5 10.5 %reduce-scatter.9.cloned.1.call-done = bf16[8,65536]{1,0:T(8,128)(2,1)} async-done(((bf16[32,65536]{1,0:T(8,128)(2,1)}), bf16[8,65536]{1,0:T(8,128)(2,1)}) %reduce-scatter.9.cloned.1.call-update) | async-done | bytes 1048592
  293.0 48.9 %reduce-scatter.7.cloned.1.call-done = bf16[8,65536]{1,0:T(8,128)(2,1)} async-done(((bf16[32,65536]{1,0:T(8,128)(2,1)}), bf16[8,65536]{1,0:T(8,128)(2,1)}) %reduce-scatter.7.cloned.1.call-update) | async-done | bytes 1048592
  341.9 2.5 add_convert_fusion
  344.4 7.3 %all-to-all-start.1 = ((bf16[8,16,4096]{2,0,1:T(8,128)(2,1)}), bf16[8,16,4096]{2,0,1:T(8,128)(2,1)}, u32[]{:S(2)}, u32[]{:S(2)}) async-start(bf16[8,16,4096]{2,0,1:T(8,128)(2,1)} %add_convert_fusion), calls=%async_computation.1 | async-start | bytes 2097152 | tf_op jit(solution)/shard_map/all_to_all | solution.py:172
  352.6 16.9 %all-to-all-done.1 = bf16[8,16,4096]{2,0,1:T(8,128)(2,1)} async-done(((bf16[8,16,4096]{2,0,1:T(8,128)(2,1)}), bf16[8,16,4096]{2,0,1:T(8,128)(2,1)}, u32[]{:S(2)}, u32[]{:S(2)}) %all-to-all-start.1) | async-done | bytes 1048608 | tf_op jit(solution)/shard_map/all_to_all | solution.py:172
  369.5 1.8 copy.59
  371.3 1.7 gather_fusion
  373.0 1.7 reshape.288
  374.7 1.4 multiply_reduce_fusion.1
  376.1 0.8 add_convert_fusion.1
  (117 shorter events, 10.6 us)
Async XLA Ops:
  6.5 3.8 copy-start
  6.5 76.0 %all-gather.2.cloned.1.call-start = ((), (), s32[]{:S(2)}) async-start(), calls=%async_computation.4 | async-start | bytes 8650752 | tf_op jit(solution)/shard_map/all_gather | solution.py:123
  7.3 127.3 %all-reduce.2.cloned.1.call-start = ((), (), s32[]{:S(2)}) async-start(), calls=%async_computation.5 | async-start | bytes 2162688 | tf_op jit(solution)/shard_map/psum | solution.py:127
  11.2 2.4 collective-permute-start
  14.6 16.5 %collective-permute-start.1 = (bf16[16,8320]{1,0:T(8,128)(2,1)S(1)}, bf16[16,8320]{1,0:T(8,128)(2,1)S(1)}, u32[]{:S(2)}, u32[]{:S(2)}) collective-permute-start(bf16[16,8320]{1,0:T(8,128)(2,1)S(1)} %pad_maximum_fusion.2), channel_id=1, source_target_pairs={{0,8},{4,12},{8,16},{12,20},{16,24},{20,28},{24,32},{28,36},{32,40... | collective-permute-start | bytes 798728 | tf_op jit(solution)/shard_map/ppermute | solution.py:32
  32.0 10.5 %collective-permute-start.2 = (bf16[16,8320]{1,0:T(8,128)(2,1)S(1)}, bf16[16,8320]{1,0:T(8,128)(2,1)S(1)}, u32[]{:S(2)}, u32[]{:S(2)}) collective-permute-start(bf16[16,8320]{1,0:T(8,128)(2,1)S(1)} %pad_maximum_fusion.3), channel_id=1, source_target_pairs={{0,16},{4,20},{8,24},{12,28},{16,32},{20,36},{24,40},{28,44},{32,4... | collective-permute-start | bytes 798728 | tf_op jit(solution)/shard_map/ppermute | solution.py:32
  44.0 18.1 %collective-permute-start.3 = (bf16[16,8320]{1,0:T(8,128)(2,1)}, bf16[16,8320]{1,0:T(8,128)(2,1)S(1)}, u32[]{:S(2)}, u32[]{:S(2)}) collective-permute-start(bf16[16,8320]{1,0:T(8,128)(2,1)} %pad_maximum_fusion.4), channel_id=1, source_target_pairs={{0,32},{4,36},{8,40},{12,44},{16,48},{20,52},{24,56},{28,60},{32,6... | collective-permute-start | bytes 798728 | tf_op jit(solution)/shard_map/ppermute | solution.py:32
  62.1 0.8 copy-start.3
  62.2 6.3 %copy-start.6 = (bf16[128,128]{1,0:T(8,128)(2,1)S(1)}, bf16[128,128]{1,0:T(8,128)(2,1)}, u32[]{:S(2)}) copy-start(bf16[128,128]{1,0:T(8,128)(2,1)} %param.20) | copy-start | bytes 98308
  63.2 9.3 %collective-permute-start.4 = (bf16[16,8320]{1,0:T(8,128)(2,1)S(1)}, bf16[16,8320]{1,0:T(8,128)(2,1)S(1)}, u32[]{:S(2)}, u32[]{:S(2)}) collective-permute-start(bf16[16,8320]{1,0:T(8,128)(2,1)S(1)} %pad_maximum_fusion.5), channel_id=1, source_target_pairs={{0,64},{4,68},{8,72},{12,76},{16,80},{20,84},{24,88},{28,92},{32,9... | collective-permute-start | bytes 798728 | tf_op jit(solution)/shard_map/ppermute | solution.py:32
  72.8 2.0 copy-start.7
  72.8 2.0 copy-start.9
  72.8 2.0 copy-start.14
  74.8 1.6 copy-start.5
  74.8 7.7 %copy-start.13 = (f32[1024]{0:T(1024)S(1)}, f32[1024]{0:T(1024)}, u32[]{:S(2)}) copy-start(f32[1024]{0:T(1024)} %param.25) | copy-start | bytes 12292
  87.2 1.6 copy-start.10
  88.5 47.6 %copy-start.4 = (bf16[128,4096]{1,0:T(8,128)(2,1)S(1)}, bf16[128,4096]{1,0:T(8,128)(2,1)}, u32[]{:S(2)}) copy-start(bf16[128,4096]{1,0:T(8,128)(2,1)} %param.27) | copy-start | bytes 3145732
  88.5 204.5 %reduce-scatter.9.cloned.1.call-start = ((), (), s32[]{:S(2)}) async-start(), calls=%async_computation.7 | async-start | bytes 5242880
  136.0 0.7 copy-start.8
  149.9 70.3 %slice-start = ((s8[7340032]{0:T(1024)(128)(4,1)}), s8[4194304]{0:T(1024)(128)(4,1)S(1)}, s32[]{:S(2)}) async-start(s8[7340032]{0:T(1024)(128)(4,1)} %bitcast.185), calls=%async_computation.8 | async-start | bytes 8388608
  206.3 13.9 %slice-start.1 = ((s8[7340032]{0:T(1024)(128)(4,1)}), s8[3145728]{0:T(1024)(128)(4,1)S(1)}, s32[]{:S(2)}) async-start(s8[7340032]{0:T(1024)(128)(4,1)} %bitcast.185), calls=%async_computation.9 | async-start | bytes 6291456
  208.6 1.9 copy-start.2
  210.6 7.7 %collective-permute-start.5 = (bf16[32,16,4096]{2,1,0:T(8,128)(2,1)S(1)}, bf16[32,16,4096]{2,1,0:T(8,128)(2,1)S(1)}, u32[]{:S(2)}, u32[]{:S(2)}) collective-permute-start(bf16[32,16,4096]{2,1,0:T(8,128)(2,1)S(1)} %copy.55), channel_id=1, source_target_pairs={{0,4},{4,0},{1,5},{5,1},{2,6},{6,2},{3,7},{7,3},{8,12},{12,8},{9,1... | collective-permute-start | bytes 12582920 | tf_op jit(solution)/shard_map/ppermute | solution.py:155
  218.2 2.0 copy-start.12
  249.0 92.9 %reduce-scatter.7.cloned.1.call-start = ((), (), s32[]{:S(2)}) async-start(), calls=%async_computation.6 | async-start | bytes 5242880
  293.0 48.9 %collective-permute-start.6 = (bf16[8,16,4096]{2,0,1:T(8,128)(2,1)}, bf16[8,16,4096]{2,0,1:T(8,128)(2,1)S(1)}, u32[]{:S(2)}, u32[]{:S(2)}) collective-permute-start(bf16[8,16,4096]{2,0,1:T(8,128)(2,1)} %bitcast.189), channel_id=1, source_target_pairs={{0,4},{4,0},{1,5},{5,1},{2,6},{6,2},{3,7},{7,3},{8,12},{12,8},{9,1... | collective-permute-start | bytes 3145736 | tf_op jit(solution)/shard_map/ppermute | solution.py:170
  341.9 10.3 %copy-start.11 = (f32[128,2]{0,1:T(2,128)S(1)}, f32[128,2]{0,1:T(2,128)}, u32[]{:S(2)}) copy-start(f32[128,2]{0,1:T(2,128)} %param.33) | copy-start | bytes 3076
  344.4 25.1 %all-to-all-start.1 = ((bf16[8,16,4096]{2,0,1:T(8,128)(2,1)}), bf16[8,16,4096]{2,0,1:T(8,128)(2,1)}, u32[]{:S(2)}, u32[]{:S(2)}) async-start(bf16[8,16,4096]{2,0,1:T(8,128)(2,1)} %add_convert_fusion), calls=%async_computation.1 | async-start | bytes 2097152 | tf_op jit(solution)/shard_map/all_to_all | solution.py:172
  371.3 5.6 %copy-start.1 = (bf16[128,128]{1,0:T(8,128)(2,1)S(1)}, bf16[128,128]{1,0:T(8,128)(2,1)}, u32[]{:S(2)}) copy-start(bf16[128,128]{1,0:T(8,128)(2,1)} %param.19) | copy-start | bytes 98308
Sparse Core Ops, SparseCore 0:
  9.5 72.9 all-gather.1
  88.6 45.9 all-reduce.1
  249.1 43.8 reduce-scatter.8
  295.4 46.4 reduce-scatter.6

commit v6 on v5

--- a/solution.py
+++ b/solution.py
@@ -161,14 +161,20 @@
         up_val = jnp.dot(flat, up_rows, preferred_element_type=jnp.float32)
         activated = (jax.nn.silu(gate_val) * up_val).astype(jnp.bfloat16)
         product = jnp.dot(activated, down_rows, preferred_element_type=jnp.float32)
-        return lax.psum_scatter(
-            product.astype(jnp.bfloat16).reshape(rows.shape), "exp", scatter_dimension=0, tiled=True
-        )
+        pieces = product.astype(jnp.bfloat16).reshape((n_exp, capacity) + rows.shape[1:])
+        place = lax.axis_index("exp")
+        total = lax.dynamic_index_in_dim(pieces, place, 0, False).astype(jnp.float32)
+        for shift in range(1, n_exp):
+            outgoing = lax.dynamic_index_in_dim(pieces, (place + shift) % n_exp, 0, False)
+            total = total + lax.ppermute(
+                outgoing, "exp", [(i, (i + shift) % n_exp) for i in range(n_exp)]
+            ).astype(jnp.float32)
+        return total
 
     own_sum = expert_rows(mine)
     partner_sum = expert_rows(other)
-    partner_half = lax.ppermute(partner_sum, "core", swap)
-    both_halves = (own_sum.astype(jnp.float32) + partner_half.astype(jnp.float32)).astype(jnp.bfloat16)
+    partner_half = lax.ppermute(partner_sum.astype(jnp.bfloat16), "core", swap)
+    both_halves = (own_sum + partner_half.astype(jnp.float32)).astype(jnp.bfloat16)
     returned = lax.all_to_all(both_halves, "chip", split_axis=1, concat_axis=1, tiled=True)
     flattened, rank_ids = route_ranks(own_ids, experts)
     fetched = returned.reshape(capacity * experts, model_width)[rank_ids * experts + flattened]

time: 390 us -> 394 us (1.010)
  starting transfers between devices: 37.6 us -> 43 us
  matrix products: 59.6 us -> 63.8 us
  waiting for transfers between devices: 161 us -> 157 us
    ppermute x1 -> x7, waiting for transfers between devices: 0.01 us -> 63 us  [the longest x6 63 us: expert_rows(): lax.ppermute(outgoing, 'exp', [(i, (i + shift) % n_exp) for i in range(n_...]
    unnamed x6 -> x2, waiting for transfers between devices: 60.2 us -> 0.73 us
    unnamed x48 -> x38, local copies, waits for them, and re-layouts: 20 us -> 3.11 us
    dynamic_slice x0 -> x8, local copies, waits for them, and re-layouts: none -> 11.7 us  [the longest x6 6.44 us: expert_rows(): lax.dynamic_index_in_dim(pieces, (place + shift) % n_exp, 0, False)]
    ppermute x1 -> x7, starting transfers between devices: 0.01 us -> 8.3 us  [the longest x6 8.22 us: expert_rows(): lax.ppermute(outgoing, 'exp', [(i, (i + shift) % n_exp) for i in range(n_...]
    ppermute x1, waiting for transfers between devices: 7.15 us -> 0.01 us  [local(): other = lax.ppermute(mine, 'core', swap)]
    dot_general x1, matrix products: 5.81 us -> 10.1 us  [expert_rows(): up_val = jnp.dot(flat, up_rows, preferred_element_type=jnp.float32)]
  transfers between devices with their start and end apart: 12 -> 16, of which waited for: 11 -> 12; matrix products, arithmetic and copies ran while one was open for 13% -> 13% of each run, Pallas kernels for 0% -> 0%
where the time goes in v6:
time: 394 us; the launch traced here: 389 us
  waiting for transfers between devices  157 us (40%)
  matrix products  63.8 us (16%)
  blocking collectives  56.2 us (14%)
  starting transfers between devices  43 us (11%)
  local copies, waits for them, and re-layouts  35.5 us (9%)
  other arithmetic  19.1 us (5%)
  between operations  14.3 us (4%)
    ppermute x6, waiting for transfers between devices, expert_rows(): lax.ppermute(outgoing, 'exp', [(i, (i + shift) % n_exp) for i in range(n_...  63 us
    all_to_all x1, blocking collectives, local(): lax.all_to_all(placed, 'chip', split_axis=1, concat_axis=1, tiled=True)  56.2 us
    psum x1, waiting for transfers between devices, local(): lax.psum(jnp.concatenate([partial_value, jnp.broadcast_to(squares[:, None...  45.4 us
    dot_general x2, matrix products, expert_rows(): product = jnp.dot(activated, down_rows, preferred_element_type=jnp.float32)  33 us
    ppermute x5, starting transfers between devices, entering(): lax.ppermute(packed, axis, [(i, i + hop) for i in range(count - hop)])  29.8 us
    ppermute x5, waiting for transfers between devices, entering(): lax.ppermute(packed, axis, [(i, i + hop) for i in range(count - hop)])  25.2 us
    all_to_all x1, waiting for transfers between devices, local(): lax.all_to_all(both_halves, 'chip', split_axis=1, concat_axis=1, tiled=True)  17.3 us
    dot_general x1, matrix products, expert_rows(): gate_val = jnp.dot(flat, gate_rows, preferred_element_type=jnp.float32)  10.1 us
  transfers between devices with their start and end apart: 16, of which 12 were waited for; matrix products, arithmetic and copies ran while one was open for 13% of the time, Pallas kernels for 0%

profile of v6, /device:TPU:0, one launch (start us, length us, event | category | flops | bytes accessed | tf_op | source)
XLA Modules:
  0.0 389.3 jit_solution(17195872911024073578)
XLA Ops:
  7.3 1.1 copy.45
  11.2 1.3 collective-permute-start
  12.6 1.1 collective-permute-done
  14.6 9.2 %collective-permute-start.1 = (bf16[16,8320]{1,0:T(8,128)(2,1)S(1)}, bf16[16,8320]{1,0:T(8,128)(2,1)S(1)}, u32[]{:S(2)}, u32[]{:S(2)}) collective-permute-start(bf16[16,8320]{1,0:T(8,128)(2,1)S(1)} %pad_maximum_fusion.2), channel_id=1, source_target_pairs={{0,8},{4,12},{8,16},{12,20},{16,24},{20,28},{24,32},{28,36},{32,40... | collective-permute-start | bytes 798728 | tf_op jit(solution)/shard_map/ppermute | solution.py:32
  23.9 7.3 %collective-permute-done.1 = bf16[16,8320]{1,0:T(8,128)(2,1)S(1)} collective-permute-done((bf16[16,8320]{1,0:T(8,128)(2,1)S(1)}, bf16[16,8320]{1,0:T(8,128)(2,1)S(1)}, u32[]{:S(2)}, u32[]{:S(2)}) %collective-permute-start.1) | collective-permute-done | bytes 266272 | tf_op jit(solution)/shard_map/ppermute | solution.py:32
  32.0 6.2 %collective-permute-start.2 = (bf16[16,8320]{1,0:T(8,128)(2,1)S(1)}, bf16[16,8320]{1,0:T(8,128)(2,1)S(1)}, u32[]{:S(2)}, u32[]{:S(2)}) collective-permute-start(bf16[16,8320]{1,0:T(8,128)(2,1)S(1)} %pad_maximum_fusion.3), channel_id=1, source_target_pairs={{0,16},{4,20},{8,24},{12,28},{16,32},{20,36},{24,40},{28,44},{32,4... | collective-permute-start | bytes 798728 | tf_op jit(solution)/shard_map/ppermute | solution.py:32
  38.3 4.1 %collective-permute-done.2 = bf16[16,8320]{1,0:T(8,128)(2,1)S(1)} collective-permute-done((bf16[16,8320]{1,0:T(8,128)(2,1)S(1)}, bf16[16,8320]{1,0:T(8,128)(2,1)S(1)}, u32[]{:S(2)}, u32[]{:S(2)}) %collective-permute-start.2) | collective-permute-done | bytes 266272 | tf_op jit(solution)/shard_map/ppermute | solution.py:32
  44.0 7.2 %collective-permute-start.3 = (bf16[16,8320]{1,0:T(8,128)(2,1)}, bf16[16,8320]{1,0:T(8,128)(2,1)S(1)}, u32[]{:S(2)}, u32[]{:S(2)}) collective-permute-start(bf16[16,8320]{1,0:T(8,128)(2,1)} %pad_maximum_fusion.4), channel_id=1, source_target_pairs={{0,32},{4,36},{8,40},{12,44},{16,48},{20,52},{24,56},{28,60},{32,6... | collective-permute-start | bytes 798728 | tf_op jit(solution)/shard_map/ppermute | solution.py:32
  51.2 10.9 %collective-permute-done.3 = bf16[16,8320]{1,0:T(8,128)(2,1)S(1)} collective-permute-done((bf16[16,8320]{1,0:T(8,128)(2,1)}, bf16[16,8320]{1,0:T(8,128)(2,1)S(1)}, u32[]{:S(2)}, u32[]{:S(2)}) %collective-permute-start.3) | collective-permute-done | bytes 266272 | tf_op jit(solution)/shard_map/ppermute | solution.py:32
  63.2 5.8 %collective-permute-start.4 = (bf16[16,8320]{1,0:T(8,128)(2,1)S(1)}, bf16[16,8320]{1,0:T(8,128)(2,1)S(1)}, u32[]{:S(2)}, u32[]{:S(2)}) collective-permute-start(bf16[16,8320]{1,0:T(8,128)(2,1)S(1)} %pad_maximum_fusion.5), channel_id=1, source_target_pairs={{0,64},{4,68},{8,72},{12,76},{16,80},{20,84},{24,88},{28,92},{32,9... | collective-permute-start | bytes 798728 | tf_op jit(solution)/shard_map/ppermute | solution.py:32
  70.7 1.8 collective-permute-done.4
  72.8 1.6 fusion.51
  74.8 1.4 fusion.29
  76.7 5.8 %all-gather.2.cloned.1.call-done = bf16[1024,4096]{1,0:T(8,128)(2,1)} async-done(((bf16[1024,128]{1,0:T(8,128)(2,1)}), bf16[1024,4096]{1,0:T(8,128)(2,1)}) %all-gather.2.cloned.1.call-update) | async-done | bytes 8388624 | tf_op jit(solution)/shard_map/all_gather | solution.py:123
  82.5 4.7 %convolution_convert_fusion.1 = bf16[128,4096]{1,0:T(8,128)(2,1)S(1)} fusion(bf16[1024,4096]{1,0:T(8,128)(2,1)} %all-gather.2.cloned.1.call-done, f32[1024]{0:T(1024)S(1)} %copy-done.11, f32[128,1024]{1,0:T(8,128)S(1)} %copy.46, bf16[128,1024]{1,0:T(8,128)(2,1)S(1)} %copy-done.4), kind=kOutput, calls=%fused_computation.16 | convolution fusion | flops 1075314688 | bytes 10227712 | tf_op jit(solution)/shard_map/dot_general | solution.py:121
  87.3 1.1 pad_maximum_fusion
  89.2 45.4 %all-reduce.2.cloned.1.call-done = bf16[128,4224]{1,0:T(8,128)(2,1)} async-done(((bf16[128,4224]{1,0:T(8,128)(2,1)}), bf16[128,4224]{1,0:T(8,128)(2,1)}) %all-reduce.2.cloned.1.call-update) | async-done | bytes 1081360 | tf_op jit(solution)/shard_map/psum | solution.py:127
  134.6 1.4 convert_element_type.118
  137.1 3.4 broadcast_in_dim.126
  140.5 4.1 %reshape.279 = bf16[4,64,4096]{2,1,0:T(8,128)(2,1)} reshape(bf16[4,32,2,4096]{3,2,1,0:T(2,128)(2,1)} %broadcast_in_dim.126) | data formatting | bytes 4194304 | tf_op jit(solution)/shard_map/vmap()/reshape | solution.py:58
  144.6 2.9 convolution_convert_fusion
  147.6 2.3 copy.48
  149.9 56.2 %all_to_all.10 = bf16[32,16,4096]{2,0,1:T(8,128)(2,1)S(1)} all-to-all(bf16[32,16,4096]{2,0,1:T(8,128)(2,1)S(1)} %copy.48), channel_id=1, replica_groups=mesh['chip'=16,'core'=2,'exp'=4] {'chip'}, dimensions={1} | all-to-all | bytes 8388608 | tf_op jit(solution)/shard_map/all_to_all | solution.py:154
  206.1 4.2 %copy.49 = bf16[32,16,4096]{2,1,0:T(8,128)(2,1)} copy(bf16[32,16,4096]{2,0,1:T(8,128)(2,1)S(1)} %all_to_all.10) | data formatting | bytes 8388608 | tf_op jit(solution)/shard_map/all_to_all | solution.py:154
  210.5 10.1 %fusion.10 = f32[512,896]{1,0:T(8,128)} fusion(bf16[512,4096]{1,0:T(8,128)(2,1)} %bitcast.10, bf16[1,4096,896]{2,1,0:T(8,128)(2,1)} %param.29), kind=kOutput, calls=%fused_computation.11 | convolution fusion | flops 3758096384 | bytes 13369344 | tf_op jit(solution)/shard_map/dot_general | solution.py:160
  220.6 10.1 %fusion.4 = f32[512,896]{1,0:T(8,128)} fusion(bf16[512,4096]{1,0:T(8,128)(2,1)} %bitcast.19, bf16[1,4096,896]{2,1,0:T(8,128)(2,1)} %param.30), kind=kOutput, calls=%fused_computation.5 | convolution fusion | flops 3758096384 | bytes 13369344 | tf_op jit(solution)/shard_map/dot_general | solution.py:161
  230.7 16.5 %fusion.15 = bf16[512,4096]{1,0:T(8,128)(2,1)} fusion(bf16[1,896,4096]{2,1,0:T(8,128)(2,1)} %param.31, f32[512,896]{1,0:T(8,128)} %fusion.4, bf16[512,4096]{1,0:T(8,128)(2,1)} %bitcast.19, bf16[1,4096,896]{2,1,0:T(8,128)(2,1)} %param.29), kind=kOutput, calls=%fused_computation.15 | convolution fusion | flops 7521042432 | bytes 24903680 | tf_op jit(solution)/shard_map/dot_general | solution.py:163
  247.2 2.6 constant_dynamic-slice_fusion.4
  249.8 1.6 copy.92
  251.4 2.3 collective-permute-start.11
  253.7 1.5 copy.93
  256.1 1.6 copy.94
  258.0 16.6 %fusion.12 = bf16[512,4096]{1,0:T(8,128)(2,1)} fusion(bf16[1,896,4096]{2,1,0:T(8,128)(2,1)} %param.31, f32[512,896]{1,0:T(8,128)} %fusion.10, bf16[512,4096]{1,0:T(8,128)(2,1)} %bitcast.10, bf16[1,4096,896]{2,1,0:T(8,128)(2,1)} %param.30), kind=kOutput, calls=%fused_computation.14 | convolution fusion | flops 7521042432 | bytes 24903680 | tf_op jit(solution)/shard_map/dot_general | solution.py:163
  274.6 2.7 constant_dynamic-slice_fusion.8
  277.8 3.2 collective-permute-start.7
  281.6 1.6 collective-permute-start.6
  283.7 16.1 %collective-permute-done.11 = bf16[8,16,4096]{2,0,1:T(8,128)(2,1)} collective-permute-done((bf16[8,16,4096]{2,0,1:T(8,128)(2,1)}, bf16[8,16,4096]{2,0,1:T(8,128)(2,1)}, u32[]{:S(2)}, u32[]{:S(2)}) %collective-permute-start.11) | collective-permute-done | bytes 1048608 | tf_op jit(solution)/shard_map/ppermute | solution.py:169
  299.8 5.8 %collective-permute-done.9 = bf16[8,16,4096]{2,0,1:T(8,128)(2,1)} collective-permute-done((bf16[8,16,4096]{2,0,1:T(8,128)(2,1)}, bf16[8,16,4096]{2,0,1:T(8,128)(2,1)}, u32[]{:S(2)}, u32[]{:S(2)}) %collective-permute-start.9) | collective-permute-done | bytes 1048608 | tf_op jit(solution)/shard_map/ppermute | solution.py:169
  305.6 2.8 fusion.21
  308.6 35.8 %collective-permute-done.7 = bf16[8,16,4096]{2,0,1:T(8,128)(2,1)S(1)} collective-permute-done((bf16[8,16,4096]{2,0,1:T(8,128)(2,1)S(1)}, bf16[8,16,4096]{2,0,1:T(8,128)(2,1)S(1)}, u32[]{:S(2)}, u32[]{:S(2)}) %collective-permute-start.7) | collective-permute-done | bytes 1048608 | tf_op jit(solution)/shard_map/ppermute | solution.py:169
  344.4 5.2 %collective-permute-done.5 = bf16[8,16,4096]{2,0,1:T(8,128)(2,1)S(1)} collective-permute-done((bf16[8,16,4096]{2,0,1:T(8,128)(2,1)S(1)}, bf16[8,16,4096]{2,0,1:T(8,128)(2,1)S(1)}, u32[]{:S(2)}, u32[]{:S(2)}) %collective-permute-start.5) | collective-permute-done | bytes 1048608 | tf_op jit(solution)/shard_map/ppermute | solution.py:169
  349.6 2.2 fusion.25
  351.8 4.7 %all-to-all-start.1 = ((bf16[8,16,4096]{2,0,1:T(8,128)(2,1)}), bf16[8,16,4096]{2,0,1:T(8,128)(2,1)}, u32[]{:S(2)}, u32[]{:S(2)}) async-start(bf16[8,16,4096]{2,0,1:T(8,128)(2,1)} %fusion.25), calls=%async_computation.1 | async-start | bytes 2097152 | tf_op jit(solution)/shard_map/all_to_all | solution.py:178
  357.5 17.3 %all-to-all-done.1 = bf16[8,16,4096]{2,0,1:T(8,128)(2,1)} async-done(((bf16[8,16,4096]{2,0,1:T(8,128)(2,1)}), bf16[8,16,4096]{2,0,1:T(8,128)(2,1)}, u32[]{:S(2)}, u32[]{:S(2)}) %all-to-all-start.1) | async-done | bytes 1048608 | tf_op jit(solution)/shard_map/all_to_all | solution.py:178
  374.8 1.8 copy.59
  376.6 1.7 gather_fusion
  378.3 1.7 reshape.294
  380.0 1.4 multiply_reduce_fusion.1
  (121 shorter events, 17.5 us)
Async XLA Ops:
  6.5 3.8 copy-start
  6.5 76.0 %all-gather.2.cloned.1.call-start = ((), (), s32[]{:S(2)}) async-start(), calls=%async_computation.2 | async-start | bytes 8650752 | tf_op jit(solution)/shard_map/all_gather | solution.py:123
  7.3 127.3 %all-reduce.2.cloned.1.call-start = ((), (), s32[]{:S(2)}) async-start(), calls=%async_computation.3 | async-start | bytes 2162688 | tf_op jit(solution)/shard_map/psum | solution.py:127
  11.2 2.4 collective-permute-start
  14.6 16.5 %collective-permute-start.1 = (bf16[16,8320]{1,0:T(8,128)(2,1)S(1)}, bf16[16,8320]{1,0:T(8,128)(2,1)S(1)}, u32[]{:S(2)}, u32[]{:S(2)}) collective-permute-start(bf16[16,8320]{1,0:T(8,128)(2,1)S(1)} %pad_maximum_fusion.2), channel_id=1, source_target_pairs={{0,8},{4,12},{8,16},{12,20},{16,24},{20,28},{24,32},{28,36},{32,40... | collective-permute-start | bytes 798728 | tf_op jit(solution)/shard_map/ppermute | solution.py:32
  32.0 10.5 %collective-permute-start.2 = (bf16[16,8320]{1,0:T(8,128)(2,1)S(1)}, bf16[16,8320]{1,0:T(8,128)(2,1)S(1)}, u32[]{:S(2)}, u32[]{:S(2)}) collective-permute-start(bf16[16,8320]{1,0:T(8,128)(2,1)S(1)} %pad_maximum_fusion.3), channel_id=1, source_target_pairs={{0,16},{4,20},{8,24},{12,28},{16,32},{20,36},{24,40},{28,44},{32,4... | collective-permute-start | bytes 798728 | tf_op jit(solution)/shard_map/ppermute | solution.py:32
  44.0 18.1 %collective-permute-start.3 = (bf16[16,8320]{1,0:T(8,128)(2,1)}, bf16[16,8320]{1,0:T(8,128)(2,1)S(1)}, u32[]{:S(2)}, u32[]{:S(2)}) collective-permute-start(bf16[16,8320]{1,0:T(8,128)(2,1)} %pad_maximum_fusion.4), channel_id=1, source_target_pairs={{0,32},{4,36},{8,40},{12,44},{16,48},{20,52},{24,56},{28,60},{32,6... | collective-permute-start | bytes 798728 | tf_op jit(solution)/shard_map/ppermute | solution.py:32
  62.1 0.8 copy-start.2
  62.2 6.8 %copy-start.5 = (bf16[128,128]{1,0:T(8,128)(2,1)S(1)}, bf16[128,128]{1,0:T(8,128)(2,1)}, u32[]{:S(2)}) copy-start(bf16[128,128]{1,0:T(8,128)(2,1)} %param.20) | copy-start | bytes 98308
  63.2 9.3 %collective-permute-start.4 = (bf16[16,8320]{1,0:T(8,128)(2,1)S(1)}, bf16[16,8320]{1,0:T(8,128)(2,1)S(1)}, u32[]{:S(2)}, u32[]{:S(2)}) collective-permute-start(bf16[16,8320]{1,0:T(8,128)(2,1)S(1)} %pad_maximum_fusion.5), channel_id=1, source_target_pairs={{0,64},{4,68},{8,72},{12,76},{16,80},{20,84},{24,88},{28,92},{32,9... | collective-permute-start | bytes 798728 | tf_op jit(solution)/shard_map/ppermute | solution.py:32
  72.8 2.0 copy-start.6
  72.8 2.0 copy-start.8
  72.8 2.0 copy-start.12
  74.8 1.6 copy-start.4
  74.8 7.7 %copy-start.11 = (f32[1024]{0:T(1024)S(1)}, f32[1024]{0:T(1024)}, u32[]{:S(2)}) copy-start(f32[1024]{0:T(1024)} %param.25) | copy-start | bytes 12292
  87.2 1.2 copy-start.9
  88.5 47.6 %copy-start.3 = (bf16[128,4096]{1,0:T(8,128)(2,1)S(1)}, bf16[128,4096]{1,0:T(8,128)(2,1)}, u32[]{:S(2)}) copy-start(bf16[128,4096]{1,0:T(8,128)(2,1)} %param.27) | copy-start | bytes 3145732
  136.1 0.7 copy-start.7
  210.3 10.3 %collective-permute-start.8 = (bf16[32,16,4096]{2,1,0:T(8,128)(2,1)}, bf16[32,16,4096]{2,1,0:T(8,128)(2,1)}, u32[]{:S(2)}, u32[]{:S(2)}) collective-permute-start(bf16[32,16,4096]{2,1,0:T(8,128)(2,1)} %copy.49), channel_id=1, source_target_pairs={{0,4},{4,0},{1,5},{5,1},{2,6},{6,2},{3,7},{7,3},{8,12},{12,8},{9,1... | collective-permute-start | bytes 12582920 | tf_op jit(solution)/shard_map/ppermute | solution.py:155
  251.4 48.4 %collective-permute-start.11 = (bf16[8,16,4096]{2,0,1:T(8,128)(2,1)}, bf16[8,16,4096]{2,0,1:T(8,128)(2,1)}, u32[]{:S(2)}, u32[]{:S(2)}) collective-permute-start(bf16[8,16,4096]{2,0,1:T(8,128)(2,1)} %bitcast.171), channel_id=1, source_target_pairs={{0,3},{1,0},{2,1},{3,2},{4,7},{5,4},{6,5},{7,6},{8,11},{9,8},{10,9... | collective-permute-start | bytes 3145736 | tf_op jit(solution)/shard_map/ppermute | solution.py:169
  255.2 44.6 %collective-permute-start.10 = (bf16[8,16,4096]{2,0,1:T(8,128)(2,1)}, bf16[8,16,4096]{2,0,1:T(8,128)(2,1)}, u32[]{:S(2)}, u32[]{:S(2)}) collective-permute-start(bf16[8,16,4096]{2,0,1:T(8,128)(2,1)} %bitcast.172), channel_id=1, source_target_pairs={{0,2},{1,3},{2,0},{3,1},{4,6},{5,7},{6,4},{7,5},{8,10},{9,11},{10,... | collective-permute-start | bytes 3145736 | tf_op jit(solution)/shard_map/ppermute | solution.py:169
  257.7 48.0 %collective-permute-start.9 = (bf16[8,16,4096]{2,0,1:T(8,128)(2,1)}, bf16[8,16,4096]{2,0,1:T(8,128)(2,1)}, u32[]{:S(2)}, u32[]{:S(2)}) collective-permute-start(bf16[8,16,4096]{2,0,1:T(8,128)(2,1)} %bitcast.173), channel_id=1, source_target_pairs={{0,1},{1,2},{2,3},{3,0},{4,5},{5,6},{6,7},{7,4},{8,9},{9,10},{10,1... | collective-permute-start | bytes 3145736 | tf_op jit(solution)/shard_map/ppermute | solution.py:169
  277.8 66.6 %collective-permute-start.7 = (bf16[8,16,4096]{2,0,1:T(8,128)(2,1)S(1)}, bf16[8,16,4096]{2,0,1:T(8,128)(2,1)S(1)}, u32[]{:S(2)}, u32[]{:S(2)}) collective-permute-start(bf16[8,16,4096]{2,0,1:T(8,128)(2,1)S(1)} %bitcast.191), channel_id=1, source_target_pairs={{0,3},{1,0},{2,1},{3,2},{4,7},{5,4},{6,5},{7,6},{8,11},{9,8},{10,9... | collective-permute-start | bytes 3145736 | tf_op jit(solution)/shard_map/ppermute | solution.py:169
  281.6 62.8 %collective-permute-start.6 = (bf16[8,16,4096]{2,0,1:T(8,128)(2,1)S(1)}, bf16[8,16,4096]{2,0,1:T(8,128)(2,1)S(1)}, u32[]{:S(2)}, u32[]{:S(2)}) collective-permute-start(bf16[8,16,4096]{2,0,1:T(8,128)(2,1)S(1)} %bitcast.192), channel_id=1, source_target_pairs={{0,2},{1,3},{2,0},{3,1},{4,6},{5,7},{6,4},{7,5},{8,10},{9,11},{10,... | collective-permute-start | bytes 3145736 | tf_op jit(solution)/shard_map/ppermute | solution.py:169
  299.8 49.8 %collective-permute-start.5 = (bf16[8,16,4096]{2,0,1:T(8,128)(2,1)S(1)}, bf16[8,16,4096]{2,0,1:T(8,128)(2,1)S(1)}, u32[]{:S(2)}, u32[]{:S(2)}) collective-permute-start(bf16[8,16,4096]{2,0,1:T(8,128)(2,1)S(1)} %bitcast.193), channel_id=1, source_target_pairs={{0,1},{1,2},{2,3},{3,0},{4,5},{5,6},{6,7},{7,4},{8,9},{9,10},{10,1... | collective-permute-start | bytes 3145736 | tf_op jit(solution)/shard_map/ppermute | solution.py:169
  308.5 41.1 %collective-permute-start.12 = (bf16[8,16,4096]{2,0,1:T(8,128)(2,1)S(1)}, bf16[8,16,4096]{2,0,1:T(8,128)(2,1)S(1)}, u32[]{:S(2)}, u32[]{:S(2)}) collective-permute-start(bf16[8,16,4096]{2,0,1:T(8,128)(2,1)S(1)} %fusion.21), channel_id=1, source_target_pairs={{0,4},{4,0},{1,5},{5,1},{2,6},{6,2},{3,7},{7,3},{8,12},{12,8},{9,1... | collective-permute-start | bytes 3145736 | tf_op jit(solution)/shard_map/ppermute | solution.py:176
  351.8 5.3 %copy-start.10 = (f32[128,2]{0,1:T(2,128)S(1)}, f32[128,2]{0,1:T(2,128)}, u32[]{:S(2)}) copy-start(f32[128,2]{0,1:T(2,128)} %param.33) | copy-start | bytes 3076
  351.8 23.0 %all-to-all-start.1 = ((bf16[8,16,4096]{2,0,1:T(8,128)(2,1)}), bf16[8,16,4096]{2,0,1:T(8,128)(2,1)}, u32[]{:S(2)}, u32[]{:S(2)}) async-start(bf16[8,16,4096]{2,0,1:T(8,128)(2,1)} %fusion.25), calls=%async_computation.1 | async-start | bytes 2097152 | tf_op jit(solution)/shard_map/all_to_all | solution.py:178
  376.6 5.6 %copy-start.1 = (bf16[128,128]{1,0:T(8,128)(2,1)S(1)}, bf16[128,128]{1,0:T(8,128)(2,1)}, u32[]{:S(2)}) copy-start(bf16[128,128]{1,0:T(8,128)(2,1)} %param.19) | copy-start | bytes 98308
Sparse Core Ops, SparseCore 0:
  9.5 72.9 all-gather.1
  88.6 45.9 all-reduce.1

commit v7 on v6

--- a/solution.py
+++ b/solution.py
@@ -151,8 +151,6 @@
     )
     placed = placed.reshape(n_exp * capacity, experts, model_width)
     swap = [(0, 1), (1, 0)]
-    mine = lax.all_to_all(placed, "chip", split_axis=1, concat_axis=1, tiled=True)
-    other = lax.ppermute(mine, "core", swap)
     hidden_own = lax.dynamic_slice_in_dim(hidden_all, first_row, tok_quarter, 0)
 
     def expert_rows(rows):
@@ -161,7 +159,7 @@
         up_val = jnp.dot(flat, up_rows, preferred_element_type=jnp.float32)
         activated = (jax.nn.silu(gate_val) * up_val).astype(jnp.bfloat16)
         product = jnp.dot(activated, down_rows, preferred_element_type=jnp.float32)
-        pieces = product.astype(jnp.bfloat16).reshape((n_exp, capacity) + rows.shape[1:])
+        pieces = product.astype(jnp.bfloat16).reshape((n_exp, rows.shape[0] // n_exp) + rows.shape[1:])
         place = lax.axis_index("exp")
         total = lax.dynamic_index_in_dim(pieces, place, 0, False).astype(jnp.float32)
         for shift in range(1, n_exp):
@@ -171,10 +169,22 @@
             ).astype(jnp.float32)
         return total
 
-    own_sum = expert_rows(mine)
-    partner_sum = expert_rows(other)
-    partner_half = lax.ppermute(partner_sum.astype(jnp.bfloat16), "core", swap)
-    both_halves = (own_sum + partner_half.astype(jnp.float32)).astype(jnp.bfloat16)
+    swap = [(0, 1), (1, 0)]
+    by_quarter = placed.reshape(n_exp, capacity, experts, model_width)
+    rank_parts = 2
+    part_rows = capacity // rank_parts
+    finished = []
+    for part in range(rank_parts):
+        chunk = by_quarter[:, part * part_rows : (part + 1) * part_rows].reshape(
+            n_exp * part_rows, experts, model_width
+        )
+        mine = lax.all_to_all(chunk, "chip", split_axis=1, concat_axis=1, tiled=True)
+        other = lax.ppermute(mine, "core", swap)
+        own_sum = expert_rows(mine)
+        partner_sum = expert_rows(other)
+        partner_half = lax.ppermute(partner_sum.astype(jnp.bfloat16), "core", swap)
+        finished.append((own_sum + partner_half.astype(jnp.float32)).astype(jnp.bfloat16))
+    both_halves = jnp.concatenate(finished, axis=0)
     returned = lax.all_to_all(both_halves, "chip", split_axis=1, concat_axis=1, tiled=True)
     flattened, rank_ids = route_ranks(own_ids, experts)
     fetched = returned.reshape(capacity * experts, model_width)[rank_ids * experts + flattened]

time: 394 us -> 406 us (1.030)
  blocking collectives: 56.2 us -> 0 us
  starting transfers between devices: 43 us -> 72.7 us
  local copies, waits for them, and re-layouts: 35.5 us -> 52.6 us
  matrix products: 63.8 us -> 80.3 us
  other arithmetic: 19.1 us -> 23.5 us
    all_to_all x1 -> x0, blocking collectives: 56.2 us -> none  [local(): lax.all_to_all(placed, 'chip', split_axis=1, concat_axis=1, tiled=True)]
    all_to_all x0 -> x2, waiting for transfers between devices: none -> 24.4 us  [local(): lax.all_to_all(chunk, 'chip', split_axis=1, concat_axis=1, tiled=True)]
    ppermute x6 -> x12, waiting for transfers between devices: 63 us -> 45.7 us  [expert_rows(): lax.ppermute(outgoing, 'exp', [(i, (i + shift) % n_exp) for i in range(n_...]
    dot_general x2 -> x4, matrix products: 33 us -> 47 us  [expert_rows(): product = jnp.dot(activated, down_rows, preferred_element_type=jnp.float32)]
    all_to_all x0 -> x2, starting transfers between devices: none -> 11.9 us  [local(): lax.all_to_all(chunk, 'chip', split_axis=1, concat_axis=1, tiled=True)]
    ppermute x6 -> x12, starting transfers between devices: 8.22 us -> 18.8 us  [expert_rows(): lax.ppermute(outgoing, 'exp', [(i, (i + shift) % n_exp) for i in range(n_...]
    all_gather x1, waiting for transfers between devices: 5.84 us -> 0.01 us  [local(): lax.all_gather(out_proj, CTX, axis=1, tiled=True)]
    ppermute x5, starting transfers between devices: 29.8 us -> 34.4 us  [entering(): lax.ppermute(packed, axis, [(i, i + hop) for i in range(count - hop)])]
  transfers between devices with their start and end apart: 16 -> 26, of which waited for: 12 -> 15; matrix products, arithmetic and copies ran while one was open for 13% -> 31% of each run, Pallas kernels for 0% -> 0%
where the time goes in v7:
time: 406 us; the launch traced here: 400 us
  waiting for transfers between devices  156 us (38%)
  matrix products  80.3 us (20%)
  starting transfers between devices  72.7 us (18%)
  local copies, waits for them, and re-layouts  52.6 us (13%)
  other arithmetic  23.5 us (6%)
  between operations  14.7 us (4%)
    dot_general x4, matrix products, expert_rows(): product = jnp.dot(activated, down_rows, preferred_element_type=jnp.float32)  47 us
    ppermute x12, waiting for transfers between devices, expert_rows(): lax.ppermute(outgoing, 'exp', [(i, (i + shift) % n_exp) for i in range(n_...  45.7 us
    psum x1, waiting for transfers between devices, local(): lax.psum(jnp.concatenate([partial_value, jnp.broadcast_to(squares[:, None...  44.3 us
    ppermute x5, starting transfers between devices, entering(): lax.ppermute(packed, axis, [(i, i + hop) for i in range(count - hop)])  34.4 us
    ppermute x5, waiting for transfers between devices, entering(): lax.ppermute(packed, axis, [(i, i + hop) for i in range(count - hop)])  25 us
    all_to_all x2, waiting for transfers between devices, local(): lax.all_to_all(chunk, 'chip', split_axis=1, concat_axis=1, tiled=True)  24.4 us
    ppermute x12, starting transfers between devices, expert_rows(): lax.ppermute(outgoing, 'exp', [(i, (i + shift) % n_exp) for i in range(n_...  18.8 us
    all_to_all x1, waiting for transfers between devices, local(): lax.all_to_all(both_halves, 'chip', split_axis=1, concat_axis=1, tiled=True)  15.9 us
  transfers between devices with their start and end apart: 26, of which 15 were waited for; matrix products, arithmetic and copies ran while one was open for 31% of the time, Pallas kernels for 0%

profile of v7, /device:TPU:0, one launch (start us, length us, event | category | flops | bytes accessed | tf_op | source)
XLA Modules:
  0.0 399.8 jit_solution(6379434687438681393)
XLA Ops:
  15.7 9.2 %collective-permute-start.1 = (bf16[16,8320]{1,0:T(8,128)(2,1)S(1)}, bf16[16,8320]{1,0:T(8,128)(2,1)S(1)}, u32[]{:S(2)}, u32[]{:S(2)}) collective-permute-start(bf16[16,8320]{1,0:T(8,128)(2,1)S(1)} %pad_maximum_fusion.3), channel_id=1, source_target_pairs={{0,8},{4,12},{8,16},{12,20},{16,24},{20,28},{24,32},{28,36},{32,40... | collective-permute-start | bytes 798728 | tf_op jit(solution)/shard_map/ppermute | solution.py:32
  24.9 6.7 %collective-permute-done.1 = bf16[16,8320]{1,0:T(8,128)(2,1)S(1)} collective-permute-done((bf16[16,8320]{1,0:T(8,128)(2,1)S(1)}, bf16[16,8320]{1,0:T(8,128)(2,1)S(1)}, u32[]{:S(2)}, u32[]{:S(2)}) %collective-permute-start.1) | collective-permute-done | bytes 266272 | tf_op jit(solution)/shard_map/ppermute | solution.py:32
  32.8 6.1 %collective-permute-start.2 = (bf16[16,8320]{1,0:T(8,128)(2,1)S(1)}, bf16[16,8320]{1,0:T(8,128)(2,1)S(1)}, u32[]{:S(2)}, u32[]{:S(2)}) collective-permute-start(bf16[16,8320]{1,0:T(8,128)(2,1)S(1)} %pad_maximum_fusion.4), channel_id=1, source_target_pairs={{0,16},{4,20},{8,24},{12,28},{16,32},{20,36},{24,40},{28,44},{32,4... | collective-permute-start | bytes 798728 | tf_op jit(solution)/shard_map/ppermute | solution.py:32
  39.7 3.1 collective-permute-done.2
  44.4 8.3 %collective-permute-start.3 = (bf16[16,8320]{1,0:T(8,128)(2,1)}, bf16[16,8320]{1,0:T(8,128)(2,1)S(1)}, u32[]{:S(2)}, u32[]{:S(2)}) collective-permute-start(bf16[16,8320]{1,0:T(8,128)(2,1)} %pad_maximum_fusion.5), channel_id=1, source_target_pairs={{0,32},{4,36},{8,40},{12,44},{16,48},{20,52},{24,56},{28,60},{32,6... | collective-permute-start | bytes 798728 | tf_op jit(solution)/shard_map/ppermute | solution.py:32
  52.6 6.8 %collective-permute-done.3 = bf16[16,8320]{1,0:T(8,128)(2,1)S(1)} collective-permute-done((bf16[16,8320]{1,0:T(8,128)(2,1)}, bf16[16,8320]{1,0:T(8,128)(2,1)S(1)}, u32[]{:S(2)}, u32[]{:S(2)}) %collective-permute-start.3) | collective-permute-done | bytes 266272 | tf_op jit(solution)/shard_map/ppermute | solution.py:32
  60.5 9.6 %collective-permute-start.4 = (bf16[16,8320]{1,0:T(8,128)(2,1)S(1)}, bf16[16,8320]{1,0:T(8,128)(2,1)S(1)}, u32[]{:S(2)}, u32[]{:S(2)}) collective-permute-start(bf16[16,8320]{1,0:T(8,128)(2,1)S(1)} %pad_maximum_fusion.6), channel_id=1, source_target_pairs={{0,64},{4,68},{8,72},{12,76},{16,80},{20,84},{24,88},{28,92},{32,9... | collective-permute-start | bytes 798728 | tf_op jit(solution)/shard_map/ppermute | solution.py:32
  71.1 7.4 %collective-permute-done.4 = bf16[16,8320]{1,0:T(8,128)(2,1)S(1)} collective-permute-done((bf16[16,8320]{1,0:T(8,128)(2,1)S(1)}, bf16[16,8320]{1,0:T(8,128)(2,1)S(1)}, u32[]{:S(2)}, u32[]{:S(2)}) %collective-permute-start.4) | collective-permute-done | bytes 266272 | tf_op jit(solution)/shard_map/ppermute | solution.py:32
  83.3 4.7 %convolution_convert_fusion.1 = bf16[128,4096]{1,0:T(8,128)(2,1)S(1)} fusion(bf16[1024,4096]{1,0:T(8,128)(2,1)} %all-gather.2.cloned.1.call-done, f32[1024]{0:T(1024)S(1)} %copy-done.19, f32[128,1024]{1,0:T(8,128)S(1)} %copy.55, bf16[128,1024]{1,0:T(8,128)(2,1)S(1)} %copy-done.9), kind=kOutput, calls=%fused_computation.30 | convolution fusion | flops 1075314688 | bytes 10227712 | tf_op jit(solution)/shard_map/dot_general | solution.py:121
  90.0 44.3 %all-reduce.2.cloned.1.call-done = bf16[128,4224]{1,0:T(8,128)(2,1)} async-done(((bf16[128,4224]{1,0:T(8,128)(2,1)}), bf16[128,4224]{1,0:T(8,128)(2,1)}) %all-reduce.2.cloned.1.call-update) | async-done | bytes 1081360 | tf_op jit(solution)/shard_map/psum | solution.py:127
  136.7 3.4 broadcast_in_dim.126
  140.2 4.1 %reshape.301 = bf16[4,64,4096]{2,1,0:T(8,128)(2,1)} reshape(bf16[4,32,2,4096]{3,2,1,0:T(2,128)(2,1)} %broadcast_in_dim.126) | data formatting | bytes 4194304 | tf_op jit(solution)/shard_map/vmap()/reshape | solution.py:58
  144.3 2.9 convolution_convert_fusion
  147.2 1.8 fusion.152
  149.0 2.5 copy.83
  151.5 7.0 %all-to-all-start = ((bf16[16,16,4096]{2,0,1:T(8,128)(2,1)}), bf16[16,16,4096]{2,0,1:T(8,128)(2,1)}, u32[]{:S(2)}, u32[]{:S(2)}) async-start(bf16[16,16,4096]{2,0,1:T(8,128)(2,1)} %copy.83), calls=%async_computation | async-start | bytes 4194304 | tf_op jit(solution)/shard_map/all_to_all | solution.py:181
  158.6 4.1 %copy.84 = bf16[16,16,4096]{2,0,1:T(8,128)(2,1)} copy(bf16[16,16,4096]{2,1,0:T(8,128)(2,1)} %bitcast.250) | data formatting | bytes 4194304 | tf_op jit(solution)/shard_map/reshape | solution.py:178
  162.7 24.4 %all-to-all-done = bf16[16,16,4096]{2,0,1:T(8,128)(2,1)} async-done(((bf16[16,16,4096]{2,0,1:T(8,128)(2,1)}), bf16[16,16,4096]{2,0,1:T(8,128)(2,1)}, u32[]{:S(2)}, u32[]{:S(2)}) %all-to-all-start) | async-done | bytes 2097184 | tf_op jit(solution)/shard_map/all_to_all | solution.py:181
  187.1 4.8 %all-to-all-start.1 = ((bf16[16,16,4096]{2,0,1:T(8,128)(2,1)}), bf16[16,16,4096]{2,0,1:T(8,128)(2,1)}, u32[]{:S(2)}, u32[]{:S(2)}) async-start(bf16[16,16,4096]{2,0,1:T(8,128)(2,1)} %copy.84), calls=%async_computation.1 | async-start | bytes 4194304 | tf_op jit(solution)/shard_map/all_to_all | solution.py:181
  191.9 4.1 %copy.58 = bf16[16,16,4096]{2,1,0:T(8,128)(2,1)} copy(bf16[16,16,4096]{2,0,1:T(8,128)(2,1)} %all-to-all-done) | data formatting | bytes 4194304 | tf_op jit(solution)/shard_map/all_to_all | solution.py:181
  196.0 6.1 %fusion.22 = f32[256,896]{1,0:T(8,128)S(1)} fusion(bf16[256,4096]{1,0:T(8,128)(2,1)} %bitcast.11, bf16[1,4096,896]{2,1,0:T(8,128)(2,1)} %param.29), kind=kOutput, calls=%fused_computation.23 | convolution fusion | flops 1879048192 | bytes 10354688 | tf_op jit(solution)/shard_map/dot_general | solution.py:158
  202.1 11.7 %fusion.24 = bf16[256,4096]{1,0:T(8,128)(2,1)} fusion(bf16[1,896,4096]{2,1,0:T(8,128)(2,1)} %param.31, bf16[256,4096]{1,0:T(8,128)(2,1)} %bitcast.11, bf16[1,4096,896]{2,1,0:T(8,128)(2,1)} %param.30, f32[256,896]{1,0:T(8,128)S(1)} %fusion.22), kind=kOutput, calls=%fused_computation.26 | convolution fusion | flops 3760521216 | bytes 19791872 | tf_op jit(solution)/shard_map/dot_general | solution.py:161
  213.7 2.7 constant_dynamic-slice_fusion.16
  219.8 2.7 collective-permute-start.6
  222.5 4.2 %copy.69 = bf16[16,16,4096]{2,1,0:T(8,128)(2,1)} copy(bf16[16,16,4096]{2,0,1:T(8,128)(2,1)} %all-to-all-done.1) | data formatting | bytes 4194304 | tf_op jit(solution)/shard_map/all_to_all | solution.py:181
  226.9 7.2 %fusion.18 = f32[256,896]{1,0:T(8,128)} fusion(bf16[256,4096]{1,0:T(8,128)(2,1)} %bitcast.27, bf16[1,4096,896]{2,1,0:T(8,128)(2,1)} %param.29), kind=kOutput, calls=%fused_computation.19 | convolution fusion | flops 1879048192 | bytes 10354688 | tf_op jit(solution)/shard_map/dot_general | solution.py:158
  234.1 4.0 %fusion.12 = f32[256,896]{1,0:T(8,128)S(1)} fusion(bf16[256,4096]{1,0:T(8,128)(2,1)} %bitcast.20, bf16[1,4096,896]{2,1,0:T(8,128)(2,1)S(1)} %bitcast.278), kind=kOutput, calls=%fused_computation.13 | convolution fusion | flops 1879048192 | bytes 10354688 | tf_op jit(solution)/shard_map/dot_general | solution.py:159
  238.2 11.6 %fusion.27 = bf16[256,4096]{1,0:T(8,128)(2,1)} fusion(bf16[1,896,4096]{2,1,0:T(8,128)(2,1)} %param.31, f32[256,896]{1,0:T(8,128)S(1)} %fusion.12, bf16[256,4096]{1,0:T(8,128)(2,1)} %bitcast.20, bf16[1,4096,896]{2,1,0:T(8,128)(2,1)} %param.29), kind=kOutput, calls=%fused_computation.27 | convolution fusion | flops 3760521216 | bytes 19791872 | tf_op jit(solution)/shard_map/dot_general | solution.py:161
  249.8 6.1 %fusion.8 = f32[256,896]{1,0:T(8,128)S(1)} fusion(bf16[256,4096]{1,0:T(8,128)(2,1)} %bitcast.33, bf16[1,4096,896]{2,1,0:T(8,128)(2,1)} %param.30), kind=kOutput, calls=%fused_computation.9 | convolution fusion | flops 1879048192 | bytes 10354688 | tf_op jit(solution)/shard_map/dot_general | solution.py:159
  255.8 11.9 %fusion.33 = bf16[256,4096]{1,0:T(8,128)(2,1)} fusion(bf16[1,896,4096]{2,1,0:T(8,128)(2,1)} %param.31, f32[256,896]{1,0:T(8,128)S(1)} %fusion.8, bf16[256,4096]{1,0:T(8,128)(2,1)} %bitcast.33, bf16[1,4096,896]{2,1,0:T(8,128)(2,1)} %param.29), kind=kOutput, calls=%fused_computation.29 | convolution fusion | flops 3760521216 | bytes 19791872 | tf_op jit(solution)/shard_map/dot_general | solution.py:161
  267.7 3.5 constant_dynamic-slice_fusion.4
  274.4 2.3 collective-permute-start.11
  277.9 11.9 %fusion.30 = bf16[256,4096]{1,0:T(8,128)(2,1)} fusion(bf16[1,896,4096]{2,1,0:T(8,128)(2,1)} %param.31, bf16[256,4096]{1,0:T(8,128)(2,1)} %bitcast.27, bf16[1,4096,896]{2,1,0:T(8,128)(2,1)} %param.30, f32[256,896]{1,0:T(8,128)} %fusion.18), kind=kOutput, calls=%fused_computation.28 | convolution fusion | flops 3760521216 | bytes 19791872 | tf_op jit(solution)/shard_map/dot_general | solution.py:161
  298.1 2.8 collective-permute-start.18
  300.9 2.3 collective-permute-start.19
  303.1 2.2 fusion.61
  305.3 6.2 %collective-permute-done.17 = bf16[4,16,4096]{2,0,1:T(4,128)(2,1)S(1)} collective-permute-done((bf16[4,16,4096]{2,0,1:T(4,128)(2,1)S(1)}, bf16[4,16,4096]{2,0,1:T(4,128)(2,1)S(1)}, u32[]{:S(2)}, u32[]{:S(2)}) %collective-permute-start.17) | collective-permute-done | bytes 524320 | tf_op jit(solution)/shard_map/ppermute | solution.py:167
  311.4 2.2 collective-permute-start.7
  313.7 9.3 %collective-permute-done.18 = bf16[4,16,4096]{2,0,1:T(4,128)(2,1)S(1)} collective-permute-done((bf16[4,16,4096]{2,0,1:T(4,128)(2,1)S(1)}, bf16[4,16,4096]{2,0,1:T(4,128)(2,1)S(1)}, u32[]{:S(2)}, u32[]{:S(2)}) %collective-permute-start.18) | collective-permute-done | bytes 524320 | tf_op jit(solution)/shard_map/ppermute | solution.py:167
  323.0 2.6 collective-permute-done.19
  326.4 2.8 collective-permute-start.14
  330.5 6.4 %collective-permute-done.7 = bf16[4,16,4096]{2,0,1:T(4,128)(2,1)S(1)} collective-permute-done((bf16[4,16,4096]{2,0,1:T(4,128)(2,1)S(1)}, bf16[4,16,4096]{2,0,1:T(4,128)(2,1)S(1)}, u32[]{:S(2)}, u32[]{:S(2)}) %collective-permute-start.7) | collective-permute-done | bytes 524320 | tf_op jit(solution)/shard_map/ppermute | solution.py:167
  336.9 2.1 fusion.65
  339.0 9.0 %collective-permute-done.13 = bf16[4,16,4096]{2,0,1:T(4,128)(2,1)S(1)} collective-permute-done((bf16[4,16,4096]{2,0,1:T(4,128)(2,1)S(1)}, bf16[4,16,4096]{2,0,1:T(4,128)(2,1)S(1)}, u32[]{:S(2)}, u32[]{:S(2)}) %collective-permute-start.13) | collective-permute-done | bytes 524320 | tf_op jit(solution)/shard_map/ppermute | solution.py:167
  348.0 10.5 %collective-permute-done.15 = bf16[4,16,4096]{2,0,1:T(4,128)(2,1)S(1)} collective-permute-done((bf16[4,16,4096]{2,0,1:T(4,128)(2,1)S(1)}, bf16[4,16,4096]{2,0,1:T(4,128)(2,1)S(1)}, u32[]{:S(2)}, u32[]{:S(2)}) %collective-permute-start.15) | collective-permute-done | bytes 524320 | tf_op jit(solution)/shard_map/ppermute | solution.py:167
  361.0 7.3 %all-to-all-start.2 = ((bf16[8,16,4096]{2,0,1:T(8,128)(2,1)}), bf16[8,16,4096]{2,0,1:T(8,128)(2,1)}, u32[]{:S(2)}, u32[]{:S(2)}) async-start(bf16[8,16,4096]{2,0,1:T(8,128)(2,1)} %pad_maximum_fusion.1), calls=%async_computation.2 | async-start | bytes 2097152 | tf_op jit(solution)/shard_map/all_to_all | solution.py:188
  369.3 15.9 %all-to-all-done.2 = bf16[8,16,4096]{2,0,1:T(8,128)(2,1)} async-done(((bf16[8,16,4096]{2,0,1:T(8,128)(2,1)}), bf16[8,16,4096]{2,0,1:T(8,128)(2,1)}, u32[]{:S(2)}, u32[]{:S(2)}) %all-to-all-start.2) | async-done | bytes 1048608 | tf_op jit(solution)/shard_map/all_to_all | solution.py:188
  385.1 1.8 copy.79
  (178 shorter events, 50.9 us)
Async XLA Ops:
  6.5 4.4 %copy-start = (bf16[128,128]{1,0:T(8,128)(2,1)S(1)}, bf16[128,128]{1,0:T(8,128)(2,1)}, u32[]{:S(2)}) copy-start(bf16[128,128]{1,0:T(8,128)(2,1)} %param.19) | copy-start | bytes 98308
  6.5 76.8 %all-gather.2.cloned.1.call-start = ((), (), s32[]{:S(2)}) async-start(), calls=%async_computation.3 | async-start | bytes 8650752 | tf_op jit(solution)/shard_map/all_gather | solution.py:123
  7.3 127.0 %all-reduce.2.cloned.1.call-start = ((), (), s32[]{:S(2)}) async-start(), calls=%async_computation.4 | async-start | bytes 2162688 | tf_op jit(solution)/shard_map/psum | solution.py:127
  11.8 2.4 collective-permute-start
  15.7 16.0 %collective-permute-start.1 = (bf16[16,8320]{1,0:T(8,128)(2,1)S(1)}, bf16[16,8320]{1,0:T(8,128)(2,1)S(1)}, u32[]{:S(2)}, u32[]{:S(2)}) collective-permute-start(bf16[16,8320]{1,0:T(8,128)(2,1)S(1)} %pad_maximum_fusion.3), channel_id=1, source_target_pairs={{0,8},{4,12},{8,16},{12,20},{16,24},{20,28},{24,32},{28,36},{32,40... | collective-permute-start | bytes 798728 | tf_op jit(solution)/shard_map/ppermute | solution.py:32
  31.6 0.8 copy-start.3
  32.8 10.0 %collective-permute-start.2 = (bf16[16,8320]{1,0:T(8,128)(2,1)S(1)}, bf16[16,8320]{1,0:T(8,128)(2,1)S(1)}, u32[]{:S(2)}, u32[]{:S(2)}) collective-permute-start(bf16[16,8320]{1,0:T(8,128)(2,1)S(1)} %pad_maximum_fusion.4), channel_id=1, source_target_pairs={{0,16},{4,20},{8,24},{12,28},{16,32},{20,36},{24,40},{28,44},{32,4... | collective-permute-start | bytes 798728 | tf_op jit(solution)/shard_map/ppermute | solution.py:32
  39.7 3.5 copy-start.15
  43.1 16.3 %copy-start.16 = (f32[16]{0:T(128)}, f32[16]{0:T(128)S(1)}, u32[]{:S(2)}) copy-start(f32[16]{0:T(128)S(1)} %fusion.132) | copy-start | bytes 196
  44.4 15.0 %collective-permute-start.3 = (bf16[16,8320]{1,0:T(8,128)(2,1)}, bf16[16,8320]{1,0:T(8,128)(2,1)S(1)}, u32[]{:S(2)}, u32[]{:S(2)}) collective-permute-start(bf16[16,8320]{1,0:T(8,128)(2,1)} %pad_maximum_fusion.5), channel_id=1, source_target_pairs={{0,32},{4,36},{8,40},{12,44},{16,48},{20,52},{24,56},{28,60},{32,6... | collective-permute-start | bytes 798728 | tf_op jit(solution)/shard_map/ppermute | solution.py:32
  59.4 0.8 copy-start.2
  59.5 10.6 %copy-start.10 = (bf16[128,128]{1,0:T(8,128)(2,1)S(1)}, bf16[128,128]{1,0:T(8,128)(2,1)}, u32[]{:S(2)}) copy-start(bf16[128,128]{1,0:T(8,128)(2,1)} %param.20) | copy-start | bytes 98308
  60.5 18.0 %collective-permute-start.4 = (bf16[16,8320]{1,0:T(8,128)(2,1)S(1)}, bf16[16,8320]{1,0:T(8,128)(2,1)S(1)}, u32[]{:S(2)}, u32[]{:S(2)}) collective-permute-start(bf16[16,8320]{1,0:T(8,128)(2,1)S(1)} %pad_maximum_fusion.6), channel_id=1, source_target_pairs={{0,64},{4,68},{8,72},{12,76},{16,80},{20,84},{24,88},{28,92},{32,9... | collective-permute-start | bytes 798728 | tf_op jit(solution)/shard_map/ppermute | solution.py:32
  78.7 2.3 copy-start.11
  79.5 1.9 copy-start.14
  79.5 1.9 copy-start.20
  81.4 1.6 copy-start.9
  81.4 1.9 copy-start.19
  88.0 1.2 copy-start.17
  89.3 46.5 %copy-start.8 = (bf16[128,4096]{1,0:T(8,128)(2,1)S(1)}, bf16[128,4096]{1,0:T(8,128)(2,1)}, u32[]{:S(2)}) copy-start(bf16[128,4096]{1,0:T(8,128)(2,1)} %param.27) | copy-start | bytes 3145732
  135.7 0.7 copy-start.12
  151.5 35.6 %all-to-all-start = ((bf16[16,16,4096]{2,0,1:T(8,128)(2,1)}), bf16[16,16,4096]{2,0,1:T(8,128)(2,1)}, u32[]{:S(2)}, u32[]{:S(2)}) async-start(bf16[16,16,4096]{2,0,1:T(8,128)(2,1)} %copy.83), calls=%async_computation | async-start | bytes 4194304 | tf_op jit(solution)/shard_map/all_to_all | solution.py:181
  187.1 35.4 %all-to-all-start.1 = ((bf16[16,16,4096]{2,0,1:T(8,128)(2,1)}), bf16[16,16,4096]{2,0,1:T(8,128)(2,1)}, u32[]{:S(2)}, u32[]{:S(2)}) async-start(bf16[16,16,4096]{2,0,1:T(8,128)(2,1)} %copy.84), calls=%async_computation.1 | async-start | bytes 4194304 | tf_op jit(solution)/shard_map/all_to_all | solution.py:181
  196.0 38.1 %collective-permute-start.8 = (bf16[16,16,4096]{2,1,0:T(8,128)(2,1)}, bf16[16,16,4096]{2,1,0:T(8,128)(2,1)}, u32[]{:S(2)}, u32[]{:S(2)}) collective-permute-start(bf16[16,16,4096]{2,1,0:T(8,128)(2,1)} %copy.58), channel_id=1, source_target_pairs={{0,4},{4,0},{1,5},{5,1},{2,6},{6,2},{3,7},{7,3},{8,12},{12,8},{9,1... | collective-permute-start | bytes 6291464 | tf_op jit(solution)/shard_map/ppermute | solution.py:182
  217.6 108.8 %collective-permute-start.5 = (bf16[4,16,4096]{2,0,1:T(4,128)(2,1)}, bf16[4,16,4096]{2,0,1:T(4,128)(2,1)}, u32[]{:S(2)}, u32[]{:S(2)}) collective-permute-start(bf16[4,16,4096]{2,0,1:T(4,128)(2,1)} %bitcast.242), channel_id=1, source_target_pairs={{0,1},{1,2},{2,3},{3,0},{4,5},{5,6},{6,7},{7,4},{8,9},{9,10},{10,1... | collective-permute-start | bytes 1572872 | tf_op jit(solution)/shard_map/ppermute | solution.py:167
  219.8 109.5 %collective-permute-start.6 = (bf16[4,16,4096]{2,0,1:T(4,128)(2,1)}, bf16[4,16,4096]{2,0,1:T(4,128)(2,1)}, u32[]{:S(2)}, u32[]{:S(2)}) collective-permute-start(bf16[4,16,4096]{2,0,1:T(4,128)(2,1)} %bitcast.241), channel_id=1, source_target_pairs={{0,2},{1,3},{2,0},{3,1},{4,6},{5,7},{6,4},{7,5},{8,10},{9,11},{10,... | collective-permute-start | bytes 1572872 | tf_op jit(solution)/shard_map/ppermute | solution.py:167
  222.5 11.6 %slice-start = ((s8[7340032]{0:T(1024)(128)(4,1)}), s8[4194304]{0:T(1024)(128)(4,1)S(1)}, s32[]{:S(2)}) async-start(s8[7340032]{0:T(1024)(128)(4,1)} %bitcast.277), calls=%async_computation.5 | async-start | bytes 8388608
  226.7 23.0 %collective-permute-start.16 = (bf16[16,16,4096]{2,1,0:T(8,128)(2,1)}, bf16[16,16,4096]{2,1,0:T(8,128)(2,1)}, u32[]{:S(2)}, u32[]{:S(2)}) collective-permute-start(bf16[16,16,4096]{2,1,0:T(8,128)(2,1)} %copy.69), channel_id=1, source_target_pairs={{0,4},{4,0},{1,5},{5,1},{2,6},{6,2},{3,7},{7,3},{8,12},{12,8},{9,1... | collective-permute-start | bytes 6291464 | tf_op jit(solution)/shard_map/ppermute | solution.py:182
  226.9 7.2 %slice-start.1 = ((s8[7340032]{0:T(1024)(128)(4,1)}), s8[3145728]{0:T(1024)(128)(4,1)S(1)}, s32[]{:S(2)}) async-start(s8[7340032]{0:T(1024)(128)(4,1)} %bitcast.277), calls=%async_computation.6 | async-start | bytes 6291456
  272.4 23.1 %collective-permute-start.10 = (bf16[4,16,4096]{2,0,1:T(4,128)(2,1)}, bf16[4,16,4096]{2,0,1:T(4,128)(2,1)}, u32[]{:S(2)}, u32[]{:S(2)}) collective-permute-start(bf16[4,16,4096]{2,0,1:T(4,128)(2,1)} %bitcast.238), channel_id=1, source_target_pairs={{0,2},{1,3},{2,0},{3,1},{4,6},{5,7},{6,4},{7,5},{8,10},{9,11},{10,... | collective-permute-start | bytes 1572872 | tf_op jit(solution)/shard_map/ppermute | solution.py:167
  274.4 23.6 %collective-permute-start.11 = (bf16[4,16,4096]{2,0,1:T(4,128)(2,1)}, bf16[4,16,4096]{2,0,1:T(4,128)(2,1)}, u32[]{:S(2)}, u32[]{:S(2)}) collective-permute-start(bf16[4,16,4096]{2,0,1:T(4,128)(2,1)} %bitcast.237), channel_id=1, source_target_pairs={{0,3},{1,0},{2,1},{3,2},{4,7},{5,4},{6,5},{7,6},{8,11},{9,8},{10,9... | collective-permute-start | bytes 1572872 | tf_op jit(solution)/shard_map/ppermute | solution.py:167
  277.9 22.9 %collective-permute-start.9 = (bf16[4,16,4096]{2,0,1:T(4,128)(2,1)}, bf16[4,16,4096]{2,0,1:T(4,128)(2,1)}, u32[]{:S(2)}, u32[]{:S(2)}) collective-permute-start(bf16[4,16,4096]{2,0,1:T(4,128)(2,1)} %bitcast.239), channel_id=1, source_target_pairs={{0,1},{1,2},{2,3},{3,0},{4,5},{5,6},{6,7},{7,4},{8,9},{9,10},{10,1... | collective-permute-start | bytes 1572872 | tf_op jit(solution)/shard_map/ppermute | solution.py:167
  293.0 1.3 copy-start.6
  293.0 1.7 copy-start.5
  293.4 1.7 copy-start.4
  295.5 15.9 %collective-permute-start.17 = (bf16[4,16,4096]{2,0,1:T(4,128)(2,1)S(1)}, bf16[4,16,4096]{2,0,1:T(4,128)(2,1)S(1)}, u32[]{:S(2)}, u32[]{:S(2)}) collective-permute-start(bf16[4,16,4096]{2,0,1:T(4,128)(2,1)S(1)} %bitcast.275), channel_id=1, source_target_pairs={{0,1},{1,2},{2,3},{3,0},{4,5},{5,6},{6,7},{7,4},{8,9},{9,10},{10,1... | collective-permute-start | bytes 1572872 | tf_op jit(solution)/shard_map/ppermute | solution.py:167
  298.1 24.9 %collective-permute-start.18 = (bf16[4,16,4096]{2,0,1:T(4,128)(2,1)S(1)}, bf16[4,16,4096]{2,0,1:T(4,128)(2,1)S(1)}, u32[]{:S(2)}, u32[]{:S(2)}) collective-permute-start(bf16[4,16,4096]{2,0,1:T(4,128)(2,1)S(1)} %bitcast.274), channel_id=1, source_target_pairs={{0,2},{1,3},{2,0},{3,1},{4,6},{5,7},{6,4},{7,5},{8,10},{9,11},{10,... | collective-permute-start | bytes 1572872 | tf_op jit(solution)/shard_map/ppermute | solution.py:167
  300.9 24.8 %collective-permute-start.19 = (bf16[4,16,4096]{2,0,1:T(4,128)(2,1)S(1)}, bf16[4,16,4096]{2,0,1:T(4,128)(2,1)S(1)}, u32[]{:S(2)}, u32[]{:S(2)}) collective-permute-start(bf16[4,16,4096]{2,0,1:T(4,128)(2,1)S(1)} %bitcast.273), channel_id=1, source_target_pairs={{0,3},{1,0},{2,1},{3,2},{4,7},{5,4},{6,5},{7,6},{8,11},{9,8},{10,9... | collective-permute-start | bytes 1572872 | tf_op jit(solution)/shard_map/ppermute | solution.py:167
  303.1 33.7 %copy-start.7 = (bf16[1,4,16,4096]{3,2,1,0:T(8,128)(2,1)S(1)}, bf16[1,4,16,4096]{3,2,1,0:T(8,128)(2,1)}, u32[]{:S(2)}) copy-start(bf16[1,4,16,4096]{3,2,1,0:T(8,128)(2,1)} %get-tuple-element.19) | copy-start | bytes 1572868
  311.4 25.4 %collective-permute-start.7 = (bf16[4,16,4096]{2,0,1:T(4,128)(2,1)S(1)}, bf16[4,16,4096]{2,0,1:T(4,128)(2,1)S(1)}, u32[]{:S(2)}, u32[]{:S(2)}) collective-permute-start(bf16[4,16,4096]{2,0,1:T(4,128)(2,1)S(1)} %bitcast.272), channel_id=1, source_target_pairs={{0,3},{1,0},{2,1},{3,2},{4,7},{5,4},{6,5},{7,6},{8,11},{9,8},{10,9... | collective-permute-start | bytes 1572872 | tf_op jit(solution)/shard_map/ppermute | solution.py:167
  323.0 25.0 %collective-permute-start.13 = (bf16[4,16,4096]{2,0,1:T(4,128)(2,1)S(1)}, bf16[4,16,4096]{2,0,1:T(4,128)(2,1)S(1)}, u32[]{:S(2)}, u32[]{:S(2)}) collective-permute-start(bf16[4,16,4096]{2,0,1:T(4,128)(2,1)S(1)} %bitcast.271), channel_id=1, source_target_pairs={{0,1},{1,2},{2,3},{3,0},{4,5},{5,6},{6,7},{7,4},{8,9},{9,10},{10,1... | collective-permute-start | bytes 1572872 | tf_op jit(solution)/shard_map/ppermute | solution.py:167
  325.6 11.2 %collective-permute-start.12 = (bf16[4,16,4096]{2,0,1:T(4,128)(2,1)S(1)}, bf16[4,16,4096]{2,0,1:T(4,128)(2,1)S(1)}, u32[]{:S(2)}, u32[]{:S(2)}) collective-permute-start(bf16[4,16,4096]{2,0,1:T(4,128)(2,1)S(1)} %fusion.61), channel_id=1, source_target_pairs={{0,4},{4,0},{1,5},{5,1},{2,6},{6,2},{3,7},{7,3},{8,12},{12,8},{9,1... | collective-permute-start | bytes 1572872 | tf_op jit(solution)/shard_map/ppermute | solution.py:185
  326.4 21.6 %collective-permute-start.14 = (bf16[4,16,4096]{2,0,1:T(4,128)(2,1)S(1)}, bf16[4,16,4096]{2,0,1:T(4,128)(2,1)S(1)}, u32[]{:S(2)}, u32[]{:S(2)}) collective-permute-start(bf16[4,16,4096]{2,0,1:T(4,128)(2,1)S(1)} %bitcast.270), channel_id=1, source_target_pairs={{0,2},{1,3},{2,0},{3,1},{4,6},{5,7},{6,4},{7,5},{8,10},{9,11},{10,... | collective-permute-start | bytes 1572872 | tf_op jit(solution)/shard_map/ppermute | solution.py:167
  329.3 29.2 %collective-permute-start.15 = (bf16[4,16,4096]{2,0,1:T(4,128)(2,1)S(1)}, bf16[4,16,4096]{2,0,1:T(4,128)(2,1)S(1)}, u32[]{:S(2)}, u32[]{:S(2)}) collective-permute-start(bf16[4,16,4096]{2,0,1:T(4,128)(2,1)S(1)} %bitcast.269), channel_id=1, source_target_pairs={{0,3},{1,0},{2,1},{3,2},{4,7},{5,4},{6,5},{7,6},{8,11},{9,8},{10,9... | collective-permute-start | bytes 1572872 | tf_op jit(solution)/shard_map/ppermute | solution.py:167
  336.8 21.6 %collective-permute-start.20 = (bf16[4,16,4096]{2,0,1:T(4,128)(2,1)S(1)}, bf16[4,16,4096]{2,0,1:T(4,128)(2,1)S(1)}, u32[]{:S(2)}, u32[]{:S(2)}) collective-permute-start(bf16[4,16,4096]{2,0,1:T(4,128)(2,1)S(1)} %fusion.54), channel_id=1, source_target_pairs={{0,4},{4,0},{1,5},{5,1},{2,6},{6,2},{3,7},{7,3},{8,12},{12,8},{9,1... | collective-permute-start | bytes 1572872 | tf_op jit(solution)/shard_map/ppermute | solution.py:185
  359.4 9.4 %copy-start.18 = (f32[128,2]{0,1:T(2,128)S(1)}, f32[128,2]{0,1:T(2,128)}, u32[]{:S(2)}) copy-start(f32[128,2]{0,1:T(2,128)} %param.33) | copy-start | bytes 3076
  361.0 24.1 %all-to-all-start.2 = ((bf16[8,16,4096]{2,0,1:T(8,128)(2,1)}), bf16[8,16,4096]{2,0,1:T(8,128)(2,1)}, u32[]{:S(2)}, u32[]{:S(2)}) async-start(bf16[8,16,4096]{2,0,1:T(8,128)(2,1)} %pad_maximum_fusion.1), calls=%async_computation.2 | async-start | bytes 2097152 | tf_op jit(solution)/shard_map/all_to_all | solution.py:188
  386.9 5.6 %copy-start.1 = (bf16[128,128]{1,0:T(8,128)(2,1)S(1)}, bf16[128,128]{1,0:T(8,128)(2,1)}, u32[]{:S(2)}) copy-start(bf16[128,128]{1,0:T(8,128)(2,1)} %param.19) | copy-start | bytes 98308
  (1 other events, 0.5 us)
Sparse Core Ops, SparseCore 0:
  9.5 70.1 all-gather.1
  89.4 44.8 all-reduce.1

commit v8 on v5

--- a/solution.py
+++ b/solution.py
@@ -1,6 +1,10 @@
+import functools
+
 import jax
 import jax.numpy as jnp
 from jax import lax
+from jax.experimental import pallas as pl
+from jax.experimental.pallas import tpu as pltpu
 from jax.sharding import Mesh, PartitionSpec as P
 
 PAIR = 2
@@ -11,34 +15,100 @@
 top_precision = lax.Precision.HIGHEST
 
 
-def combine(earlier, later):
-    first_decay, first_state = earlier
-    second_decay, second_state = later
-    return (first_decay * second_decay, second_decay[:, None, None] * first_state + second_state)
-
-
-def entering(decay, state, axis):
-    place = lax.axis_index("chip") * lax.axis_size("core") + lax.axis_index("core")
-    count = lax.axis_size("chip") * lax.axis_size("core")
-    heads, rows, width = state.shape
-    inclusive = (decay, state)
-    exclusive = (jnp.ones_like(decay), jnp.zeros_like(state))
+def scan_kernel(count, decay_ref, state_ref, out_decay, out_state, inc_buf, recv_buf,
+                inc_decay, inc_state, send_sem, recv_sem):
+    chip = lax.axis_index("chip")
+    core = lax.axis_index("core")
+    member = lax.axis_index("exp")
+    place = chip * 2 + core
+    width = state_ref.shape[1]
+    hops = []
     hop = 1
     while hop < count:
-        packed = jnp.concatenate(
-            [inclusive[1].reshape(heads, rows * width), jnp.broadcast_to(inclusive[0][:, None], (heads, width))],
-            axis=1,
-        ).astype(jnp.bfloat16)
-        got = lax.ppermute(packed, axis, [(i, i + hop) for i in range(count - hop)]).astype(jnp.float32)
-        valid = place >= hop
-        arrived = (
-            jnp.where(valid, got[:, rows * width], 1.0),
-            jnp.where(valid, got[:, : rows * width], 0.0).reshape(heads, rows, width),
+        hops.append(hop)
+        hop *= 2
+
+    def target(index):
+        return (index // 2, index % 2, member)
+
+    barrier = pltpu.get_barrier_semaphore()
+    partners = 0
+    for hop in hops:
+        ahead = place + hop < count
+        behind = place >= hop
+        partners = partners + ahead.astype(jnp.int32) + behind.astype(jnp.int32)
+
+        @pl.when(ahead)
+        def _():
+            pl.semaphore_signal(barrier, inc=1, device_id=target(place + hop), device_id_type=pl.DeviceIdType.MESH)
+
+        @pl.when(behind)
+        def _():
+            pl.semaphore_signal(barrier, inc=1, device_id=target(place - hop), device_id_type=pl.DeviceIdType.MESH)
+
+    pl.semaphore_wait(barrier, partners)
+    inc_decay[...] = decay_ref[...]
+    inc_state[...] = state_ref[...]
+    out_decay[...] = jnp.ones_like(out_decay)
+    out_state[...] = jnp.zeros_like(out_state)
+    for step, hop in enumerate(hops):
+        ahead = place + hop < count
+        behind = place >= hop
+        inc_buf[step, :, :width] = inc_state[...].astype(jnp.bfloat16)
+        inc_buf[step, :, width:] = inc_decay[...].astype(jnp.bfloat16)
+        copy = pltpu.make_async_remote_copy(
+            src_ref=inc_buf.at[step],
+            dst_ref=recv_buf.at[step],
+            send_sem=send_sem.at[step],
+            recv_sem=recv_sem.at[step],
+            device_id=target(jnp.minimum(place + hop, count - 1)),
+            device_id_type=pl.DeviceIdType.MESH,
         )
-        inclusive = combine(arrived, inclusive)
-        exclusive = combine(arrived, exclusive)
-        hop *= 2
-    return exclusive
+
+        @pl.when(ahead)
+        def _():
+            copy.start()
+
+        @pl.when(behind)
+        def _():
+            copy.wait_recv()
+            got_state = recv_buf[step, :, :width].astype(jnp.float32)
+            got_decay = recv_buf[step, :, width:].astype(jnp.float32)
+            inc_state[...] = inc_decay[:, 0:1] * got_state + inc_state[...]
+            inc_decay[...] = got_decay * inc_decay[...]
+            out_state[...] = out_decay[:, 0:1] * got_state + out_state[...]
+            out_decay[...] = got_decay * out_decay[...]
+
+        @pl.when(ahead)
+        def _():
+            copy.wait_send()
+
+
+def entering(decay, state, count):
+    heads, rows, width = state.shape
+    flat = rows * width
+    lanes = 128
+    vmem = pl.BlockSpec(memory_space=pltpu.VMEM)
+    steps = max(1, (count - 1).bit_length())
+    out_decay, out_state = pl.pallas_call(
+        functools.partial(scan_kernel, count),
+        out_shape=(
+            jax.ShapeDtypeStruct((heads, lanes), jnp.float32),
+            jax.ShapeDtypeStruct((heads, flat), jnp.float32),
+        ),
+        in_specs=[vmem, vmem],
+        out_specs=(vmem, vmem),
+        scratch_shapes=[
+            pltpu.VMEM((steps, heads, flat + lanes), jnp.bfloat16),
+            pltpu.VMEM((steps, heads, flat + lanes), jnp.bfloat16),
+            pltpu.VMEM((heads, lanes), jnp.float32),
+            pltpu.VMEM((heads, flat), jnp.float32),
+            pltpu.SemaphoreType.DMA((steps,)),
+            pltpu.SemaphoreType.DMA((steps,)),
+        ],
+        compiler_params=pltpu.CompilerParams(collective_id=0, has_side_effects=True),
+    )(jnp.broadcast_to(decay[:, None], (heads, lanes)), state.reshape(heads, flat))
+    return out_decay[:, 0], out_state.reshape(heads, rows, width)
 
 
 def route_ranks(quarter_ids, experts):
@@ -106,7 +176,7 @@
     inside_part = jnp.einsum("hts,shp->thp", mixing, x_local, precision=top_precision)
     ending = jnp.exp(-(span_total[:, None] - cumulative)) * step_size
     local_state = jnp.einsum("hs,shp,sn->hpn", ending, x_local, b_local, precision=top_precision)
-    prior_decay, prior_state = entering(jnp.exp(-span_total), local_state, CTX)
+    prior_decay, prior_state = entering(jnp.exp(-span_total), local_state, n_ctx)
     incoming = prior_state + prior_decay[:, None, None] * start_state
     carried = (
         jnp.einsum("hpn,tn->thp", incoming, c_local, precision=top_precision)

time: 390 us -> 385 us (0.987)
  Pallas kernels: 0 us -> 36.9 us
  starting transfers between devices: 37.6 us -> 8.37 us
  waiting for transfers between devices: 161 us -> 153 us
  other arithmetic: 16.5 us -> 11.3 us
    pallas_call x0 -> x1, Pallas kernels: none -> 36.9 us  [entering(): pl.pallas_call(functools.partial(scan_kernel, count), out_shape=(jax.Shap...]
    ppermute x5 -> x0, starting transfers between devices: 29.2 us -> none  [entering(): lax.ppermute(packed, axis, [(i, i + hop) for i in range(count - hop)])]
    ppermute x5 -> x0, waiting for transfers between devices: 25.7 us -> none  [entering(): lax.ppermute(packed, axis, [(i, i + hop) for i in range(count - hop)])]
    all_gather x1, waiting for transfers between devices: 5.83 us -> 24.3 us  [local(): lax.all_gather(out_proj, CTX, axis=1, tiled=True)]
    unnamed x48 -> x38, local copies, waits for them, and re-layouts: 20 us -> 20.7 us
  transfers between devices with their start and end apart: 12 -> 7, of which waited for: 11 -> 6; matrix products, arithmetic and copies ran while one was open for 13% -> 12% of each run, Pallas kernels for 0% -> 10%
where the time goes in v8:
time: 385 us; the launch traced here: 379 us
  waiting for transfers between devices  153 us (40%)
  matrix products  58.9 us (15%)
  blocking collectives  56.4 us (15%)
  local copies, waits for them, and re-layouts  40.4 us (10%)
  Pallas kernels  36.9 us (10%)
  between operations  13.7 us (4%)
  other arithmetic  11.3 us (3%)
  starting transfers between devices  8.37 us (2%)
    unnamed x6, waiting for transfers between devices  60.2 us
    all_to_all x1, blocking collectives, local(): lax.all_to_all(placed, 'chip', split_axis=1, concat_axis=1, tiled=True)  56.4 us
    psum x1, waiting for transfers between devices, local(): lax.psum(jnp.concatenate([partial_value, jnp.broadcast_to(squares[:, None...  44.6 us
    pallas_call x1, Pallas kernels, entering(): pl.pallas_call(functools.partial(scan_kernel, count), out_shape=(jax.Shap...  36.9 us
    dot_general x2, matrix products, expert_rows(): product = jnp.dot(activated, down_rows, preferred_element_type=jnp.float32)  33.1 us
    all_gather x1, waiting for transfers between devices, local(): lax.all_gather(out_proj, CTX, axis=1, tiled=True)  24.3 us
    unnamed x38, local copies, waits for them, and re-layouts  20.7 us
    all_to_all x1, waiting for transfers between devices, local(): lax.all_to_all(both_halves, 'chip', split_axis=1, concat_axis=1, tiled=True)  16.9 us
  transfers between devices with their start and end apart: 7, of which 6 were waited for; matrix products, arithmetic and copies ran while one was open for 12% of the time, Pallas kernels for 10%

profile of v8, /device:TPU:0, one launch (start us, length us, event | category | flops | bytes accessed | tf_op | source)
XLA Modules:
  0.0 379.2 jit_solution(13486771151823172702)
XLA Ops:
  6.5 0.7 all-gather.2.cloned.1.call-update
  7.3 1.2 copy.51
  8.5 1.0 reduce_window_sum.33
  9.7 0.8 exponential_bitcast_fusion
  10.4 0.4 fusion.38
  10.8 1.2 copy.72
  12.0 0.7 broadcast_in_dim.29.decay_ref
  12.7 36.9 %shard_map.163 = (f32[16,128]{1,0:T(8,128)}, f32[16,8192]{1,0:T(8,128)}) custom-call(f32[16,128]{1,0:T(8,128)} %broadcast_in_dim.29.decay_ref, f32[16,8192]{1,0:T(8,128)} %bitcast.96), custom_call_target="tpu_custom_call" | custom-call | tf_op jit(solution)/shard_map/pallas_call | solution.py:93
  49.6 1.1 copy.68
  50.7 0.8 slice_reduce_fusion
  51.9 0.4 fusion.23
  52.3 1.4 fusion.22
  53.9 0.2 multiply_reduce_fusion.2
  54.2 24.3 %all-gather.2.cloned.1.call-done = bf16[1024,4096]{1,0:T(8,128)(2,1)} async-done(((bf16[1024,128]{1,0:T(8,128)(2,1)}), bf16[1024,4096]{1,0:T(8,128)(2,1)}) %all-gather.2.cloned.1.call-update) | async-done | bytes 8388624 | tf_op jit(solution)/shard_map/all_gather | solution.py:193
  78.5 4.7 %convolution_convert_fusion.1 = bf16[128,4096]{1,0:T(8,128)(2,1)S(1)} fusion(bf16[1024,4096]{1,0:T(8,128)(2,1)} %all-gather.2.cloned.1.call-done, f32[1024]{0:T(1024)S(1)} %copy-done.12, f32[128,1024]{1,0:T(8,128)S(1)} %copy.52, bf16[128,1024]{1,0:T(8,128)(2,1)S(1)} %copy-done.5), kind=kOutput, calls=%fused_computation.16 | convolution fusion | flops 1075314688 | bytes 10227712 | tf_op jit(solution)/shard_map/dot_general | solution.py:191
  83.3 1.1 pad_maximum_fusion
  84.4 0.3 reduce-scatter.9.cloned.1.call-start
  85.2 0.2 select_reduce_fusion
  85.5 44.6 %all-reduce.2.cloned.1.call-done = bf16[128,4224]{1,0:T(8,128)(2,1)} async-done(((bf16[128,4224]{1,0:T(8,128)(2,1)}), bf16[128,4224]{1,0:T(8,128)(2,1)}) %all-reduce.2.cloned.1.call-update) | async-done | bytes 1081360 | tf_op jit(solution)/shard_map/psum | solution.py:197
  130.1 1.4 convert_element_type.63
  131.6 0.6 multiply_reduce_fusion
  132.3 0.3 multiply_convert_fusion
  132.6 3.4 broadcast_in_dim.31
  136.1 4.1 %reshape.129 = bf16[4,64,4096]{2,1,0:T(8,128)(2,1)} reshape(bf16[4,32,2,4096]{3,2,1,0:T(2,128)(2,1)} %broadcast_in_dim.31) | data formatting | bytes 4194304 | tf_op jit(solution)/shard_map/vmap()/reshape | solution.py:128
  140.2 2.9 convolution_convert_fusion
  143.1 2.3 copy.54
  145.5 56.4 %all_to_all.10 = bf16[32,16,4096]{2,0,1:T(8,128)(2,1)S(1)} all-to-all(bf16[32,16,4096]{2,0,1:T(8,128)(2,1)S(1)} %copy.54), channel_id=1, replica_groups=mesh['chip'=16,'core'=2,'exp'=4] {'chip'}, dimensions={1} | all-to-all | bytes 8388608 | tf_op jit(solution)/shard_map/all_to_all | solution.py:224
  201.9 2.3 copy.55
  204.2 1.9 copy-done.2
  206.1 0.5 collective-permute-start
  206.6 7.1 %collective-permute-done = bf16[32,16,4096]{2,1,0:T(8,128)(2,1)S(1)} collective-permute-done((bf16[32,16,4096]{2,1,0:T(8,128)(2,1)S(1)}, bf16[32,16,4096]{2,1,0:T(8,128)(2,1)S(1)}, u32[]{:S(2)}, u32[]{:S(2)}) %collective-permute-start) | collective-permute-done | bytes 4194336 | tf_op jit(solution)/shard_map/ppermute | solution.py:225
  213.8 2.0 copy-done.11
  215.8 5.8 %fusion.4 = f32[512,896]{1,0:T(8,128)} fusion(bf16[512,4096]{1,0:T(8,128)(2,1)S(1)} %bitcast.105, bf16[1,4096,896]{2,1,0:T(8,128)(2,1)S(1)} %bitcast.104), kind=kOutput, calls=%fused_computation.5 | convolution fusion | flops 3758096384 | bytes 13369344 | tf_op jit(solution)/shard_map/dot_general | solution.py:231
  221.6 16.5 %fusion.15 = bf16[512,4096]{1,0:T(8,128)(2,1)} fusion(bf16[1,896,4096]{2,1,0:T(8,128)(2,1)} %param.31, f32[512,896]{1,0:T(8,128)} %fusion.4, bf16[512,4096]{1,0:T(8,128)(2,1)} %bitcast.106, bf16[1,4096,896]{2,1,0:T(8,128)(2,1)} %param.29), kind=kOutput, calls=%fused_computation.15 | convolution fusion | flops 7521042432 | bytes 24903680 | tf_op jit(solution)/shard_map/dot_general | solution.py:233
  238.0 6.5 %copy.70 = bf16[4,8,16,4096]{3,1,2,0:T(8,128)(2,1)} copy(bf16[4,8,16,4096]{3,2,1,0:T(8,128)(2,1)} %bitcast.94) | data formatting | bytes 8388608
  244.8 10.1 %fusion.10 = f32[512,896]{1,0:T(8,128)} fusion(bf16[512,4096]{1,0:T(8,128)(2,1)} %bitcast.92, bf16[1,4096,896]{2,1,0:T(8,128)(2,1)} %param.29), kind=kOutput, calls=%fused_computation.11 | convolution fusion | flops 3758096384 | bytes 13369344 | tf_op jit(solution)/shard_map/dot_general | solution.py:230
  254.9 16.6 %fusion.12 = bf16[512,4096]{1,0:T(8,128)(2,1)} fusion(bf16[1,896,4096]{2,1,0:T(8,128)(2,1)} %param.31, f32[512,896]{1,0:T(8,128)} %fusion.10, bf16[512,4096]{1,0:T(8,128)(2,1)} %bitcast.93, bf16[1,4096,896]{2,1,0:T(8,128)(2,1)} %param.30), kind=kOutput, calls=%fused_computation.14 | convolution fusion | flops 7521042432 | bytes 24903680 | tf_op jit(solution)/shard_map/dot_general | solution.py:233
  271.5 6.5 %copy.69 = bf16[4,8,16,4096]{3,1,2,0:T(8,128)(2,1)} copy(bf16[4,8,16,4096]{3,2,1,0:T(8,128)(2,1)} %bitcast.95) | data formatting | bytes 8388608
  278.1 10.5 %reduce-scatter.9.cloned.1.call-done = bf16[8,65536]{1,0:T(8,128)(2,1)} async-done(((bf16[32,65536]{1,0:T(8,128)(2,1)}), bf16[8,65536]{1,0:T(8,128)(2,1)}) %reduce-scatter.9.cloned.1.call-update) | async-done | bytes 1048592
  288.6 48.9 %reduce-scatter.7.cloned.1.call-done = bf16[8,65536]{1,0:T(8,128)(2,1)} async-done(((bf16[32,65536]{1,0:T(8,128)(2,1)}), bf16[8,65536]{1,0:T(8,128)(2,1)}) %reduce-scatter.7.cloned.1.call-update) | async-done | bytes 1048592
  337.5 2.5 add_convert_fusion
  340.0 7.3 %all-to-all-start.1 = ((bf16[8,16,4096]{2,0,1:T(8,128)(2,1)}), bf16[8,16,4096]{2,0,1:T(8,128)(2,1)}, u32[]{:S(2)}, u32[]{:S(2)}) async-start(bf16[8,16,4096]{2,0,1:T(8,128)(2,1)} %add_convert_fusion), calls=%async_computation.1 | async-start | bytes 2097152 | tf_op jit(solution)/shard_map/all_to_all | solution.py:242
  348.2 16.9 %all-to-all-done.1 = bf16[8,16,4096]{2,0,1:T(8,128)(2,1)} async-done(((bf16[8,16,4096]{2,0,1:T(8,128)(2,1)}), bf16[8,16,4096]{2,0,1:T(8,128)(2,1)}, u32[]{:S(2)}, u32[]{:S(2)}) %all-to-all-start.1) | async-done | bytes 1048608 | tf_op jit(solution)/shard_map/all_to_all | solution.py:242
  365.1 1.8 copy.59
  366.9 1.7 gather_fusion
  368.5 1.7 reshape.137
  370.2 1.4 multiply_reduce_fusion.1
  371.7 0.8 add_convert_fusion.1
  (63 shorter events, 2.7 us)
Async XLA Ops:
  6.5 3.9 %copy-start = (bf16[128,128]{1,0:T(8,128)(2,1)S(1)}, bf16[128,128]{1,0:T(8,128)(2,1)}, u32[]{:S(2)}) copy-start(bf16[128,128]{1,0:T(8,128)(2,1)} %param.19) | copy-start | bytes 98308
  6.5 45.0 %copy-start.6 = (bf16[128,128]{1,0:T(8,128)(2,1)S(1)}, bf16[128,128]{1,0:T(8,128)(2,1)}, u32[]{:S(2)}) copy-start(bf16[128,128]{1,0:T(8,128)(2,1)} %param.20) | copy-start | bytes 98308
  6.5 71.9 %all-gather.2.cloned.1.call-start = ((), (), s32[]{:S(2)}) async-start(), calls=%async_computation.4 | async-start | bytes 8650752 | tf_op jit(solution)/shard_map/all_gather | solution.py:193
  7.3 44.5 %copy-start.4 = (f32[16,64,128]{2,1,0:T(8,128)S(1)}, f32[16,64,128]{2,1,0:T(8,128)}, u32[]{:S(2)}) copy-start(f32[16,64,128]{2,1,0:T(8,128)} %param.24) | copy-start | bytes 1572868
  7.3 122.8 %all-reduce.2.cloned.1.call-start = ((), (), s32[]{:S(2)}) async-start(), calls=%async_computation.5 | async-start | bytes 2162688 | tf_op jit(solution)/shard_map/psum | solution.py:197
  12.7 39.6 %copy-start.8 = (f32[16,128]{1,0:T(8,128)S(1)}, f32[16,128]{1,0:T(8,128)}, u32[]{:S(2)}) copy-start(f32[16,128]{1,0:T(8,128)} %param.21) | copy-start | bytes 24580
  12.7 39.6 %copy-start.13 = (f32[16]{0:T(128)S(1)}, f32[16]{0:T(128)}, u32[]{:S(2)}) copy-start(f32[16]{0:T(128)} %param.23) | copy-start | bytes 196
  52.3 1.6 copy-start.5
  52.3 26.2 %copy-start.12 = (f32[1024]{0:T(1024)S(1)}, f32[1024]{0:T(1024)}, u32[]{:S(2)}) copy-start(f32[1024]{0:T(1024)} %param.25) | copy-start | bytes 12292
  83.2 1.6 copy-start.9
  84.4 47.2 %copy-start.3 = (bf16[128,4096]{1,0:T(8,128)(2,1)S(1)}, bf16[128,4096]{1,0:T(8,128)(2,1)}, u32[]{:S(2)}) copy-start(bf16[128,4096]{1,0:T(8,128)(2,1)} %param.27) | copy-start | bytes 3145732
  84.4 204.2 %reduce-scatter.9.cloned.1.call-start = ((), (), s32[]{:S(2)}) async-start(), calls=%async_computation.7 | async-start | bytes 5242880
  131.6 0.7 copy-start.7
  145.4 70.3 %slice-start = ((s8[7340032]{0:T(1024)(128)(4,1)}), s8[4194304]{0:T(1024)(128)(4,1)S(1)}, s32[]{:S(2)}) async-start(s8[7340032]{0:T(1024)(128)(4,1)} %bitcast.103), calls=%async_computation.8 | async-start | bytes 8388608
  201.9 13.9 %slice-start.1 = ((s8[7340032]{0:T(1024)(128)(4,1)}), s8[3145728]{0:T(1024)(128)(4,1)S(1)}, s32[]{:S(2)}) async-start(s8[7340032]{0:T(1024)(128)(4,1)} %bitcast.103), calls=%async_computation.9 | async-start | bytes 6291456
  204.2 1.9 copy-start.2
  206.1 7.7 %collective-permute-start = (bf16[32,16,4096]{2,1,0:T(8,128)(2,1)S(1)}, bf16[32,16,4096]{2,1,0:T(8,128)(2,1)S(1)}, u32[]{:S(2)}, u32[]{:S(2)}) collective-permute-start(bf16[32,16,4096]{2,1,0:T(8,128)(2,1)S(1)} %copy.55), channel_id=1, source_target_pairs={{0,4},{4,0},{1,5},{5,1},{2,6},{6,2},{3,7},{7,3},{8,12},{12,8},{9,1... | collective-permute-start | bytes 12582920 | tf_op jit(solution)/shard_map/ppermute | solution.py:225
  213.8 2.0 copy-start.11
  244.6 92.9 %reduce-scatter.7.cloned.1.call-start = ((), (), s32[]{:S(2)}) async-start(), calls=%async_computation.6 | async-start | bytes 5242880
  288.6 48.9 %collective-permute-start.1 = (bf16[8,16,4096]{2,0,1:T(8,128)(2,1)}, bf16[8,16,4096]{2,0,1:T(8,128)(2,1)S(1)}, u32[]{:S(2)}, u32[]{:S(2)}) collective-permute-start(bf16[8,16,4096]{2,0,1:T(8,128)(2,1)} %bitcast.107), channel_id=1, source_target_pairs={{0,4},{4,0},{1,5},{5,1},{2,6},{6,2},{3,7},{7,3},{8,12},{12,8},{9,1... | collective-permute-start | bytes 3145736 | tf_op jit(solution)/shard_map/ppermute | solution.py:240
  337.5 10.3 %copy-start.10 = (f32[128,2]{0,1:T(2,128)S(1)}, f32[128,2]{0,1:T(2,128)}, u32[]{:S(2)}) copy-start(f32[128,2]{0,1:T(2,128)} %param.33) | copy-start | bytes 3076
  340.0 25.1 %all-to-all-start.1 = ((bf16[8,16,4096]{2,0,1:T(8,128)(2,1)}), bf16[8,16,4096]{2,0,1:T(8,128)(2,1)}, u32[]{:S(2)}, u32[]{:S(2)}) async-start(bf16[8,16,4096]{2,0,1:T(8,128)(2,1)} %add_convert_fusion), calls=%async_computation.1 | async-start | bytes 2097152 | tf_op jit(solution)/shard_map/all_to_all | solution.py:242
  366.9 5.6 %copy-start.1 = (bf16[128,128]{1,0:T(8,128)(2,1)S(1)}, bf16[128,128]{1,0:T(8,128)(2,1)}, u32[]{:S(2)}) copy-start(bf16[128,128]{1,0:T(8,128)(2,1)} %param.19) | copy-start | bytes 98308
Sparse Core Ops, SparseCore 0:
  9.5 68.8 all-gather.1
  84.5 45.5 all-reduce.1
  244.7 43.8 reduce-scatter.8
  291.0 46.4 reduce-scatter.6

commit v9 on v8

--- a/solution.py
+++ b/solution.py
@@ -194,12 +194,16 @@
         preferred_element_type=jnp.float32,
     )
     width_out = partial_value.shape[1]
-    summed_parts = lax.psum(
-        jnp.concatenate(
-            [partial_value, jnp.broadcast_to(squares[:, None], (tok_ctx, 128))], axis=1
-        ).astype(jnp.bfloat16),
-        "exp",
-    ).astype(jnp.float32)
+    joined = jnp.concatenate(
+        [partial_value, jnp.broadcast_to(squares[:, None], (tok_ctx, 128))], axis=1
+    ).astype(jnp.bfloat16)
+    quarters = lax.all_to_all(
+        joined.reshape(n_exp, tok_quarter, joined.shape[1]), "exp", split_axis=0, concat_axis=0, tiled=True
+    )
+    quarter_sum = jnp.sum(quarters.astype(jnp.float32), axis=0).astype(jnp.bfloat16)
+    summed_parts = lax.all_to_all(
+        jnp.broadcast_to(quarter_sum[None], (n_exp,) + quarter_sum.shape), "exp", split_axis=0, concat_axis=0, tiled=True
+    ).reshape(tok_ctx, joined.shape[1]).astype(jnp.float32)
     scaling = lax.rsqrt(summed_parts[:, width_out] / (head_count * head_dim * n_exp) + eps_norm)
     mixed_all = summed_parts[:, :width_out] * scaling[:, None]
     gate_rows = w_gate[0]

time: 385 us -> 374 us (0.971)
  waiting for transfers between devices: 153 us -> 121 us
  blocking collectives: 56.4 us -> 74.6 us
    psum x1 -> x0, waiting for transfers between devices: 44.6 us -> none  [local(): lax.psum(jnp.concatenate([partial_value, jnp.broadcast_to(squares[:, None...]
    all_to_all x0 -> x1, blocking collectives: none -> 19.9 us  [local(): lax.all_to_all(joined.reshape(n_exp, tok_quarter, joined.shape[1]), 'exp'...]
    all_to_all x0 -> x1, waiting for transfers between devices: none -> 13.9 us  [local(): lax.all_to_all(jnp.broadcast_to(quarter_sum[None], (n_exp,) + quarter_sum...]
    unnamed x6 -> x5, waiting for transfers between devices: 60.2 us -> 59.2 us
where the time goes in v9:
time: 374 us; the launch traced here: 368 us
  waiting for transfers between devices  121 us (32%)
  blocking collectives  74.6 us (20%)
  matrix products  59 us (16%)
  local copies, waits for them, and re-layouts  41.5 us (11%)
  Pallas kernels  36.9 us (10%)
  between operations  13.7 us (4%)
  starting transfers between devices  11.8 us (3%)
  other arithmetic  9.39 us (3%)
    unnamed x5, waiting for transfers between devices  59.2 us
    all_to_all x1, blocking collectives, local(): lax.all_to_all(placed, 'chip', split_axis=1, concat_axis=1, tiled=True)  54.7 us
    pallas_call x1, Pallas kernels, entering(): pl.pallas_call(functools.partial(scan_kernel, count), out_shape=(jax.Shap...  36.9 us
    dot_general x2, matrix products, expert_rows(): product = jnp.dot(activated, down_rows, preferred_element_type=jnp.float32)  33.1 us
    all_gather x1, waiting for transfers between devices, local(): lax.all_gather(out_proj, CTX, axis=1, tiled=True)  24.2 us
    unnamed x38, local copies, waits for them, and re-layouts  20.6 us
    all_to_all x1, blocking collectives, local(): lax.all_to_all(joined.reshape(n_exp, tok_quarter, joined.shape[1]), 'exp'...  19.9 us
    all_to_all x1, waiting for transfers between devices, local(): lax.all_to_all(both_halves, 'chip', split_axis=1, concat_axis=1, tiled=True)  16.9 us
  transfers between devices with their start and end apart: 7, of which 6 were waited for; matrix products, arithmetic and copies ran while one was open for 12% of the time, Pallas kernels for 10%

profile of v9, /device:TPU:0, one launch (start us, length us, event | category | flops | bytes accessed | tf_op | source)
XLA Modules:
  0.0 368.2 jit_solution(14521864661098199224)
XLA Ops:
  6.5 0.7 all-gather.2.cloned.1.call-update
  7.3 1.2 copy.51
  8.5 1.0 reduce_window_sum.33
  9.6 0.8 exponential_bitcast_fusion
  10.4 0.4 fusion.38
  10.8 1.2 copy.72
  12.0 0.7 broadcast_in_dim.33.decay_ref
  12.6 36.9 %shard_map.163 = (f32[16,128]{1,0:T(8,128)}, f32[16,8192]{1,0:T(8,128)}) custom-call(f32[16,128]{1,0:T(8,128)} %broadcast_in_dim.33.decay_ref, f32[16,8192]{1,0:T(8,128)} %bitcast.100), custom_call_target="tpu_custom_call" | custom-call | tf_op jit(solution)/shard_map/pallas_call | solution.py:93
  49.5 1.1 copy.68
  50.7 0.8 slice_reduce_fusion
  51.8 0.4 fusion.23
  52.2 1.4 fusion.22
  53.9 0.2 multiply_reduce_fusion.2
  54.2 24.2 %all-gather.2.cloned.1.call-done = bf16[1024,4096]{1,0:T(8,128)(2,1)} async-done(((bf16[1024,128]{1,0:T(8,128)(2,1)}), bf16[1024,4096]{1,0:T(8,128)(2,1)}) %all-gather.2.cloned.1.call-update) | async-done | bytes 8388624 | tf_op jit(solution)/shard_map/all_gather | solution.py:193
  78.4 4.7 %convolution_convert_fusion.1 = bf16[128,4096]{1,0:T(8,128)(2,1)S(1)} fusion(bf16[1024,4096]{1,0:T(8,128)(2,1)} %all-gather.2.cloned.1.call-done, f32[1024]{0:T(1024)S(1)} %copy-done.12, f32[128,1024]{1,0:T(8,128)S(1)} %copy.52, bf16[128,1024]{1,0:T(8,128)(2,1)S(1)} %copy-done.5), kind=kOutput, calls=%fused_computation.16 | convolution fusion | flops 1075314688 | bytes 10227712 | tf_op jit(solution)/shard_map/dot_general | solution.py:191
  83.2 19.9 %all_to_all.20 = bf16[4,32,4224]{2,1,0:T(8,128)(2,1)S(1)} all-to-all(bf16[4,32,4224]{2,1,0:T(8,128)(2,1)S(1)} %pad_maximum_fusion), channel_id=1, replica_groups=mesh['chip'=16,'core'=2,'exp'=4] {'exp'}, dimensions={0} | all-to-all | bytes 2162688 | tf_op jit(solution)/shard_map/all_to_all | solution.py:200
  103.4 1.1 broadcast_in_dim.36
  104.5 3.5 all-to-all-start.1
  108.0 0.3 reduce-scatter.9.cloned.1.call-start
  109.1 13.9 %all-to-all-done.1 = bf16[4,32,4224]{2,1,0:T(8,128)(2,1)S(1)} async-done(((bf16[4,32,4224]{2,1,0:T(8,128)(2,1)}), bf16[4,32,4224]{2,1,0:T(8,128)(2,1)S(1)}, u32[]{:S(2)}, u32[]{:S(2)}) %all-to-all-start.1) | async-done | bytes 1081376 | tf_op jit(solution)/shard_map/all_to_all | solution.py:204
  123.3 0.6 multiply_reduce_fusion
  124.0 0.3 multiply_convert_fusion
  124.3 3.4 broadcast_in_dim.37
  127.8 4.1 %reshape.142 = bf16[4,64,4096]{2,1,0:T(8,128)(2,1)} reshape(bf16[4,32,2,4096]{3,2,1,0:T(2,128)(2,1)} %broadcast_in_dim.37) | data formatting | bytes 4194304 | tf_op jit(solution)/shard_map/vmap()/reshape | solution.py:128
  131.9 2.9 convolution_convert_fusion
  134.8 2.3 copy.54
  137.2 54.7 %all_to_all.21 = bf16[32,16,4096]{2,0,1:T(8,128)(2,1)S(1)} all-to-all(bf16[32,16,4096]{2,0,1:T(8,128)(2,1)S(1)} %copy.54), channel_id=1, replica_groups=mesh['chip'=16,'core'=2,'exp'=4] {'chip'}, dimensions={1} | all-to-all | bytes 8388608 | tf_op jit(solution)/shard_map/all_to_all | solution.py:228
  191.8 2.3 copy.55
  194.1 1.9 copy-done.2
  196.0 0.5 collective-permute-start
  196.6 7.1 %collective-permute-done = bf16[32,16,4096]{2,1,0:T(8,128)(2,1)S(1)} collective-permute-done((bf16[32,16,4096]{2,1,0:T(8,128)(2,1)S(1)}, bf16[32,16,4096]{2,1,0:T(8,128)(2,1)S(1)}, u32[]{:S(2)}, u32[]{:S(2)}) %collective-permute-start) | collective-permute-done | bytes 4194336 | tf_op jit(solution)/shard_map/ppermute | solution.py:229
  203.7 2.0 copy-done.11
  205.7 5.8 %fusion.4 = f32[512,896]{1,0:T(8,128)} fusion(bf16[512,4096]{1,0:T(8,128)(2,1)S(1)} %bitcast.110, bf16[1,4096,896]{2,1,0:T(8,128)(2,1)S(1)} %bitcast.109), kind=kOutput, calls=%fused_computation.5 | convolution fusion | flops 3758096384 | bytes 13369344 | tf_op jit(solution)/shard_map/dot_general | solution.py:235
  211.5 16.5 %fusion.15 = bf16[512,4096]{1,0:T(8,128)(2,1)} fusion(bf16[1,896,4096]{2,1,0:T(8,128)(2,1)} %param.31, f32[512,896]{1,0:T(8,128)} %fusion.4, bf16[512,4096]{1,0:T(8,128)(2,1)} %bitcast.111, bf16[1,4096,896]{2,1,0:T(8,128)(2,1)} %param.29), kind=kOutput, calls=%fused_computation.15 | convolution fusion | flops 7521042432 | bytes 24903680 | tf_op jit(solution)/shard_map/dot_general | solution.py:237
  227.9 6.5 %copy.70 = bf16[4,8,16,4096]{3,1,2,0:T(8,128)(2,1)} copy(bf16[4,8,16,4096]{3,2,1,0:T(8,128)(2,1)} %bitcast.98) | data formatting | bytes 8388608
  234.7 10.1 %fusion.10 = f32[512,896]{1,0:T(8,128)} fusion(bf16[512,4096]{1,0:T(8,128)(2,1)} %bitcast.96, bf16[1,4096,896]{2,1,0:T(8,128)(2,1)} %param.29), kind=kOutput, calls=%fused_computation.11 | convolution fusion | flops 3758096384 | bytes 13369344 | tf_op jit(solution)/shard_map/dot_general | solution.py:234
  244.8 16.7 %fusion.12 = bf16[512,4096]{1,0:T(8,128)(2,1)} fusion(bf16[1,896,4096]{2,1,0:T(8,128)(2,1)} %param.31, f32[512,896]{1,0:T(8,128)} %fusion.10, bf16[512,4096]{1,0:T(8,128)(2,1)} %bitcast.97, bf16[1,4096,896]{2,1,0:T(8,128)(2,1)} %param.30), kind=kOutput, calls=%fused_computation.14 | convolution fusion | flops 7521042432 | bytes 24903680 | tf_op jit(solution)/shard_map/dot_general | solution.py:237
  261.5 6.5 %copy.69 = bf16[4,8,16,4096]{3,1,2,0:T(8,128)(2,1)} copy(bf16[4,8,16,4096]{3,2,1,0:T(8,128)(2,1)} %bitcast.99) | data formatting | bytes 8388608
  268.0 9.4 %reduce-scatter.9.cloned.1.call-done = bf16[8,65536]{1,0:T(8,128)(2,1)} async-done(((bf16[32,65536]{1,0:T(8,128)(2,1)}), bf16[8,65536]{1,0:T(8,128)(2,1)}) %reduce-scatter.9.cloned.1.call-update) | async-done | bytes 1048592
  277.4 49.1 %reduce-scatter.7.cloned.1.call-done = bf16[8,65536]{1,0:T(8,128)(2,1)} async-done(((bf16[32,65536]{1,0:T(8,128)(2,1)}), bf16[8,65536]{1,0:T(8,128)(2,1)}) %reduce-scatter.7.cloned.1.call-update) | async-done | bytes 1048592
  326.5 2.5 add_convert_fusion
  329.0 7.2 %all-to-all-start.3 = ((bf16[8,16,4096]{2,0,1:T(8,128)(2,1)}), bf16[8,16,4096]{2,0,1:T(8,128)(2,1)}, u32[]{:S(2)}, u32[]{:S(2)}) async-start(bf16[8,16,4096]{2,0,1:T(8,128)(2,1)} %add_convert_fusion), calls=%async_computation.3 | async-start | bytes 2097152 | tf_op jit(solution)/shard_map/all_to_all | solution.py:246
  337.1 16.9 %all-to-all-done.3 = bf16[8,16,4096]{2,0,1:T(8,128)(2,1)} async-done(((bf16[8,16,4096]{2,0,1:T(8,128)(2,1)}), bf16[8,16,4096]{2,0,1:T(8,128)(2,1)}, u32[]{:S(2)}, u32[]{:S(2)}) %all-to-all-start.3) | async-done | bytes 1048608 | tf_op jit(solution)/shard_map/all_to_all | solution.py:246
  354.0 1.8 copy.59
  355.8 1.7 gather_fusion
  357.5 1.7 reshape.152
  359.2 1.4 multiply_reduce_fusion.1
  360.6 0.8 add_convert_fusion.1
  (66 shorter events, 3.5 us)
Async XLA Ops:
  6.5 3.9 %copy-start = (bf16[128,128]{1,0:T(8,128)(2,1)S(1)}, bf16[128,128]{1,0:T(8,128)(2,1)}, u32[]{:S(2)}) copy-start(bf16[128,128]{1,0:T(8,128)(2,1)} %param.19) | copy-start | bytes 98308
  6.5 45.0 %copy-start.6 = (bf16[128,128]{1,0:T(8,128)(2,1)S(1)}, bf16[128,128]{1,0:T(8,128)(2,1)}, u32[]{:S(2)}) copy-start(bf16[128,128]{1,0:T(8,128)(2,1)} %param.20) | copy-start | bytes 98308
  6.5 71.8 %all-gather.2.cloned.1.call-start = ((), (), s32[]{:S(2)}) async-start(), calls=%async_computation.6 | async-start | bytes 8650752 | tf_op jit(solution)/shard_map/all_gather | solution.py:193
  7.3 44.4 %copy-start.4 = (f32[16,64,128]{2,1,0:T(8,128)S(1)}, f32[16,64,128]{2,1,0:T(8,128)}, u32[]{:S(2)}) copy-start(f32[16,64,128]{2,1,0:T(8,128)} %param.24) | copy-start | bytes 1572868
  12.6 39.6 %copy-start.8 = (f32[16,128]{1,0:T(8,128)S(1)}, f32[16,128]{1,0:T(8,128)}, u32[]{:S(2)}) copy-start(f32[16,128]{1,0:T(8,128)} %param.21) | copy-start | bytes 24580
  12.6 39.6 %copy-start.13 = (f32[16]{0:T(128)S(1)}, f32[16]{0:T(128)}, u32[]{:S(2)}) copy-start(f32[16]{0:T(128)} %param.23) | copy-start | bytes 196
  52.2 1.6 copy-start.5
  52.2 26.1 %copy-start.12 = (f32[1024]{0:T(1024)S(1)}, f32[1024]{0:T(1024)}, u32[]{:S(2)}) copy-start(f32[1024]{0:T(1024)} %param.25) | copy-start | bytes 12292
  103.2 5.2 %copy-start.9 = (s32[128,2]{0,1:T(2,128)S(1)}, s32[128,2]{0,1:T(2,128)}, u32[]{:S(2)}) copy-start(s32[128,2]{0,1:T(2,128)} %param.32) | copy-start | bytes 3076
  104.5 18.5 %all-to-all-start.1 = ((bf16[4,32,4224]{2,1,0:T(8,128)(2,1)}), bf16[4,32,4224]{2,1,0:T(8,128)(2,1)S(1)}, u32[]{:S(2)}, u32[]{:S(2)}) async-start(bf16[4,32,4224]{2,1,0:T(8,128)(2,1)} %broadcast_in_dim.36), calls=%async_computation.1 | async-start | bytes 2162688 | tf_op jit(solution)/shard_map/all_to_all | solution.py:204
  108.0 15.3 %copy-start.3 = (bf16[128,4096]{1,0:T(8,128)(2,1)S(1)}, bf16[128,4096]{1,0:T(8,128)(2,1)}, u32[]{:S(2)}) copy-start(bf16[128,4096]{1,0:T(8,128)(2,1)} %param.27) | copy-start | bytes 3145732
  108.0 169.4 %reduce-scatter.9.cloned.1.call-start = ((), (), s32[]{:S(2)}) async-start(), calls=%async_computation.8 | async-start | bytes 5242880
  123.3 0.7 copy-start.7
  137.1 68.5 %slice-start = ((s8[7340032]{0:T(1024)(128)(4,1)}), s8[4194304]{0:T(1024)(128)(4,1)S(1)}, s32[]{:S(2)}) async-start(s8[7340032]{0:T(1024)(128)(4,1)} %bitcast.108), calls=%async_computation.9 | async-start | bytes 8388608
  191.8 13.9 %slice-start.1 = ((s8[7340032]{0:T(1024)(128)(4,1)}), s8[3145728]{0:T(1024)(128)(4,1)S(1)}, s32[]{:S(2)}) async-start(s8[7340032]{0:T(1024)(128)(4,1)} %bitcast.108), calls=%async_computation.10 | async-start | bytes 6291456
  194.1 1.9 copy-start.2
  196.0 7.7 %collective-permute-start = (bf16[32,16,4096]{2,1,0:T(8,128)(2,1)S(1)}, bf16[32,16,4096]{2,1,0:T(8,128)(2,1)S(1)}, u32[]{:S(2)}, u32[]{:S(2)}) collective-permute-start(bf16[32,16,4096]{2,1,0:T(8,128)(2,1)S(1)} %copy.55), channel_id=1, source_target_pairs={{0,4},{4,0},{1,5},{5,1},{2,6},{6,2},{3,7},{7,3},{8,12},{12,8},{9,1... | collective-permute-start | bytes 12582920 | tf_op jit(solution)/shard_map/ppermute | solution.py:229
  203.7 2.0 copy-start.11
  234.5 92.0 %reduce-scatter.7.cloned.1.call-start = ((), (), s32[]{:S(2)}) async-start(), calls=%async_computation.7 | async-start | bytes 5242880
  277.4 49.1 %collective-permute-start.1 = (bf16[8,16,4096]{2,0,1:T(8,128)(2,1)}, bf16[8,16,4096]{2,0,1:T(8,128)(2,1)S(1)}, u32[]{:S(2)}, u32[]{:S(2)}) collective-permute-start(bf16[8,16,4096]{2,0,1:T(8,128)(2,1)} %bitcast.112), channel_id=1, source_target_pairs={{0,4},{4,0},{1,5},{5,1},{2,6},{6,2},{3,7},{7,3},{8,12},{12,8},{9,1... | collective-permute-start | bytes 3145736 | tf_op jit(solution)/shard_map/ppermute | solution.py:244
  326.5 10.3 %copy-start.10 = (f32[128,2]{0,1:T(2,128)S(1)}, f32[128,2]{0,1:T(2,128)}, u32[]{:S(2)}) copy-start(f32[128,2]{0,1:T(2,128)} %param.33) | copy-start | bytes 3076
  329.0 25.1 %all-to-all-start.3 = ((bf16[8,16,4096]{2,0,1:T(8,128)(2,1)}), bf16[8,16,4096]{2,0,1:T(8,128)(2,1)}, u32[]{:S(2)}, u32[]{:S(2)}) async-start(bf16[8,16,4096]{2,0,1:T(8,128)(2,1)} %add_convert_fusion), calls=%async_computation.3 | async-start | bytes 2097152 | tf_op jit(solution)/shard_map/all_to_all | solution.py:246
  355.8 5.6 %copy-start.1 = (bf16[128,128]{1,0:T(8,128)(2,1)S(1)}, bf16[128,128]{1,0:T(8,128)(2,1)}, u32[]{:S(2)}) copy-start(bf16[128,128]{1,0:T(8,128)(2,1)} %param.19) | copy-start | bytes 98308
Sparse Core Ops, SparseCore 0:
  9.5 68.7 all-gather.1
  234.6 42.7 reduce-scatter.8
  279.9 46.5 reduce-scatter.6

commit v10 on v9

--- a/solution.py
+++ b/solution.py
@@ -229,18 +229,27 @@
     other = lax.ppermute(mine, "core", swap)
     hidden_own = lax.dynamic_slice_in_dim(hidden_all, first_row, tok_quarter, 0)
 
-    def expert_rows(rows):
+    def expert_rows(rows, by_permutes):
         flat = rows.reshape(-1, model_width)
         gate_val = jnp.dot(flat, gate_rows, preferred_element_type=jnp.float32)
         up_val = jnp.dot(flat, up_rows, preferred_element_type=jnp.float32)
         activated = (jax.nn.silu(gate_val) * up_val).astype(jnp.bfloat16)
         product = jnp.dot(activated, down_rows, preferred_element_type=jnp.float32)
-        return lax.psum_scatter(
-            product.astype(jnp.bfloat16).reshape(rows.shape), "exp", scatter_dimension=0, tiled=True
-        )
-
-    own_sum = expert_rows(mine)
-    partner_sum = expert_rows(other)
+        pieces = product.astype(jnp.bfloat16).reshape(rows.shape)
+        if not by_permutes:
+            return lax.psum_scatter(pieces, "exp", scatter_dimension=0, tiled=True)
+        pieces = pieces.reshape((n_exp, capacity) + rows.shape[1:])
+        place = lax.axis_index("exp")
+        total = lax.dynamic_index_in_dim(pieces, place, 0, False).astype(jnp.float32)
+        for shift in range(1, n_exp):
+            outgoing = lax.dynamic_index_in_dim(pieces, (place + shift) % n_exp, 0, False)
+            total = total + lax.ppermute(
+                outgoing, "exp", [(i, (i + shift) % n_exp) for i in range(n_exp)]
+            ).astype(jnp.float32)
+        return total.astype(jnp.bfloat16)
+
+    own_sum = expert_rows(mine, False)
+    partner_sum = expert_rows(other, True)
     partner_half = lax.ppermute(partner_sum, "core", swap)
     both_halves = (own_sum.astype(jnp.float32) + partner_half.astype(jnp.float32)).astype(jnp.bfloat16)
     returned = lax.all_to_all(both_halves, "chip", split_axis=1, concat_axis=1, tiled=True)

time: 374 us -> 366 us (0.979)
  waiting for transfers between devices: 121 us -> 110 us
  local copies, waits for them, and re-layouts: 41.5 us -> 37.5 us
    unnamed x5 -> x3, waiting for transfers between devices: 59.2 us -> 0.73 us
    ppermute x0 -> x3, waiting for transfers between devices: none -> 51.9 us  [expert_rows(): lax.ppermute(outgoing, 'exp', [(i, (i + shift) % n_exp) for i in range(n_...]
    unnamed x38 -> x33, local copies, waits for them, and re-layouts: 20.6 us -> 10.3 us
    ppermute x1, waiting for transfers between devices: 7.15 us -> 0.01 us  [local(): other = lax.ppermute(mine, 'core', swap)]
    dynamic_slice x0 -> x4, local copies, waits for them, and re-layouts: none -> 4.41 us  [the longest x1 2.66 us: expert_rows(): lax.dynamic_index_in_dim(pieces, place, 0, False).astype(jnp.float32)]
    dot_general x1, matrix products: 5.81 us -> 10.1 us  [expert_rows(): up_val = jnp.dot(flat, up_rows, preferred_element_type=jnp.float32)]
  transfers between devices with their start and end apart: 7 -> 9, of which waited for: 6 -> 6; matrix products, arithmetic and copies ran while one was open for 12% -> 21% of each run, Pallas kernels for 10% -> 10%
where the time goes in v10:
time: 366 us; the launch traced here: 360 us
  waiting for transfers between devices  110 us (30%)
  blocking collectives  74.6 us (20%)
  matrix products  61.4 us (17%)
  local copies, waits for them, and re-layouts  37.5 us (10%)
  Pallas kernels  36.9 us (10%)
  starting transfers between devices  14.8 us (4%)
  between operations  14.1 us (4%)
  other arithmetic  10.4 us (3%)
    all_to_all x1, blocking collectives, local(): lax.all_to_all(placed, 'chip', split_axis=1, concat_axis=1, tiled=True)  54.7 us
    ppermute x3, waiting for transfers between devices, expert_rows(): lax.ppermute(outgoing, 'exp', [(i, (i + shift) % n_exp) for i in range(n_...  51.9 us
    pallas_call x1, Pallas kernels, entering(): pl.pallas_call(functools.partial(scan_kernel, count), out_shape=(jax.Shap...  36.9 us
    dot_general x2, matrix products, expert_rows(): product = jnp.dot(activated, down_rows, preferred_element_type=jnp.float32)  33.4 us
    all_gather x1, waiting for transfers between devices, local(): lax.all_gather(out_proj, CTX, axis=1, tiled=True)  24.2 us
    all_to_all x1, blocking collectives, local(): lax.all_to_all(joined.reshape(n_exp, tok_quarter, joined.shape[1]), 'exp'...  19.9 us
    all_to_all x1, waiting for transfers between devices, local(): lax.all_to_all(both_halves, 'chip', split_axis=1, concat_axis=1, tiled=True)  17.2 us
    all_to_all x1, waiting for transfers between devices, local(): lax.all_to_all(jnp.broadcast_to(quarter_sum[None], (n_exp,) + quarter_sum...  13.7 us
  transfers between devices with their start and end apart: 9, of which 6 were waited for; matrix products, arithmetic and copies ran while one was open for 21% of the time, Pallas kernels for 10%

profile of v10, /device:TPU:0, one launch (start us, length us, event | category | flops | bytes accessed | tf_op | source)
XLA Modules:
  0.0 360.1 jit_solution(5206080995642218870)
XLA Ops:
  6.5 0.7 all-gather.2.cloned.1.call-update
  7.3 1.2 copy.57
  8.5 1.0 reduce_window_sum.33
  9.6 0.8 exponential_bitcast_fusion
  10.8 1.2 copy.88
  12.0 0.7 broadcast_in_dim.33.decay_ref
  12.6 36.9 %shard_map.163 = (f32[16,128]{1,0:T(8,128)}, f32[16,8192]{1,0:T(8,128)}) custom-call(f32[16,128]{1,0:T(8,128)} %broadcast_in_dim.33.decay_ref, f32[16,8192]{1,0:T(8,128)} %bitcast.107), custom_call_target="tpu_custom_call" | custom-call | tf_op jit(solution)/shard_map/pallas_call | solution.py:93
  49.5 1.1 copy.76
  50.7 0.8 slice_reduce_fusion
  52.2 1.4 fusion.25
  54.2 24.2 %all-gather.2.cloned.1.call-done = bf16[1024,4096]{1,0:T(8,128)(2,1)} async-done(((bf16[1024,128]{1,0:T(8,128)(2,1)}), bf16[1024,4096]{1,0:T(8,128)(2,1)}) %all-gather.2.cloned.1.call-update) | async-done | bytes 8388624 | tf_op jit(solution)/shard_map/all_gather | solution.py:193
  78.4 4.7 %convolution_convert_fusion.1 = bf16[128,4096]{1,0:T(8,128)(2,1)S(1)} fusion(bf16[1024,4096]{1,0:T(8,128)(2,1)} %all-gather.2.cloned.1.call-done, f32[1024]{0:T(1024)S(1)} %copy-done.10, f32[128,1024]{1,0:T(8,128)S(1)} %copy.58, bf16[128,1024]{1,0:T(8,128)(2,1)S(1)} %copy-done.4), kind=kOutput, calls=%fused_computation.16 | convolution fusion | flops 1075314688 | bytes 10227712 | tf_op jit(solution)/shard_map/dot_general | solution.py:191
  83.2 19.9 %all_to_all.20 = bf16[4,32,4224]{2,1,0:T(8,128)(2,1)S(1)} all-to-all(bf16[4,32,4224]{2,1,0:T(8,128)(2,1)S(1)} %pad_maximum_fusion), channel_id=1, replica_groups=mesh['chip'=16,'core'=2,'exp'=4] {'exp'}, dimensions={0} | all-to-all | bytes 2162688 | tf_op jit(solution)/shard_map/all_to_all | solution.py:200
  103.4 1.1 broadcast_in_dim.36
  104.5 3.5 all-to-all-start.1
  108.0 0.5 reduce-scatter.4.cloned.1.call-start
  109.2 13.7 %all-to-all-done.1 = bf16[4,32,4224]{2,1,0:T(8,128)(2,1)S(1)} async-done(((bf16[4,32,4224]{2,1,0:T(8,128)(2,1)}), bf16[4,32,4224]{2,1,0:T(8,128)(2,1)S(1)}, u32[]{:S(2)}, u32[]{:S(2)}) %all-to-all-start.1) | async-done | bytes 1081376 | tf_op jit(solution)/shard_map/all_to_all | solution.py:204
  123.3 0.6 multiply_reduce_fusion
  124.3 3.4 broadcast_in_dim.37
  127.8 4.1 %reshape.141 = bf16[4,64,4096]{2,1,0:T(8,128)(2,1)} reshape(bf16[4,32,2,4096]{3,2,1,0:T(2,128)(2,1)} %broadcast_in_dim.37) | data formatting | bytes 4194304 | tf_op jit(solution)/shard_map/vmap()/reshape | solution.py:128
  131.9 2.9 convolution_convert_fusion
  134.8 2.3 copy.60
  137.1 54.7 %all_to_all.21 = bf16[32,16,4096]{2,0,1:T(8,128)(2,1)S(1)} all-to-all(bf16[32,16,4096]{2,0,1:T(8,128)(2,1)S(1)} %copy.60), channel_id=1, replica_groups=mesh['chip'=16,'core'=2,'exp'=4] {'chip'}, dimensions={1} | all-to-all | bytes 8388608 | tf_op jit(solution)/shard_map/all_to_all | solution.py:228
  191.8 4.3 %copy.61 = bf16[32,16,4096]{2,1,0:T(8,128)(2,1)} copy(bf16[32,16,4096]{2,0,1:T(8,128)(2,1)S(1)} %all_to_all.21) | data formatting | bytes 8388608 | tf_op jit(solution)/shard_map/all_to_all | solution.py:228
  196.3 8.0 %fusion.10 = f32[512,896]{1,0:T(8,128)} fusion(bf16[512,4096]{1,0:T(8,128)(2,1)} %bitcast.13, bf16[1,4096,896]{2,1,0:T(8,128)(2,1)S(1)} %bitcast.119), kind=kOutput, calls=%fused_computation.11 | convolution fusion | flops 3758096384 | bytes 13369344 | tf_op jit(solution)/shard_map/dot_general | solution.py:234
  204.3 16.5 %fusion.12 = bf16[512,4096]{1,0:T(8,128)(2,1)} fusion(bf16[1,896,4096]{2,1,0:T(8,128)(2,1)} %param.31, f32[512,896]{1,0:T(8,128)} %fusion.10, bf16[512,4096]{1,0:T(8,128)(2,1)} %bitcast.13, bf16[1,4096,896]{2,1,0:T(8,128)(2,1)} %param.30), kind=kOutput, calls=%fused_computation.14 | convolution fusion | flops 7521042432 | bytes 24903680 | tf_op jit(solution)/shard_map/dot_general | solution.py:237
  220.8 6.5 %copy.77 = bf16[4,8,16,4096]{3,1,2,0:T(8,128)(2,1)} copy(bf16[4,8,16,4096]{3,2,1,0:T(8,128)(2,1)} %bitcast.106) | data formatting | bytes 8388608
  227.4 10.1 %fusion.4 = f32[512,896]{1,0:T(8,128)} fusion(bf16[512,4096]{1,0:T(8,128)(2,1)} %bitcast.18, bf16[1,4096,896]{2,1,0:T(8,128)(2,1)} %param.30), kind=kOutput, calls=%fused_computation.5 | convolution fusion | flops 3758096384 | bytes 13369344 | tf_op jit(solution)/shard_map/dot_general | solution.py:235
  237.5 16.8 %fusion.15 = bf16[512,4096]{1,0:T(8,128)(2,1)} fusion(bf16[1,896,4096]{2,1,0:T(8,128)(2,1)} %param.31, f32[512,896]{1,0:T(8,128)} %fusion.4, bf16[512,4096]{1,0:T(8,128)(2,1)} %bitcast.18, bf16[1,4096,896]{2,1,0:T(8,128)(2,1)} %param.29), kind=kOutput, calls=%fused_computation.15 | convolution fusion | flops 7521042432 | bytes 24903680 | tf_op jit(solution)/shard_map/dot_general | solution.py:237
  254.4 2.7 constant_dynamic-slice_fusion.4
  257.1 0.6 copy.87
  257.6 0.6 collective-permute-start.1
  258.3 0.6 copy.86
  258.9 2.2 collective-permute-start.2
  261.0 0.6 copy.85
  261.6 0.7 collective-permute-start.3
  262.3 29.2 %collective-permute-done.1 = bf16[8,16,4096]{2,0,1:T(8,128)(2,1)S(1)} collective-permute-done((bf16[8,16,4096]{2,0,1:T(8,128)(2,1)S(1)}, bf16[8,16,4096]{2,0,1:T(8,128)(2,1)S(1)}, u32[]{:S(2)}, u32[]{:S(2)}) %collective-permute-start.1) | collective-permute-done | bytes 1048608 | tf_op jit(solution)/shard_map/ppermute | solution.py:246
  291.5 22.8 %collective-permute-done.2 = bf16[8,16,4096]{2,0,1:T(8,128)(2,1)S(1)} collective-permute-done((bf16[8,16,4096]{2,0,1:T(8,128)(2,1)S(1)}, bf16[8,16,4096]{2,0,1:T(8,128)(2,1)S(1)}, u32[]{:S(2)}, u32[]{:S(2)}) %collective-permute-start.2) | collective-permute-done | bytes 1048608 | tf_op jit(solution)/shard_map/ppermute | solution.py:246
  314.2 1.0 fusion.21
  315.3 2.6 collective-permute-done.4
  318.0 2.5 add_convert_fusion
  320.5 7.0 %all-to-all-start.3 = ((bf16[8,16,4096]{2,0,1:T(8,128)(2,1)}), bf16[8,16,4096]{2,0,1:T(8,128)(2,1)}, u32[]{:S(2)}, u32[]{:S(2)}) async-start(bf16[8,16,4096]{2,0,1:T(8,128)(2,1)} %add_convert_fusion), calls=%async_computation.3 | async-start | bytes 2097152 | tf_op jit(solution)/shard_map/all_to_all | solution.py:255
  328.4 17.2 %all-to-all-done.3 = bf16[8,16,4096]{2,0,1:T(8,128)(2,1)} async-done(((bf16[8,16,4096]{2,0,1:T(8,128)(2,1)}), bf16[8,16,4096]{2,0,1:T(8,128)(2,1)}, u32[]{:S(2)}, u32[]{:S(2)}) %all-to-all-start.3) | async-done | bytes 1048608 | tf_op jit(solution)/shard_map/all_to_all | solution.py:255
  345.7 1.8 copy.68
  347.5 1.7 gather_fusion
  349.1 1.7 reshape.151
  350.8 1.4 multiply_reduce_fusion.1
  352.3 0.8 add_convert_fusion.1
  (69 shorter events, 4.8 us)
Async XLA Ops:
  6.5 3.9 %copy-start = (bf16[128,128]{1,0:T(8,128)(2,1)S(1)}, bf16[128,128]{1,0:T(8,128)(2,1)}, u32[]{:S(2)}) copy-start(bf16[128,128]{1,0:T(8,128)(2,1)} %param.19) | copy-start | bytes 98308
  6.5 45.0 %copy-start.5 = (bf16[128,128]{1,0:T(8,128)(2,1)S(1)}, bf16[128,128]{1,0:T(8,128)(2,1)}, u32[]{:S(2)}) copy-start(bf16[128,128]{1,0:T(8,128)(2,1)} %param.20) | copy-start | bytes 98308
  6.5 71.8 %all-gather.2.cloned.1.call-start = ((), (), s32[]{:S(2)}) async-start(), calls=%async_computation.5 | async-start | bytes 8650752 | tf_op jit(solution)/shard_map/all_gather | solution.py:193
  7.3 44.4 %copy-start.3 = (f32[16,64,128]{2,1,0:T(8,128)S(1)}, f32[16,64,128]{2,1,0:T(8,128)}, u32[]{:S(2)}) copy-start(f32[16,64,128]{2,1,0:T(8,128)} %param.24) | copy-start | bytes 1572868
  12.6 39.6 %copy-start.7 = (f32[16,128]{1,0:T(8,128)S(1)}, f32[16,128]{1,0:T(8,128)}, u32[]{:S(2)}) copy-start(f32[16,128]{1,0:T(8,128)} %param.21) | copy-start | bytes 24580
  12.6 39.6 %copy-start.11 = (f32[16]{0:T(128)S(1)}, f32[16]{0:T(128)}, u32[]{:S(2)}) copy-start(f32[16]{0:T(128)} %param.23) | copy-start | bytes 196
  52.2 1.6 copy-start.4
  52.2 26.1 %copy-start.10 = (f32[1024]{0:T(1024)S(1)}, f32[1024]{0:T(1024)}, u32[]{:S(2)}) copy-start(f32[1024]{0:T(1024)} %param.25) | copy-start | bytes 12292
  103.2 5.4 %copy-start.8 = (s32[128,2]{0,1:T(2,128)S(1)}, s32[128,2]{0,1:T(2,128)}, u32[]{:S(2)}) copy-start(s32[128,2]{0,1:T(2,128)} %param.32) | copy-start | bytes 3076
  104.5 18.5 %all-to-all-start.1 = ((bf16[4,32,4224]{2,1,0:T(8,128)(2,1)}), bf16[4,32,4224]{2,1,0:T(8,128)(2,1)S(1)}, u32[]{:S(2)}, u32[]{:S(2)}) async-start(bf16[4,32,4224]{2,1,0:T(8,128)(2,1)} %broadcast_in_dim.36), calls=%async_computation.1 | async-start | bytes 2162688 | tf_op jit(solution)/shard_map/all_to_all | solution.py:204
  108.0 15.3 %copy-start.2 = (bf16[128,4096]{1,0:T(8,128)(2,1)S(1)}, bf16[128,4096]{1,0:T(8,128)(2,1)}, u32[]{:S(2)}) copy-start(bf16[128,4096]{1,0:T(8,128)(2,1)} %param.27) | copy-start | bytes 3145732
  108.0 210.0 %reduce-scatter.4.cloned.1.call-start = ((), (), s32[]{:S(2)}) async-start(), calls=%async_computation.6 | async-start | bytes 5242880
  123.3 0.7 copy-start.6
  137.1 59.1 %slice-start = ((s8[7340032]{0:T(1024)(128)(4,1)}), s8[3145728]{0:T(1024)(128)(4,1)S(1)}, s32[]{:S(2)}) async-start(s8[7340032]{0:T(1024)(128)(4,1)} %bitcast.118), calls=%async_computation.7 | async-start | bytes 6291456
  191.8 4.5 %slice-start.1 = ((s8[7340032]{0:T(1024)(128)(4,1)}), s8[4194304]{0:T(1024)(128)(4,1)S(1)}, s32[]{:S(2)}) async-start(s8[7340032]{0:T(1024)(128)(4,1)} %bitcast.118), calls=%async_computation.8 | async-start | bytes 8388608
  196.1 31.3 %collective-permute-start = (bf16[32,16,4096]{2,1,0:T(8,128)(2,1)}, bf16[32,16,4096]{2,1,0:T(8,128)(2,1)}, u32[]{:S(2)}, u32[]{:S(2)}) collective-permute-start(bf16[32,16,4096]{2,1,0:T(8,128)(2,1)} %copy.61), channel_id=1, source_target_pairs={{0,4},{4,0},{1,5},{5,1},{2,6},{6,2},{3,7},{7,3},{8,12},{12,8},{9,1... | collective-permute-start | bytes 12582920 | tf_op jit(solution)/shard_map/ppermute | solution.py:229
  257.6 33.8 %collective-permute-start.1 = (bf16[8,16,4096]{2,0,1:T(8,128)(2,1)S(1)}, bf16[8,16,4096]{2,0,1:T(8,128)(2,1)S(1)}, u32[]{:S(2)}, u32[]{:S(2)}) collective-permute-start(bf16[8,16,4096]{2,0,1:T(8,128)(2,1)S(1)} %bitcast.112), channel_id=1, source_target_pairs={{0,1},{1,2},{2,3},{3,0},{4,5},{5,6},{6,7},{7,4},{8,9},{9,10},{10,1... | collective-permute-start | bytes 3145736 | tf_op jit(solution)/shard_map/ppermute | solution.py:246
  258.9 55.4 %collective-permute-start.2 = (bf16[8,16,4096]{2,0,1:T(8,128)(2,1)S(1)}, bf16[8,16,4096]{2,0,1:T(8,128)(2,1)S(1)}, u32[]{:S(2)}, u32[]{:S(2)}) collective-permute-start(bf16[8,16,4096]{2,0,1:T(8,128)(2,1)S(1)} %bitcast.113), channel_id=1, source_target_pairs={{0,2},{1,3},{2,0},{3,1},{4,6},{5,7},{6,4},{7,5},{8,10},{9,11},{10,... | collective-permute-start | bytes 3145736 | tf_op jit(solution)/shard_map/ppermute | solution.py:246
  261.6 52.6 %collective-permute-start.3 = (bf16[8,16,4096]{2,0,1:T(8,128)(2,1)S(1)}, bf16[8,16,4096]{2,0,1:T(8,128)(2,1)S(1)}, u32[]{:S(2)}, u32[]{:S(2)}) collective-permute-start(bf16[8,16,4096]{2,0,1:T(8,128)(2,1)S(1)} %bitcast.114), channel_id=1, source_target_pairs={{0,3},{1,0},{2,1},{3,2},{4,7},{5,4},{6,5},{7,6},{8,11},{9,8},{10,9... | collective-permute-start | bytes 3145736 | tf_op jit(solution)/shard_map/ppermute | solution.py:246
  315.2 2.7 collective-permute-start.4
  318.0 10.1 %copy-start.9 = (f32[128,2]{0,1:T(2,128)S(1)}, f32[128,2]{0,1:T(2,128)}, u32[]{:S(2)}) copy-start(f32[128,2]{0,1:T(2,128)} %param.33) | copy-start | bytes 3076
  320.5 25.2 %all-to-all-start.3 = ((bf16[8,16,4096]{2,0,1:T(8,128)(2,1)}), bf16[8,16,4096]{2,0,1:T(8,128)(2,1)}, u32[]{:S(2)}, u32[]{:S(2)}) async-start(bf16[8,16,4096]{2,0,1:T(8,128)(2,1)} %add_convert_fusion), calls=%async_computation.3 | async-start | bytes 2097152 | tf_op jit(solution)/shard_map/all_to_all | solution.py:255
  347.5 5.6 %copy-start.1 = (bf16[128,128]{1,0:T(8,128)(2,1)S(1)}, bf16[128,128]{1,0:T(8,128)(2,1)}, u32[]{:S(2)}) copy-start(bf16[128,128]{1,0:T(8,128)(2,1)} %param.19) | copy-start | bytes 98308
Sparse Core Ops, SparseCore 0:
  9.5 68.7 all-gather.1
  227.5 65.1 reduce-scatter.3

commit v11 on v10

--- a/solution.py
+++ b/solution.py
@@ -248,8 +248,8 @@
             ).astype(jnp.float32)
         return total.astype(jnp.bfloat16)
 
-    own_sum = expert_rows(mine, False)
-    partner_sum = expert_rows(other, True)
+    own_sum = expert_rows(mine, True)
+    partner_sum = expert_rows(other, False)
     partner_half = lax.ppermute(partner_sum, "core", swap)
     both_halves = (own_sum.astype(jnp.float32) + partner_half.astype(jnp.float32)).astype(jnp.bfloat16)
     returned = lax.all_to_all(both_halves, "chip", split_axis=1, concat_axis=1, tiled=True)

time: 366 us -> 370 us (1.011)
  local copies, waits for them, and re-layouts: 37.5 us -> 42.4 us
    ppermute x3, waiting for transfers between devices: 51.9 us -> 19.5 us  [expert_rows(): lax.ppermute(outgoing, 'exp', [(i, (i + shift) % n_exp) for i in range(n_...]
    unnamed x3, waiting for transfers between devices: 0.73 us -> 30.7 us
    ppermute x1, waiting for transfers between devices: 0.01 us -> 7.15 us  [local(): other = lax.ppermute(mine, 'core', swap)]
    dot_general x1, matrix products: 10.1 us -> 5.81 us  [expert_rows(): up_val = jnp.dot(flat, up_rows, preferred_element_type=jnp.float32)]
    unnamed x33 -> x37, local copies, waits for them, and re-layouts: 10.3 us -> 14.1 us
  transfers between devices with their start and end apart: 9 -> 9, of which waited for: 6 -> 6; matrix products, arithmetic and copies ran while one was open for 21% -> 13% of each run, Pallas kernels for 10% -> 10%
where the time goes in v11:
time: 370 us; the launch traced here: 365 us
  waiting for transfers between devices  112 us (30%)
  blocking collectives  74.6 us (20%)
  matrix products  59.2 us (16%)
  local copies, waits for them, and re-layouts  42.4 us (11%)
  Pallas kernels  36.9 us (10%)
  starting transfers between devices  14.3 us (4%)
  between operations  14.1 us (4%)
  other arithmetic  10.9 us (3%)
    all_to_all x1, blocking collectives, local(): lax.all_to_all(placed, 'chip', split_axis=1, concat_axis=1, tiled=True)  54.7 us
    pallas_call x1, Pallas kernels, entering(): pl.pallas_call(functools.partial(scan_kernel, count), out_shape=(jax.Shap...  36.9 us
    dot_general x2, matrix products, expert_rows(): product = jnp.dot(activated, down_rows, preferred_element_type=jnp.float32)  33.4 us
    unnamed x3, waiting for transfers between devices  30.7 us
    all_gather x1, waiting for transfers between devices, local(): lax.all_gather(out_proj, CTX, axis=1, tiled=True)  24.2 us
    all_to_all x1, blocking collectives, local(): lax.all_to_all(joined.reshape(n_exp, tok_quarter, joined.shape[1]), 'exp'...  19.9 us
    ppermute x3, waiting for transfers between devices, expert_rows(): lax.ppermute(outgoing, 'exp', [(i, (i + shift) % n_exp) for i in range(n_...  19.5 us
    all_to_all x1, waiting for transfers between devices, local(): lax.all_to_all(both_halves, 'chip', split_axis=1, concat_axis=1, tiled=True)  17 us
  transfers between devices with their start and end apart: 9, of which 6 were waited for; matrix products, arithmetic and copies ran while one was open for 13% of the time, Pallas kernels for 10%

profile of v11, /device:TPU:0, one launch (start us, length us, event | category | flops | bytes accessed | tf_op | source)
XLA Modules:
  0.0 364.5 jit_solution(13972647879693295788)
XLA Ops:
  6.5 0.7 all-gather.2.cloned.1.call-update
  7.3 1.2 copy.57
  8.5 1.0 reduce_window_sum.33
  9.6 0.8 exponential_bitcast_fusion
  10.8 1.2 copy.88
  12.0 0.7 broadcast_in_dim.33.decay_ref
  12.6 36.9 %shard_map.163 = (f32[16,128]{1,0:T(8,128)}, f32[16,8192]{1,0:T(8,128)}) custom-call(f32[16,128]{1,0:T(8,128)} %broadcast_in_dim.33.decay_ref, f32[16,8192]{1,0:T(8,128)} %bitcast.109), custom_call_target="tpu_custom_call" | custom-call | tf_op jit(solution)/shard_map/pallas_call | solution.py:93
  49.5 1.1 copy.76
  50.7 0.8 slice_reduce_fusion
  52.2 1.4 fusion.25
  54.2 24.2 %all-gather.2.cloned.1.call-done = bf16[1024,4096]{1,0:T(8,128)(2,1)} async-done(((bf16[1024,128]{1,0:T(8,128)(2,1)}), bf16[1024,4096]{1,0:T(8,128)(2,1)}) %all-gather.2.cloned.1.call-update) | async-done | bytes 8388624 | tf_op jit(solution)/shard_map/all_gather | solution.py:193
  78.4 4.7 %convolution_convert_fusion.1 = bf16[128,4096]{1,0:T(8,128)(2,1)S(1)} fusion(bf16[1024,4096]{1,0:T(8,128)(2,1)} %all-gather.2.cloned.1.call-done, f32[1024]{0:T(1024)S(1)} %copy-done.12, f32[128,1024]{1,0:T(8,128)S(1)} %copy.58, bf16[128,1024]{1,0:T(8,128)(2,1)S(1)} %copy-done.5), kind=kOutput, calls=%fused_computation.16 | convolution fusion | flops 1075314688 | bytes 10227712 | tf_op jit(solution)/shard_map/dot_general | solution.py:191
  83.2 19.9 %all_to_all.20 = bf16[4,32,4224]{2,1,0:T(8,128)(2,1)S(1)} all-to-all(bf16[4,32,4224]{2,1,0:T(8,128)(2,1)S(1)} %pad_maximum_fusion), channel_id=1, replica_groups=mesh['chip'=16,'core'=2,'exp'=4] {'exp'}, dimensions={0} | all-to-all | bytes 2162688 | tf_op jit(solution)/shard_map/all_to_all | solution.py:200
  103.4 1.1 broadcast_in_dim.36
  104.5 3.5 all-to-all-start.1
  108.0 0.6 reduce-scatter.4.cloned.1.call-start
  109.3 13.7 %all-to-all-done.1 = bf16[4,32,4224]{2,1,0:T(8,128)(2,1)S(1)} async-done(((bf16[4,32,4224]{2,1,0:T(8,128)(2,1)}), bf16[4,32,4224]{2,1,0:T(8,128)(2,1)S(1)}, u32[]{:S(2)}, u32[]{:S(2)}) %all-to-all-start.1) | async-done | bytes 1081376 | tf_op jit(solution)/shard_map/all_to_all | solution.py:204
  123.3 0.6 multiply_reduce_fusion
  124.3 3.4 broadcast_in_dim.37
  127.8 4.1 %reshape.141 = bf16[4,64,4096]{2,1,0:T(8,128)(2,1)} reshape(bf16[4,32,2,4096]{3,2,1,0:T(2,128)(2,1)} %broadcast_in_dim.37) | data formatting | bytes 4194304 | tf_op jit(solution)/shard_map/vmap()/reshape | solution.py:128
  131.9 2.9 convolution_convert_fusion
  134.8 2.3 copy.60
  137.1 54.7 %all_to_all.21 = bf16[32,16,4096]{2,0,1:T(8,128)(2,1)S(1)} all-to-all(bf16[32,16,4096]{2,0,1:T(8,128)(2,1)S(1)} %copy.60), channel_id=1, replica_groups=mesh['chip'=16,'core'=2,'exp'=4] {'chip'}, dimensions={1} | all-to-all | bytes 8388608 | tf_op jit(solution)/shard_map/all_to_all | solution.py:228
  191.8 2.3 copy.61
  194.1 2.0 copy-done.2
  196.3 7.1 %collective-permute-done.3 = bf16[32,16,4096]{2,1,0:T(8,128)(2,1)S(1)} collective-permute-done((bf16[32,16,4096]{2,1,0:T(8,128)(2,1)S(1)}, bf16[32,16,4096]{2,1,0:T(8,128)(2,1)S(1)}, u32[]{:S(2)}, u32[]{:S(2)}) %collective-permute-start.3) | collective-permute-done | bytes 4194336 | tf_op jit(solution)/shard_map/ppermute | solution.py:229
  203.4 1.9 copy-done.11
  205.3 5.8 %fusion.4 = f32[512,896]{1,0:T(8,128)} fusion(bf16[512,4096]{1,0:T(8,128)(2,1)S(1)} %bitcast.118, bf16[1,4096,896]{2,1,0:T(8,128)(2,1)S(1)} %bitcast.117), kind=kOutput, calls=%fused_computation.5 | convolution fusion | flops 3758096384 | bytes 13369344 | tf_op jit(solution)/shard_map/dot_general | solution.py:235
  211.1 16.5 %fusion.15 = bf16[512,4096]{1,0:T(8,128)(2,1)} fusion(bf16[1,896,4096]{2,1,0:T(8,128)(2,1)} %param.31, f32[512,896]{1,0:T(8,128)} %fusion.4, bf16[512,4096]{1,0:T(8,128)(2,1)} %bitcast.119, bf16[1,4096,896]{2,1,0:T(8,128)(2,1)} %param.29), kind=kOutput, calls=%fused_computation.15 | convolution fusion | flops 7521042432 | bytes 24903680 | tf_op jit(solution)/shard_map/dot_general | solution.py:237
  227.6 6.5 %copy.77 = bf16[4,8,16,4096]{3,1,2,0:T(8,128)(2,1)} copy(bf16[4,8,16,4096]{3,2,1,0:T(8,128)(2,1)} %bitcast.108) | data formatting | bytes 8388608
  234.1 10.1 %fusion.10 = f32[512,896]{1,0:T(8,128)} fusion(bf16[512,4096]{1,0:T(8,128)(2,1)} %bitcast.106, bf16[1,4096,896]{2,1,0:T(8,128)(2,1)} %param.29), kind=kOutput, calls=%fused_computation.11 | convolution fusion | flops 3758096384 | bytes 13369344 | tf_op jit(solution)/shard_map/dot_general | solution.py:234
  244.3 16.9 %fusion.12 = bf16[512,4096]{1,0:T(8,128)(2,1)} fusion(bf16[1,896,4096]{2,1,0:T(8,128)(2,1)} %param.31, f32[512,896]{1,0:T(8,128)} %fusion.10, bf16[512,4096]{1,0:T(8,128)(2,1)} %bitcast.107, bf16[1,4096,896]{2,1,0:T(8,128)(2,1)} %param.30), kind=kOutput, calls=%fused_computation.14 | convolution fusion | flops 7521042432 | bytes 24903680 | tf_op jit(solution)/shard_map/dot_general | solution.py:237
  261.1 2.6 constant_dynamic-slice_fusion.4
  263.8 1.6 copy.85
  265.3 1.1 collective-permute-start.2
  266.5 1.6 copy.86
  268.1 1.5 collective-permute-start.1
  269.6 1.6 copy.87
  271.2 30.0 %reduce-scatter.4.cloned.1.call-done = bf16[8,65536]{1,0:T(8,128)(2,1)} async-done(((bf16[32,65536]{1,0:T(8,128)(2,1)}), bf16[8,65536]{1,0:T(8,128)(2,1)}) %reduce-scatter.4.cloned.1.call-update) | async-done | bytes 1048592
  301.2 19.5 %collective-permute-done = bf16[8,16,4096]{2,0,1:T(8,128)(2,1)} collective-permute-done((bf16[8,16,4096]{2,0,1:T(8,128)(2,1)}, bf16[8,16,4096]{2,0,1:T(8,128)(2,1)}, u32[]{:S(2)}, u32[]{:S(2)}) %collective-permute-start) | collective-permute-done | bytes 1048608 | tf_op jit(solution)/shard_map/ppermute | solution.py:246
  320.7 4.0 %add_convert_fusion = bf16[8,16,4096]{2,0,1:T(8,128)(2,1)} fusion(bf16[8,16,4096]{2,0,1:T(8,128)(2,1)S(1)} %collective-permute-done.4, bf16[8,16,4096]{2,0,1:T(8,128)(2,1)} %collective-permute-done.2, bf16[8,16,4096]{2,0,1:T(8,128)(2,1)} %collective-permute-done.1, bf16[8,16,4096]{2,0,1:T(8,128)(2,1)} %collective-permute-done, ...), kind=kLoop, calls=%fused_computation.23 | loop fusion | flops 6291456 | bytes 6291456 | tf_op jit(solution)/shard_map/convert_element_type | solution.py:254
  324.7 7.4 %all-to-all-start.3 = ((bf16[8,16,4096]{2,0,1:T(8,128)(2,1)}), bf16[8,16,4096]{2,0,1:T(8,128)(2,1)}, u32[]{:S(2)}, u32[]{:S(2)}) async-start(bf16[8,16,4096]{2,0,1:T(8,128)(2,1)} %add_convert_fusion), calls=%async_computation.3 | async-start | bytes 2097152 | tf_op jit(solution)/shard_map/all_to_all | solution.py:255
  333.1 17.0 %all-to-all-done.3 = bf16[8,16,4096]{2,0,1:T(8,128)(2,1)} async-done(((bf16[8,16,4096]{2,0,1:T(8,128)(2,1)}), bf16[8,16,4096]{2,0,1:T(8,128)(2,1)}, u32[]{:S(2)}, u32[]{:S(2)}) %all-to-all-start.3) | async-done | bytes 1048608 | tf_op jit(solution)/shard_map/all_to_all | solution.py:255
  350.0 1.8 copy.68
  351.8 1.7 gather_fusion
  353.5 1.7 reshape.151
  355.2 1.4 multiply_reduce_fusion.1
  356.6 0.8 add_convert_fusion.1
  (72 shorter events, 4.7 us)
Async XLA Ops:
  6.5 3.9 %copy-start = (bf16[128,128]{1,0:T(8,128)(2,1)S(1)}, bf16[128,128]{1,0:T(8,128)(2,1)}, u32[]{:S(2)}) copy-start(bf16[128,128]{1,0:T(8,128)(2,1)} %param.19) | copy-start | bytes 98308
  6.5 45.0 %copy-start.6 = (bf16[128,128]{1,0:T(8,128)(2,1)S(1)}, bf16[128,128]{1,0:T(8,128)(2,1)}, u32[]{:S(2)}) copy-start(bf16[128,128]{1,0:T(8,128)(2,1)} %param.20) | copy-start | bytes 98308
  6.5 71.8 %all-gather.2.cloned.1.call-start = ((), (), s32[]{:S(2)}) async-start(), calls=%async_computation.5 | async-start | bytes 8650752 | tf_op jit(solution)/shard_map/all_gather | solution.py:193
  7.3 44.4 %copy-start.4 = (f32[16,64,128]{2,1,0:T(8,128)S(1)}, f32[16,64,128]{2,1,0:T(8,128)}, u32[]{:S(2)}) copy-start(f32[16,64,128]{2,1,0:T(8,128)} %param.24) | copy-start | bytes 1572868
  12.6 39.6 %copy-start.8 = (f32[16,128]{1,0:T(8,128)S(1)}, f32[16,128]{1,0:T(8,128)}, u32[]{:S(2)}) copy-start(f32[16,128]{1,0:T(8,128)} %param.21) | copy-start | bytes 24580
  12.6 39.6 %copy-start.13 = (f32[16]{0:T(128)S(1)}, f32[16]{0:T(128)}, u32[]{:S(2)}) copy-start(f32[16]{0:T(128)} %param.23) | copy-start | bytes 196
  52.2 1.6 copy-start.5
  52.2 26.1 %copy-start.12 = (f32[1024]{0:T(1024)S(1)}, f32[1024]{0:T(1024)}, u32[]{:S(2)}) copy-start(f32[1024]{0:T(1024)} %param.25) | copy-start | bytes 12292
  103.2 5.4 %copy-start.9 = (s32[128,2]{0,1:T(2,128)S(1)}, s32[128,2]{0,1:T(2,128)}, u32[]{:S(2)}) copy-start(s32[128,2]{0,1:T(2,128)} %param.32) | copy-start | bytes 3076
  104.5 18.5 %all-to-all-start.1 = ((bf16[4,32,4224]{2,1,0:T(8,128)(2,1)}), bf16[4,32,4224]{2,1,0:T(8,128)(2,1)S(1)}, u32[]{:S(2)}, u32[]{:S(2)}) async-start(bf16[4,32,4224]{2,1,0:T(8,128)(2,1)} %broadcast_in_dim.36), calls=%async_computation.1 | async-start | bytes 2162688 | tf_op jit(solution)/shard_map/all_to_all | solution.py:204
  108.0 15.3 %copy-start.3 = (bf16[128,4096]{1,0:T(8,128)(2,1)S(1)}, bf16[128,4096]{1,0:T(8,128)(2,1)}, u32[]{:S(2)}) copy-start(bf16[128,4096]{1,0:T(8,128)(2,1)} %param.27) | copy-start | bytes 3145732
  108.0 193.2 %reduce-scatter.4.cloned.1.call-start = ((), (), s32[]{:S(2)}) async-start(), calls=%async_computation.6 | async-start | bytes 5242880
  123.3 0.7 copy-start.7
  137.1 68.2 %slice-start = ((s8[7340032]{0:T(1024)(128)(4,1)}), s8[4194304]{0:T(1024)(128)(4,1)S(1)}, s32[]{:S(2)}) async-start(s8[7340032]{0:T(1024)(128)(4,1)} %bitcast.116), calls=%async_computation.7 | async-start | bytes 8388608
  191.8 13.5 %slice-start.1 = ((s8[7340032]{0:T(1024)(128)(4,1)}), s8[3145728]{0:T(1024)(128)(4,1)S(1)}, s32[]{:S(2)}) async-start(s8[7340032]{0:T(1024)(128)(4,1)} %bitcast.116), calls=%async_computation.8 | async-start | bytes 6291456
  194.1 2.0 copy-start.2
  196.1 7.3 %collective-permute-start.3 = (bf16[32,16,4096]{2,1,0:T(8,128)(2,1)S(1)}, bf16[32,16,4096]{2,1,0:T(8,128)(2,1)S(1)}, u32[]{:S(2)}, u32[]{:S(2)}) collective-permute-start(bf16[32,16,4096]{2,1,0:T(8,128)(2,1)S(1)} %copy.61), channel_id=1, source_target_pairs={{0,4},{4,0},{1,5},{5,1},{2,6},{6,2},{3,7},{7,3},{8,12},{12,8},{9,1... | collective-permute-start | bytes 12582920 | tf_op jit(solution)/shard_map/ppermute | solution.py:229
  203.4 1.9 copy-start.11
  265.3 35.8 %collective-permute-start.2 = (bf16[8,16,4096]{2,0,1:T(8,128)(2,1)}, bf16[8,16,4096]{2,0,1:T(8,128)(2,1)}, u32[]{:S(2)}, u32[]{:S(2)}) collective-permute-start(bf16[8,16,4096]{2,0,1:T(8,128)(2,1)} %bitcast.97), channel_id=1, source_target_pairs={{0,3},{1,0},{2,1},{3,2},{4,7},{5,4},{6,5},{7,6},{8,11},{9,8},{10,9... | collective-permute-start | bytes 3145736 | tf_op jit(solution)/shard_map/ppermute | solution.py:246
  268.1 33.0 %collective-permute-start.1 = (bf16[8,16,4096]{2,0,1:T(8,128)(2,1)}, bf16[8,16,4096]{2,0,1:T(8,128)(2,1)}, u32[]{:S(2)}, u32[]{:S(2)}) collective-permute-start(bf16[8,16,4096]{2,0,1:T(8,128)(2,1)} %bitcast.98), channel_id=1, source_target_pairs={{0,2},{1,3},{2,0},{3,1},{4,6},{5,7},{6,4},{7,5},{8,10},{9,11},{10,... | collective-permute-start | bytes 3145736 | tf_op jit(solution)/shard_map/ppermute | solution.py:246
  271.2 49.5 %collective-permute-start = (bf16[8,16,4096]{2,0,1:T(8,128)(2,1)}, bf16[8,16,4096]{2,0,1:T(8,128)(2,1)}, u32[]{:S(2)}, u32[]{:S(2)}) collective-permute-start(bf16[8,16,4096]{2,0,1:T(8,128)(2,1)} %bitcast.99), channel_id=1, source_target_pairs={{0,1},{1,2},{2,3},{3,0},{4,5},{5,6},{6,7},{7,4},{8,9},{9,10},{10,1... | collective-permute-start | bytes 3145736 | tf_op jit(solution)/shard_map/ppermute | solution.py:246
  301.2 19.5 %collective-permute-start.4 = (bf16[8,16,4096]{2,0,1:T(8,128)(2,1)}, bf16[8,16,4096]{2,0,1:T(8,128)(2,1)S(1)}, u32[]{:S(2)}, u32[]{:S(2)}) collective-permute-start(bf16[8,16,4096]{2,0,1:T(8,128)(2,1)} %bitcast.120), channel_id=1, source_target_pairs={{0,4},{4,0},{1,5},{5,1},{2,6},{6,2},{3,7},{7,3},{8,12},{12,8},{9,1... | collective-permute-start | bytes 3145736 | tf_op jit(solution)/shard_map/ppermute | solution.py:253
  324.7 8.0 %copy-start.10 = (f32[128,2]{0,1:T(2,128)S(1)}, f32[128,2]{0,1:T(2,128)}, u32[]{:S(2)}) copy-start(f32[128,2]{0,1:T(2,128)} %param.33) | copy-start | bytes 3076
  324.7 25.3 %all-to-all-start.3 = ((bf16[8,16,4096]{2,0,1:T(8,128)(2,1)}), bf16[8,16,4096]{2,0,1:T(8,128)(2,1)}, u32[]{:S(2)}, u32[]{:S(2)}) async-start(bf16[8,16,4096]{2,0,1:T(8,128)(2,1)} %add_convert_fusion), calls=%async_computation.3 | async-start | bytes 2097152 | tf_op jit(solution)/shard_map/all_to_all | solution.py:255
  351.8 5.6 %copy-start.1 = (bf16[128,128]{1,0:T(8,128)(2,1)S(1)}, bf16[128,128]{1,0:T(8,128)(2,1)}, u32[]{:S(2)}) copy-start(bf16[128,128]{1,0:T(8,128)(2,1)} %param.19) | copy-start | bytes 98308
Sparse Core Ops, SparseCore 0:
  9.5 68.7 all-gather.1
  234.2 66.8 reduce-scatter.3

commit v12 on v10

--- a/solution.py
+++ b/solution.py
@@ -201,11 +201,9 @@
         joined.reshape(n_exp, tok_quarter, joined.shape[1]), "exp", split_axis=0, concat_axis=0, tiled=True
     )
     quarter_sum = jnp.sum(quarters.astype(jnp.float32), axis=0).astype(jnp.bfloat16)
-    summed_parts = lax.all_to_all(
-        jnp.broadcast_to(quarter_sum[None], (n_exp,) + quarter_sum.shape), "exp", split_axis=0, concat_axis=0, tiled=True
-    ).reshape(tok_ctx, joined.shape[1]).astype(jnp.float32)
-    scaling = lax.rsqrt(summed_parts[:, width_out] / (head_count * head_dim * n_exp) + eps_norm)
-    mixed_all = summed_parts[:, :width_out] * scaling[:, None]
+    own_parts = quarter_sum.astype(jnp.float32)
+    scaling = lax.rsqrt(own_parts[:, width_out] / (head_count * head_dim * n_exp) + eps_norm)
+    mixed_own = own_parts[:, :width_out] * scaling[:, None]
     gate_rows = w_gate[0]
     up_rows = w_up[0]
     down_rows = w_down[0]
@@ -213,8 +211,12 @@
     first_row = lax.axis_index("exp") * tok_quarter
     own_ids = lax.dynamic_slice_in_dim(route_ids, first_row, tok_quarter, 0)
     own_gates = lax.dynamic_slice_in_dim(route_gates, first_row, tok_quarter, 0)
-    hidden_all = residual.astype(jnp.float32) + mixed_all
-    moe_all = rms_rows(hidden_all, moe_gain)
+    own_residual = lax.dynamic_slice_in_dim(residual, first_row, tok_quarter, 0)
+    hidden_own = own_residual.astype(jnp.float32) + mixed_own
+    moe_own = rms_rows(hidden_own, moe_gain)
+    moe_all = lax.all_to_all(
+        jnp.broadcast_to(moe_own[None], (n_exp,) + moe_own.shape), "exp", split_axis=0, concat_axis=0, tiled=True
+    ).reshape(tok_ctx, model_width)
 
     def place_quarter(quarter_rows, quarter_ids):
         return place_rows(quarter_rows, quarter_ids, experts, capacity)
@@ -227,7 +229,6 @@
     swap = [(0, 1), (1, 0)]
     mine = lax.all_to_all(placed, "chip", split_axis=1, concat_axis=1, tiled=True)
     other = lax.ppermute(mine, "core", swap)
-    hidden_own = lax.dynamic_slice_in_dim(hidden_all, first_row, tok_quarter, 0)
 
     def expert_rows(rows, by_permutes):
         flat = rows.reshape(-1, model_width)

time: 366 us -> 361 us (0.986)
  blocking collectives: 74.6 us -> 55.5 us
  waiting for transfers between devices: 110 us -> 127 us
  local copies, waits for them, and re-layouts: 37.5 us -> 33 us
  starting transfers between devices: 14.8 us -> 19.1 us
  matrix products: 61.4 us -> 57.3 us
    all_to_all x1 -> x0, blocking collectives: 19.9 us -> none  [local(): lax.all_to_all(joined.reshape(n_exp, tok_quarter, joined.shape[1]), 'exp'...]
    all_to_all x1 -> x2, waiting for transfers between devices: 13.7 us -> 29.3 us  [the longest x1 15.9 us: local(): lax.all_to_all(joined.reshape(n_exp, tok_quarter, joined.shape[1]), 'exp'...]
    all_to_all x1 -> x2, starting transfers between devices: 3.52 us -> 7.76 us  [the longest x1 4.25 us: local(): lax.all_to_all(joined.reshape(n_exp, tok_quarter, joined.shape[1]), 'exp'...]
  transfers between devices with their start and end apart: 9 -> 10, of which waited for: 6 -> 7; matrix products, arithmetic and copies ran while one was open for 21% -> 20% of each run, Pallas kernels for 10% -> 10%
where the time goes in v12:
time: 361 us; the launch traced here: 355 us
  waiting for transfers between devices  127 us (35%)
  matrix products  57.3 us (16%)
  blocking collectives  55.5 us (15%)
  Pallas kernels  36.9 us (10%)
  local copies, waits for them, and re-layouts  33 us (9%)
  starting transfers between devices  19.1 us (5%)
  between operations  14.1 us (4%)
  other arithmetic  11.8 us (3%)
    all_to_all x1, blocking collectives, local(): lax.all_to_all(placed, 'chip', split_axis=1, concat_axis=1, tiled=True)  55.5 us
    ppermute x3, waiting for transfers between devices, expert_rows(): lax.ppermute(outgoing, 'exp', [(i, (i + shift) % n_exp) for i in range(n_...  53.2 us
    pallas_call x1, Pallas kernels, entering(): pl.pallas_call(functools.partial(scan_kernel, count), out_shape=(jax.Shap...  36.9 us
    dot_general x2, matrix products, expert_rows(): product = jnp.dot(activated, down_rows, preferred_element_type=jnp.float32)  32.8 us
    all_gather x1, waiting for transfers between devices, local(): lax.all_gather(out_proj, CTX, axis=1, tiled=True)  24.2 us
    all_to_all x1, waiting for transfers between devices, local(): lax.all_to_all(both_halves, 'chip', split_axis=1, concat_axis=1, tiled=True)  17.2 us
    all_to_all x1, waiting for transfers between devices, local(): lax.all_to_all(joined.reshape(n_exp, tok_quarter, joined.shape[1]), 'exp'...  15.9 us
    all_to_all x1, waiting for transfers between devices, local(): lax.all_to_all(jnp.broadcast_to(moe_own[None], (n_exp,) + moe_own.shape),...  13.4 us
  transfers between devices with their start and end apart: 10, of which 7 were waited for; matrix products, arithmetic and copies ran while one was open for 20% of the time, Pallas kernels for 10%

profile of v12, /device:TPU:0, one launch (start us, length us, event | category | flops | bytes accessed | tf_op | source)
XLA Modules:
  0.0 354.9 jit_solution(16872304449107002295)
XLA Ops:
  6.6 0.7 all-gather.2.cloned.1.call-update
  7.3 1.1 copy.57
  8.4 1.0 reduce_window_sum.33
  9.6 0.8 exponential_bitcast_fusion
  10.8 1.2 copy.88
  11.9 0.7 broadcast_in_dim.33.decay_ref
  12.6 36.9 %shard_map.163 = (f32[16,128]{1,0:T(8,128)}, f32[16,8192]{1,0:T(8,128)}) custom-call(f32[16,128]{1,0:T(8,128)} %broadcast_in_dim.33.decay_ref, f32[16,8192]{1,0:T(8,128)} %bitcast.102), custom_call_target="tpu_custom_call" | custom-call | tf_op jit(solution)/shard_map/pallas_call | solution.py:93
  49.5 1.1 copy.76
  50.7 0.8 slice_reduce_fusion
  52.2 1.4 fusion.24
  54.1 24.2 %all-gather.2.cloned.1.call-done = bf16[1024,4096]{1,0:T(8,128)(2,1)} async-done(((bf16[1024,128]{1,0:T(8,128)(2,1)}), bf16[1024,4096]{1,0:T(8,128)(2,1)}) %all-gather.2.cloned.1.call-update) | async-done | bytes 8388624 | tf_op jit(solution)/shard_map/all_gather | solution.py:193
  78.3 4.7 %convolution_convert_fusion.1 = bf16[128,4096]{1,0:T(8,128)(2,1)S(1)} fusion(bf16[1024,4096]{1,0:T(8,128)(2,1)} %all-gather.2.cloned.1.call-done, f32[1024]{0:T(1024)S(1)} %copy-done.10, f32[128,1024]{1,0:T(8,128)S(1)} %copy.58, bf16[128,1024]{1,0:T(8,128)(2,1)S(1)} %copy-done.4), kind=kOutput, calls=%fused_computation.16 | convolution fusion | flops 1075314688 | bytes 10227712 | tf_op jit(solution)/shard_map/dot_general | solution.py:191
  83.2 1.1 pad_maximum_fusion
  84.2 4.2 %all-to-all-start = ((bf16[4,32,4224]{2,1,0:T(8,128)(2,1)}), bf16[4,32,4224]{2,1,0:T(8,128)(2,1)S(1)}, u32[]{:S(2)}, u32[]{:S(2)}) async-start(bf16[4,32,4224]{2,1,0:T(8,128)(2,1)} %pad_maximum_fusion), calls=%async_computation | async-start | bytes 2162688 | tf_op jit(solution)/shard_map/all_to_all | solution.py:200
  88.5 15.9 %all-to-all-done = bf16[4,32,4224]{2,1,0:T(8,128)(2,1)S(1)} async-done(((bf16[4,32,4224]{2,1,0:T(8,128)(2,1)}), bf16[4,32,4224]{2,1,0:T(8,128)(2,1)S(1)}, u32[]{:S(2)}, u32[]{:S(2)}) %all-to-all-start) | async-done | bytes 1081376 | tf_op jit(solution)/shard_map/all_to_all | solution.py:200
  105.2 1.1 broadcast_in_dim.36
  106.3 3.5 all-to-all-start.1
  111.1 13.4 %all-to-all-done.1 = bf16[4,32,4096]{2,1,0:T(8,128)(2,1)S(1)} async-done(((bf16[4,32,4096]{2,1,0:T(8,128)(2,1)}), bf16[4,32,4096]{2,1,0:T(8,128)(2,1)S(1)}, u32[]{:S(2)}, u32[]{:S(2)}) %all-to-all-start.1) | async-done | bytes 1048608 | tf_op jit(solution)/shard_map/all_to_all | solution.py:217
  124.5 3.4 broadcast_in_dim.37
  127.9 2.7 reshape.134
  130.7 1.4 convolution_convert_fusion
  132.0 2.3 copy.60
  134.3 55.5 %all_to_all.20 = bf16[32,16,4096]{2,0,1:T(8,128)(2,1)S(1)} all-to-all(bf16[32,16,4096]{2,0,1:T(8,128)(2,1)S(1)} %copy.60), channel_id=1, replica_groups=mesh['chip'=16,'core'=2,'exp'=4] {'chip'}, dimensions={1} | all-to-all | bytes 8388608 | tf_op jit(solution)/shard_map/all_to_all | solution.py:230
  189.8 4.3 %copy.61 = bf16[32,16,4096]{2,1,0:T(8,128)(2,1)} copy(bf16[32,16,4096]{2,0,1:T(8,128)(2,1)S(1)} %all_to_all.20) | data formatting | bytes 8388608 | tf_op jit(solution)/shard_map/all_to_all | solution.py:230
  194.3 6.4 %fusion.10 = f32[512,896]{1,0:T(8,128)S(1)} fusion(bf16[512,4096]{1,0:T(8,128)(2,1)} %bitcast.10, bf16[1,4096,896]{2,1,0:T(8,128)(2,1)S(1)} %bitcast.114), kind=kOutput, calls=%fused_computation.11 | convolution fusion | flops 3758096384 | bytes 13369344 | tf_op jit(solution)/shard_map/dot_general | solution.py:235
  200.7 16.3 %fusion.12 = bf16[512,4096]{1,0:T(8,128)(2,1)} fusion(bf16[1,896,4096]{2,1,0:T(8,128)(2,1)} %param.31, f32[512,896]{1,0:T(8,128)S(1)} %fusion.10, bf16[512,4096]{1,0:T(8,128)(2,1)} %bitcast.10, bf16[1,4096,896]{2,1,0:T(8,128)(2,1)} %param.30), kind=kOutput, calls=%fused_computation.14 | convolution fusion | flops 7521042432 | bytes 24903680 | tf_op jit(solution)/shard_map/dot_general | solution.py:238
  217.0 6.5 %copy.77 = bf16[4,8,16,4096]{3,1,2,0:T(8,128)(2,1)} copy(bf16[4,8,16,4096]{3,2,1,0:T(8,128)(2,1)} %bitcast.101) | data formatting | bytes 8388608
  223.6 9.8 %fusion.4 = f32[512,896]{1,0:T(8,128)S(1)} fusion(bf16[512,4096]{1,0:T(8,128)(2,1)} %bitcast.15, bf16[1,4096,896]{2,1,0:T(8,128)(2,1)} %param.30), kind=kOutput, calls=%fused_computation.5 | convolution fusion | flops 3758096384 | bytes 13369344 | tf_op jit(solution)/shard_map/dot_general | solution.py:236
  233.4 16.5 %fusion.15 = bf16[512,4096]{1,0:T(8,128)(2,1)} fusion(bf16[1,896,4096]{2,1,0:T(8,128)(2,1)} %param.31, f32[512,896]{1,0:T(8,128)S(1)} %fusion.4, bf16[512,4096]{1,0:T(8,128)(2,1)} %bitcast.15, bf16[1,4096,896]{2,1,0:T(8,128)(2,1)} %param.29), kind=kOutput, calls=%fused_computation.15 | convolution fusion | flops 7521042432 | bytes 24903680 | tf_op jit(solution)/shard_map/dot_general | solution.py:238
  249.9 2.7 constant_dynamic-slice_fusion.4
  252.7 0.6 copy.87
  253.2 0.7 collective-permute-start.1
  253.9 0.6 copy.86
  254.5 2.1 collective-permute-start.2
  256.6 0.6 copy.85
  257.2 0.7 collective-permute-start.3
  257.9 30.5 %collective-permute-done.1 = bf16[8,16,4096]{2,0,1:T(8,128)(2,1)S(1)} collective-permute-done((bf16[8,16,4096]{2,0,1:T(8,128)(2,1)S(1)}, bf16[8,16,4096]{2,0,1:T(8,128)(2,1)S(1)}, u32[]{:S(2)}, u32[]{:S(2)}) %collective-permute-start.1) | collective-permute-done | bytes 1048608 | tf_op jit(solution)/shard_map/ppermute | solution.py:247
  288.4 22.8 %collective-permute-done.2 = bf16[8,16,4096]{2,0,1:T(8,128)(2,1)S(1)} collective-permute-done((bf16[8,16,4096]{2,0,1:T(8,128)(2,1)S(1)}, bf16[8,16,4096]{2,0,1:T(8,128)(2,1)S(1)}, u32[]{:S(2)}, u32[]{:S(2)}) %collective-permute-start.2) | collective-permute-done | bytes 1048608 | tf_op jit(solution)/shard_map/ppermute | solution.py:247
  311.2 1.0 fusion.20
  312.3 2.6 collective-permute-done.4
  314.9 2.5 add_convert_fusion
  317.4 7.0 %all-to-all-start.3 = ((bf16[8,16,4096]{2,0,1:T(8,128)(2,1)}), bf16[8,16,4096]{2,0,1:T(8,128)(2,1)S(1)}, u32[]{:S(2)}, u32[]{:S(2)}) async-start(bf16[8,16,4096]{2,0,1:T(8,128)(2,1)} %add_convert_fusion), calls=%async_computation.3 | async-start | bytes 2097152 | tf_op jit(solution)/shard_map/all_to_all | solution.py:256
  325.3 17.2 %all-to-all-done.3 = bf16[8,16,4096]{2,0,1:T(8,128)(2,1)S(1)} async-done(((bf16[8,16,4096]{2,0,1:T(8,128)(2,1)}), bf16[8,16,4096]{2,0,1:T(8,128)(2,1)S(1)}, u32[]{:S(2)}, u32[]{:S(2)}) %all-to-all-start.3) | async-done | bytes 1048608 | tf_op jit(solution)/shard_map/all_to_all | solution.py:256
  342.5 0.6 copy.68
  343.1 0.9 gather_fusion
  343.9 0.7 reshape.143
  344.6 1.4 multiply_reduce_fusion
  346.0 1.8 add_convert_fusion.1
  (70 shorter events, 5.2 us)
Async XLA Ops:
  6.5 3.8 %copy-start = (bf16[128,128]{1,0:T(8,128)(2,1)S(1)}, bf16[128,128]{1,0:T(8,128)(2,1)}, u32[]{:S(2)}) copy-start(bf16[128,128]{1,0:T(8,128)(2,1)} %param.19) | copy-start | bytes 98308
  6.5 45.6 %copy-start.7 = (f32[16,128]{1,0:T(8,128)S(1)}, f32[16,128]{1,0:T(8,128)}, u32[]{:S(2)}) copy-start(f32[16,128]{1,0:T(8,128)} %param.21) | copy-start | bytes 24580
  6.5 45.0 %copy-start.5 = (bf16[128,128]{1,0:T(8,128)(2,1)S(1)}, bf16[128,128]{1,0:T(8,128)(2,1)}, u32[]{:S(2)}) copy-start(bf16[128,128]{1,0:T(8,128)(2,1)} %param.20) | copy-start | bytes 98308
  6.5 45.1 %copy-start.3 = (f32[16,64,128]{2,1,0:T(8,128)S(1)}, f32[16,64,128]{2,1,0:T(8,128)}, u32[]{:S(2)}) copy-start(f32[16,64,128]{2,1,0:T(8,128)} %param.24) | copy-start | bytes 1572868
  6.5 45.6 %copy-start.11 = (f32[16]{0:T(128)S(1)}, f32[16]{0:T(128)}, u32[]{:S(2)}) copy-start(f32[16]{0:T(128)} %param.23) | copy-start | bytes 196
  6.5 71.8 %all-gather.2.cloned.1.call-start = ((), (), s32[]{:S(2)}) async-start(), calls=%async_computation.5 | async-start | bytes 8650752 | tf_op jit(solution)/shard_map/all_gather | solution.py:193
  12.6 41.2 %copy-start.4 = (bf16[128,1024]{1,0:T(8,128)(2,1)S(1)}, bf16[128,1024]{1,0:T(8,128)(2,1)}, u32[]{:S(2)}) copy-start(bf16[128,1024]{1,0:T(8,128)(2,1)} %param.18) | copy-start | bytes 786436
  49.5 28.9 %copy-start.10 = (f32[1024]{0:T(1024)S(1)}, f32[1024]{0:T(1024)}, u32[]{:S(2)}) copy-start(f32[1024]{0:T(1024)} %param.25) | copy-start | bytes 12292
  83.1 21.7 %copy-start.2 = (bf16[128,4096]{1,0:T(8,128)(2,1)S(1)}, bf16[128,4096]{1,0:T(8,128)(2,1)}, u32[]{:S(2)}) copy-start(bf16[128,4096]{1,0:T(8,128)(2,1)} %param.27) | copy-start | bytes 3145732
  83.1 22.0 %copy-start.6 = (f32[4096]{0:T(1024)S(1)}, f32[4096]{0:T(1024)}, u32[]{:S(2)}) copy-start(f32[4096]{0:T(1024)} %param.28) | copy-start | bytes 49156
  84.2 20.1 %all-to-all-start = ((bf16[4,32,4224]{2,1,0:T(8,128)(2,1)}), bf16[4,32,4224]{2,1,0:T(8,128)(2,1)S(1)}, u32[]{:S(2)}, u32[]{:S(2)}) async-start(bf16[4,32,4224]{2,1,0:T(8,128)(2,1)} %pad_maximum_fusion), calls=%async_computation | async-start | bytes 2162688 | tf_op jit(solution)/shard_map/all_to_all | solution.py:200
  88.5 21.9 %copy-start.8 = (s32[128,2]{0,1:T(2,128)S(1)}, s32[128,2]{0,1:T(2,128)}, u32[]{:S(2)}) copy-start(s32[128,2]{0,1:T(2,128)} %param.32) | copy-start | bytes 3076
  106.3 18.2 %all-to-all-start.1 = ((bf16[4,32,4096]{2,1,0:T(8,128)(2,1)}), bf16[4,32,4096]{2,1,0:T(8,128)(2,1)S(1)}, u32[]{:S(2)}, u32[]{:S(2)}) async-start(bf16[4,32,4096]{2,1,0:T(8,128)(2,1)} %broadcast_in_dim.36), calls=%async_computation.1 | async-start | bytes 2097152 | tf_op jit(solution)/shard_map/all_to_all | solution.py:217
  109.8 205.1 %reduce-scatter.4.cloned.1.call-start = ((), (), s32[]{:S(2)}) async-start(), calls=%async_computation.6 | async-start | bytes 5242880
  134.3 59.9 %slice-start = ((s8[7340032]{0:T(1024)(128)(4,1)}), s8[3145728]{0:T(1024)(128)(4,1)S(1)}, s32[]{:S(2)}) async-start(s8[7340032]{0:T(1024)(128)(4,1)} %bitcast.113), calls=%async_computation.7 | async-start | bytes 6291456
  189.8 4.5 %slice-start.1 = ((s8[7340032]{0:T(1024)(128)(4,1)}), s8[4194304]{0:T(1024)(128)(4,1)S(1)}, s32[]{:S(2)}) async-start(s8[7340032]{0:T(1024)(128)(4,1)} %bitcast.113), calls=%async_computation.8 | async-start | bytes 8388608
  194.1 29.5 %collective-permute-start = (bf16[32,16,4096]{2,1,0:T(8,128)(2,1)}, bf16[32,16,4096]{2,1,0:T(8,128)(2,1)}, u32[]{:S(2)}, u32[]{:S(2)}) collective-permute-start(bf16[32,16,4096]{2,1,0:T(8,128)(2,1)} %copy.61), channel_id=1, source_target_pairs={{0,4},{4,0},{1,5},{5,1},{2,6},{6,2},{3,7},{7,3},{8,12},{12,8},{9,1... | collective-permute-start | bytes 12582920 | tf_op jit(solution)/shard_map/ppermute | solution.py:231
  253.2 35.1 %collective-permute-start.1 = (bf16[8,16,4096]{2,0,1:T(8,128)(2,1)S(1)}, bf16[8,16,4096]{2,0,1:T(8,128)(2,1)S(1)}, u32[]{:S(2)}, u32[]{:S(2)}) collective-permute-start(bf16[8,16,4096]{2,0,1:T(8,128)(2,1)S(1)} %bitcast.107), channel_id=1, source_target_pairs={{0,1},{1,2},{2,3},{3,0},{4,5},{5,6},{6,7},{7,4},{8,9},{9,10},{10,1... | collective-permute-start | bytes 3145736 | tf_op jit(solution)/shard_map/ppermute | solution.py:247
  254.5 56.7 %collective-permute-start.2 = (bf16[8,16,4096]{2,0,1:T(8,128)(2,1)S(1)}, bf16[8,16,4096]{2,0,1:T(8,128)(2,1)S(1)}, u32[]{:S(2)}, u32[]{:S(2)}) collective-permute-start(bf16[8,16,4096]{2,0,1:T(8,128)(2,1)S(1)} %bitcast.108), channel_id=1, source_target_pairs={{0,2},{1,3},{2,0},{3,1},{4,6},{5,7},{6,4},{7,5},{8,10},{9,11},{10,... | collective-permute-start | bytes 3145736 | tf_op jit(solution)/shard_map/ppermute | solution.py:247
  257.2 53.9 %collective-permute-start.3 = (bf16[8,16,4096]{2,0,1:T(8,128)(2,1)S(1)}, bf16[8,16,4096]{2,0,1:T(8,128)(2,1)S(1)}, u32[]{:S(2)}, u32[]{:S(2)}) collective-permute-start(bf16[8,16,4096]{2,0,1:T(8,128)(2,1)S(1)} %bitcast.109), channel_id=1, source_target_pairs={{0,3},{1,0},{2,1},{3,2},{4,7},{5,4},{6,5},{7,6},{8,11},{9,8},{10,9... | collective-permute-start | bytes 3145736 | tf_op jit(solution)/shard_map/ppermute | solution.py:247
  311.2 13.8 %copy-start.9 = (f32[128,2]{0,1:T(2,128)S(1)}, f32[128,2]{0,1:T(2,128)}, u32[]{:S(2)}) copy-start(f32[128,2]{0,1:T(2,128)} %param.33) | copy-start | bytes 3076
  312.2 2.7 collective-permute-start.4
  317.4 25.1 %all-to-all-start.3 = ((bf16[8,16,4096]{2,0,1:T(8,128)(2,1)}), bf16[8,16,4096]{2,0,1:T(8,128)(2,1)S(1)}, u32[]{:S(2)}, u32[]{:S(2)}) async-start(bf16[8,16,4096]{2,0,1:T(8,128)(2,1)} %add_convert_fusion), calls=%async_computation.3 | async-start | bytes 2097152 | tf_op jit(solution)/shard_map/all_to_all | solution.py:256
  343.0 4.8 %copy-start.1 = (bf16[128,128]{1,0:T(8,128)(2,1)S(1)}, bf16[128,128]{1,0:T(8,128)(2,1)}, u32[]{:S(2)}) copy-start(bf16[128,128]{1,0:T(8,128)(2,1)} %param.19) | copy-start | bytes 98308
Sparse Core Ops, SparseCore 0:
  9.6 68.7 all-gather.1
  223.7 67.2 reduce-scatter.3

commit v13 on v12

--- a/solution.py
+++ b/solution.py
@@ -239,7 +239,9 @@
         pieces = product.astype(jnp.bfloat16).reshape(rows.shape)
         if not by_permutes:
             return lax.psum_scatter(pieces, "exp", scatter_dimension=0, tiled=True)
-        pieces = pieces.reshape((n_exp, capacity) + rows.shape[1:])
+        split = rows.shape[1] // 2
+        by_call = lax.psum_scatter(pieces[:, :split], "exp", scatter_dimension=0, tiled=True)
+        pieces = pieces[:, split:].reshape((n_exp, capacity, rows.shape[1] - split) + rows.shape[2:])
         place = lax.axis_index("exp")
         total = lax.dynamic_index_in_dim(pieces, place, 0, False).astype(jnp.float32)
         for shift in range(1, n_exp):
@@ -247,7 +249,7 @@
             total = total + lax.ppermute(
                 outgoing, "exp", [(i, (i + shift) % n_exp) for i in range(n_exp)]
             ).astype(jnp.float32)
-        return total.astype(jnp.bfloat16)
+        return jnp.concatenate([by_call, total.astype(jnp.bfloat16)], axis=1)
 
     own_sum = expert_rows(mine, False)
     partner_sum = expert_rows(other, True)

time: 361 us -> 357 us (0.989); the launches traced: 355 us -> 356 us
  waiting for transfers between devices: 127 us -> 135 us
    reduce_scatter x0 -> x2, waiting for transfers between devices: none -> 14.9 us  [the longest x1 14.9 us: expert_rows(): return lax.psum_scatter(pieces, 'exp', scatter_dimension=0, tiled=True)]
    ppermute x3, waiting for transfers between devices: 53.2 us -> 41.3 us  [expert_rows(): lax.ppermute(outgoing, 'exp', [(i, (i + shift) % n_exp) for i in range(n_...]
    ppermute x1, waiting for transfers between devices: 0.01 us -> 7.16 us  [local(): other = lax.ppermute(mine, 'core', swap)]
    dot_general x1, matrix products: 9.81 us -> 4.52 us  [expert_rows(): up_val = jnp.dot(flat, up_rows, preferred_element_type=jnp.float32)]
    dynamic_slice x4 -> x0, local copies, waits for them, and re-layouts: 4.48 us -> none  [the longest x1 2.73 us: expert_rows(): lax.dynamic_index_in_dim(pieces, place, 0, False).astype(jnp.float32)]
    slice x0 -> x1, local copies, waits for them, and re-layouts: none -> 4 us  [expert_rows(): pieces[:, :split]]
    dot_general x1, matrix products: 6.41 us -> 10.1 us  [expert_rows(): gate_val = jnp.dot(flat, gate_rows, preferred_element_type=jnp.float32)]
    unnamed x33 -> x36, local copies, waits for them, and re-layouts: 10.1 us -> 7.54 us
  transfers between devices with their start and end apart: 10 -> 11, of which waited for: 7 -> 9; matrix products, arithmetic and copies ran while one was open for 20% -> 12% of each run, Pallas kernels for 10% -> 10%
where the time goes in v13:
time: 357 us; the launch traced here: 356 us
  waiting for transfers between devices  135 us (38%)
  matrix products  55.8 us (16%)
  blocking collectives  55.5 us (16%)
  Pallas kernels  36.9 us (10%)
  local copies, waits for them, and re-layouts  30.7 us (9%)
  starting transfers between devices  15.8 us (4%)
  between operations  13.5 us (4%)
  other arithmetic  12.6 us (4%)
    all_to_all x1, blocking collectives, local(): lax.all_to_all(placed, 'chip', split_axis=1, concat_axis=1, tiled=True)  55.5 us
    ppermute x3, waiting for transfers between devices, expert_rows(): lax.ppermute(outgoing, 'exp', [(i, (i + shift) % n_exp) for i in range(n_...  41.3 us
    pallas_call x1, Pallas kernels, entering(): pl.pallas_call(functools.partial(scan_kernel, count), out_shape=(jax.Shap...  36.9 us
    dot_general x2, matrix products, expert_rows(): product = jnp.dot(activated, down_rows, preferred_element_type=jnp.float32)  32.9 us
    all_gather x1, waiting for transfers between devices, local(): lax.all_gather(out_proj, CTX, axis=1, tiled=True)  24.2 us
    all_to_all x1, waiting for transfers between devices, local(): lax.all_to_all(both_halves, 'chip', split_axis=1, concat_axis=1, tiled=True)  17.1 us
    all_to_all x1, waiting for transfers between devices, local(): lax.all_to_all(joined.reshape(n_exp, tok_quarter, joined.shape[1]), 'exp'...  15.9 us
    reduce_scatter x1, waiting for transfers between devices, expert_rows(): return lax.psum_scatter(pieces, 'exp', scatter_dimension=0, tiled=True)  14.9 us
  transfers between devices with their start and end apart: 11, of which 9 were waited for; matrix products, arithmetic and copies ran while one was open for 12% of the time, Pallas kernels for 10%

profile of v13, /device:TPU:0, one launch (start us, length us, event | category | flops | bytes accessed | tf_op | source)
XLA Modules:
  0.0 355.8 jit_solution(490353315523534440)
XLA Ops:
  6.6 0.7 all-gather.2.cloned.1.call-update
  7.3 1.1 copy.39
  8.4 1.0 reduce_window_sum.33
  9.6 0.8 exponential_bitcast_fusion
  10.8 1.2 copy.53
  11.9 0.7 broadcast_in_dim.33.decay_ref
  12.6 36.9 %shard_map.163 = (f32[16,128]{1,0:T(8,128)}, f32[16,8192]{1,0:T(8,128)}) custom-call(f32[16,128]{1,0:T(8,128)} %broadcast_in_dim.33.decay_ref, f32[16,8192]{1,0:T(8,128)} %bitcast.97), custom_call_target="tpu_custom_call" | custom-call | tf_op jit(solution)/shard_map/pallas_call | solution.py:93
  49.5 1.1 copy.51
  50.7 0.8 slice_reduce_fusion
  52.2 1.4 fusion.21
  54.1 24.2 %all-gather.2.cloned.1.call-done = bf16[1024,4096]{1,0:T(8,128)(2,1)} async-done(((bf16[1024,128]{1,0:T(8,128)(2,1)}), bf16[1024,4096]{1,0:T(8,128)(2,1)}) %all-gather.2.cloned.1.call-update) | async-done | bytes 8388624 | tf_op jit(solution)/shard_map/all_gather | solution.py:193
  78.3 4.7 %convolution_convert_fusion.1 = bf16[128,4096]{1,0:T(8,128)(2,1)S(1)} fusion(bf16[1024,4096]{1,0:T(8,128)(2,1)} %all-gather.2.cloned.1.call-done, f32[1024]{0:T(1024)S(1)} %copy-done.12, f32[128,1024]{1,0:T(8,128)S(1)} %copy.40, bf16[128,1024]{1,0:T(8,128)(2,1)S(1)} %copy-done.5), kind=kOutput, calls=%fused_computation.16 | convolution fusion | flops 1075314688 | bytes 10227712 | tf_op jit(solution)/shard_map/dot_general | solution.py:191
  83.2 1.1 pad_maximum_fusion
  84.2 4.2 %all-to-all-start = ((bf16[4,32,4224]{2,1,0:T(8,128)(2,1)}), bf16[4,32,4224]{2,1,0:T(8,128)(2,1)S(1)}, u32[]{:S(2)}, u32[]{:S(2)}) async-start(bf16[4,32,4224]{2,1,0:T(8,128)(2,1)} %pad_maximum_fusion), calls=%async_computation | async-start | bytes 2162688 | tf_op jit(solution)/shard_map/all_to_all | solution.py:200
  88.5 15.9 %all-to-all-done = bf16[4,32,4224]{2,1,0:T(8,128)(2,1)S(1)} async-done(((bf16[4,32,4224]{2,1,0:T(8,128)(2,1)}), bf16[4,32,4224]{2,1,0:T(8,128)(2,1)S(1)}, u32[]{:S(2)}, u32[]{:S(2)}) %all-to-all-start) | async-done | bytes 1081376 | tf_op jit(solution)/shard_map/all_to_all | solution.py:200
  105.2 1.1 broadcast_in_dim.36
  106.3 3.5 all-to-all-start.1
  110.8 13.7 %all-to-all-done.1 = bf16[4,32,4096]{2,1,0:T(8,128)(2,1)S(1)} async-done(((bf16[4,32,4096]{2,1,0:T(8,128)(2,1)}), bf16[4,32,4096]{2,1,0:T(8,128)(2,1)S(1)}, u32[]{:S(2)}, u32[]{:S(2)}) %all-to-all-start.1) | async-done | bytes 1048608 | tf_op jit(solution)/shard_map/all_to_all | solution.py:217
  124.5 3.4 broadcast_in_dim.37
  127.9 2.7 reshape.140
  130.7 1.4 convolution_convert_fusion
  132.0 2.3 copy.42
  134.3 55.5 %all_to_all.20 = bf16[32,16,4096]{2,0,1:T(8,128)(2,1)S(1)} all-to-all(bf16[32,16,4096]{2,0,1:T(8,128)(2,1)S(1)} %copy.42), channel_id=1, replica_groups=mesh['chip'=16,'core'=2,'exp'=4] {'chip'}, dimensions={1} | all-to-all | bytes 8388608 | tf_op jit(solution)/shard_map/all_to_all | solution.py:230
  189.9 2.3 copy.43
  192.2 2.0 copy-done.2
  194.1 7.2 %collective-permute-done = bf16[32,16,4096]{2,1,0:T(8,128)(2,1)S(1)} collective-permute-done((bf16[32,16,4096]{2,1,0:T(8,128)(2,1)S(1)}, bf16[32,16,4096]{2,1,0:T(8,128)(2,1)S(1)}, u32[]{:S(2)}, u32[]{:S(2)}) %collective-permute-start) | collective-permute-done | bytes 4194336 | tf_op jit(solution)/shard_map/ppermute | solution.py:231
  201.3 2.0 copy-done.11
  203.3 4.5 %fusion.4 = f32[512,896]{1,0:T(8,128)S(1)} fusion(bf16[512,4096]{1,0:T(8,128)(2,1)S(1)} %bitcast.106, bf16[1,4096,896]{2,1,0:T(8,128)(2,1)S(1)} %bitcast.105), kind=kOutput, calls=%fused_computation.5 | convolution fusion | flops 3758096384 | bytes 13369344 | tf_op jit(solution)/shard_map/dot_general | solution.py:236
  207.8 16.2 %fusion.15 = bf16[512,4096]{1,0:T(8,128)(2,1)} fusion(bf16[1,896,4096]{2,1,0:T(8,128)(2,1)} %param.31, f32[512,896]{1,0:T(8,128)S(1)} %fusion.4, bf16[512,4096]{1,0:T(8,128)(2,1)} %bitcast.107, bf16[1,4096,896]{2,1,0:T(8,128)(2,1)} %param.29), kind=kOutput, calls=%fused_computation.15 | convolution fusion | flops 7521042432 | bytes 24903680 | tf_op jit(solution)/shard_map/dot_general | solution.py:238
  224.0 4.0 %fusion.67 = (bf16[32,8,4096]{2,1,0:T(8,128)(2,1)}, bf16[32,8,4096]{2,1,0:T(8,128)(2,1)S(1)}) fusion(bf16[32,16,4096]{2,1,0:T(8,128)(2,1)} %bitcast.96), kind=kLoop, calls=%fused_computation.100 | loop fusion | bytes 8388608 | tf_op jit(solution)/shard_map/slice | solution.py:243
  228.3 10.1 %fusion.10 = f32[512,896]{1,0:T(8,128)} fusion(bf16[512,4096]{1,0:T(8,128)(2,1)} %bitcast.94, bf16[1,4096,896]{2,1,0:T(8,128)(2,1)} %param.29), kind=kOutput, calls=%fused_computation.11 | convolution fusion | flops 3758096384 | bytes 13369344 | tf_op jit(solution)/shard_map/dot_general | solution.py:235
  238.4 16.7 %fusion.12 = bf16[512,4096]{1,0:T(8,128)(2,1)} fusion(bf16[1,896,4096]{2,1,0:T(8,128)(2,1)} %param.31, f32[512,896]{1,0:T(8,128)} %fusion.10, bf16[512,4096]{1,0:T(8,128)(2,1)} %bitcast.95, bf16[1,4096,896]{2,1,0:T(8,128)(2,1)} %param.30), kind=kOutput, calls=%fused_computation.14 | convolution fusion | flops 7521042432 | bytes 24903680 | tf_op jit(solution)/shard_map/dot_general | solution.py:238
  255.2 1.1 dynamic-slice_bitcast_fusion.2
  256.9 2.1 collective-permute-start.2
  259.5 18.3 %collective-permute-done.1 = bf16[8,8,4096]{2,1,0:T(8,128)(2,1)} collective-permute-done((bf16[8,8,4096]{2,1,0:T(8,128)(2,1)}, bf16[8,8,4096]{2,1,0:T(8,128)(2,1)}, u32[]{:S(2)}, u32[]{:S(2)}) %collective-permute-start.1) | collective-permute-done | bytes 524320 | tf_op jit(solution)/shard_map/ppermute | solution.py:249
  277.9 18.7 %collective-permute-done.2 = bf16[8,8,4096]{2,1,0:T(8,128)(2,1)} collective-permute-done((bf16[8,8,4096]{2,1,0:T(8,128)(2,1)}, bf16[8,8,4096]{2,1,0:T(8,128)(2,1)}, u32[]{:S(2)}, u32[]{:S(2)}) %collective-permute-start.2) | collective-permute-done | bytes 524320 | tf_op jit(solution)/shard_map/ppermute | solution.py:249
  296.6 4.2 %collective-permute-done.3 = bf16[8,8,4096]{2,1,0:T(8,128)(2,1)} collective-permute-done((bf16[8,8,4096]{2,1,0:T(8,128)(2,1)S(1)}, bf16[8,8,4096]{2,1,0:T(8,128)(2,1)}, u32[]{:S(2)}, u32[]{:S(2)}) %collective-permute-start.3) | collective-permute-done | bytes 524320 | tf_op jit(solution)/shard_map/ppermute | solution.py:249
  300.8 1.6 fusion.25
  302.4 1.1 pad_maximum_fusion.1
  303.7 14.9 %reduce-scatter.3.cloned.1.call-done = bf16[8,16,4096]{2,1,0:T(8,128)(2,1)} async-done(((bf16[32,16,4096]{2,1,0:T(8,128)(2,1)}), bf16[8,16,4096]{2,1,0:T(8,128)(2,1)}) %reduce-scatter.3.cloned.1.call-update) | async-done | bytes 1048592 | tf_op jit(solution)/shard_map/reduce_scatter | solution.py:241
  318.6 1.5 add_convert_fusion
  320.1 1.6 copy.45
  321.6 4.2 %all-to-all-start.3 = ((bf16[8,16,4096]{2,0,1:T(8,128)(2,1)}), bf16[8,16,4096]{2,0,1:T(8,128)(2,1)S(1)}, u32[]{:S(2)}, u32[]{:S(2)}) async-start(bf16[8,16,4096]{2,0,1:T(8,128)(2,1)} %copy.45), calls=%async_computation.5 | async-start | bytes 2097152 | tf_op jit(solution)/shard_map/all_to_all | solution.py:258
  326.8 17.1 %all-to-all-done.3 = bf16[8,16,4096]{2,0,1:T(8,128)(2,1)S(1)} async-done(((bf16[8,16,4096]{2,0,1:T(8,128)(2,1)}), bf16[8,16,4096]{2,0,1:T(8,128)(2,1)S(1)}, u32[]{:S(2)}, u32[]{:S(2)}) %all-to-all-start.3) | async-done | bytes 1048608 | tf_op jit(solution)/shard_map/all_to_all | solution.py:258
  344.5 0.9 gather_fusion
  345.4 0.7 reshape.151
  346.0 1.4 multiply_reduce_fusion
  347.5 1.8 add_convert_fusion.1
  (76 shorter events, 6.8 us)
Async XLA Ops:
  6.5 3.8 %copy-start = (bf16[128,128]{1,0:T(8,128)(2,1)S(1)}, bf16[128,128]{1,0:T(8,128)(2,1)}, u32[]{:S(2)}) copy-start(bf16[128,128]{1,0:T(8,128)(2,1)} %param.19) | copy-start | bytes 98308
  6.5 45.6 %copy-start.8 = (f32[16,128]{1,0:T(8,128)S(1)}, f32[16,128]{1,0:T(8,128)}, u32[]{:S(2)}) copy-start(f32[16,128]{1,0:T(8,128)} %param.21) | copy-start | bytes 24580
  6.5 44.9 %copy-start.6 = (bf16[128,128]{1,0:T(8,128)(2,1)S(1)}, bf16[128,128]{1,0:T(8,128)(2,1)}, u32[]{:S(2)}) copy-start(bf16[128,128]{1,0:T(8,128)(2,1)} %param.20) | copy-start | bytes 98308
  6.5 45.1 %copy-start.4 = (f32[16,64,128]{2,1,0:T(8,128)S(1)}, f32[16,64,128]{2,1,0:T(8,128)}, u32[]{:S(2)}) copy-start(f32[16,64,128]{2,1,0:T(8,128)} %param.24) | copy-start | bytes 1572868
  6.5 45.6 %copy-start.13 = (f32[16]{0:T(128)S(1)}, f32[16]{0:T(128)}, u32[]{:S(2)}) copy-start(f32[16]{0:T(128)} %param.23) | copy-start | bytes 196
  6.5 71.8 %all-gather.2.cloned.1.call-start = ((), (), s32[]{:S(2)}) async-start(), calls=%async_computation.6 | async-start | bytes 8650752 | tf_op jit(solution)/shard_map/all_gather | solution.py:193
  12.6 41.2 %copy-start.5 = (bf16[128,1024]{1,0:T(8,128)(2,1)S(1)}, bf16[128,1024]{1,0:T(8,128)(2,1)}, u32[]{:S(2)}) copy-start(bf16[128,1024]{1,0:T(8,128)(2,1)} %param.18) | copy-start | bytes 786436
  49.5 28.9 %copy-start.12 = (f32[1024]{0:T(1024)S(1)}, f32[1024]{0:T(1024)}, u32[]{:S(2)}) copy-start(f32[1024]{0:T(1024)} %param.25) | copy-start | bytes 12292
  83.1 21.7 %copy-start.3 = (bf16[128,4096]{1,0:T(8,128)(2,1)S(1)}, bf16[128,4096]{1,0:T(8,128)(2,1)}, u32[]{:S(2)}) copy-start(bf16[128,4096]{1,0:T(8,128)(2,1)} %param.27) | copy-start | bytes 3145732
  83.1 22.0 %copy-start.7 = (f32[4096]{0:T(1024)S(1)}, f32[4096]{0:T(1024)}, u32[]{:S(2)}) copy-start(f32[4096]{0:T(1024)} %param.28) | copy-start | bytes 49156
  84.2 20.1 %all-to-all-start = ((bf16[4,32,4224]{2,1,0:T(8,128)(2,1)}), bf16[4,32,4224]{2,1,0:T(8,128)(2,1)S(1)}, u32[]{:S(2)}, u32[]{:S(2)}) async-start(bf16[4,32,4224]{2,1,0:T(8,128)(2,1)} %pad_maximum_fusion), calls=%async_computation | async-start | bytes 2162688 | tf_op jit(solution)/shard_map/all_to_all | solution.py:200
  88.5 21.6 %copy-start.9 = (s32[128,2]{0,1:T(2,128)S(1)}, s32[128,2]{0,1:T(2,128)}, u32[]{:S(2)}) copy-start(s32[128,2]{0,1:T(2,128)} %param.32) | copy-start | bytes 3076
  106.3 18.2 %all-to-all-start.1 = ((bf16[4,32,4096]{2,1,0:T(8,128)(2,1)}), bf16[4,32,4096]{2,1,0:T(8,128)(2,1)S(1)}, u32[]{:S(2)}, u32[]{:S(2)}) async-start(bf16[4,32,4096]{2,1,0:T(8,128)(2,1)} %broadcast_in_dim.36), calls=%async_computation.1 | async-start | bytes 2097152 | tf_op jit(solution)/shard_map/all_to_all | solution.py:217
  109.8 192.6 %reduce-scatter.5.cloned.1.call-start = ((), (), s32[]{:S(2)}) async-start(), calls=%async_computation.8 | async-start | bytes 2621440 | tf_op jit(solution)/shard_map/reduce_scatter | solution.py:243
  134.3 68.9 %slice-start = ((s8[7340032]{0:T(1024)(128)(4,1)}), s8[4194304]{0:T(1024)(128)(4,1)S(1)}, s32[]{:S(2)}) async-start(s8[7340032]{0:T(1024)(128)(4,1)} %bitcast.104), calls=%async_computation.9 | async-start | bytes 8388608
  189.9 13.4 %slice-start.1 = ((s8[7340032]{0:T(1024)(128)(4,1)}), s8[3145728]{0:T(1024)(128)(4,1)S(1)}, s32[]{:S(2)}) async-start(s8[7340032]{0:T(1024)(128)(4,1)} %bitcast.104), calls=%async_computation.10 | async-start | bytes 6291456
  192.2 2.0 copy-start.2
  194.1 7.2 %collective-permute-start = (bf16[32,16,4096]{2,1,0:T(8,128)(2,1)S(1)}, bf16[32,16,4096]{2,1,0:T(8,128)(2,1)S(1)}, u32[]{:S(2)}, u32[]{:S(2)}) collective-permute-start(bf16[32,16,4096]{2,1,0:T(8,128)(2,1)S(1)} %copy.43), channel_id=1, source_target_pairs={{0,4},{4,0},{1,5},{5,1},{2,6},{6,2},{3,7},{7,3},{8,12},{12,8},{9,1... | collective-permute-start | bytes 12582920 | tf_op jit(solution)/shard_map/ppermute | solution.py:231
  201.3 2.0 copy-start.11
  228.0 90.6 %reduce-scatter.3.cloned.1.call-start = ((), (), s32[]{:S(2)}) async-start(), calls=%async_computation.7 | async-start | bytes 5242880 | tf_op jit(solution)/shard_map/reduce_scatter | solution.py:241
  256.3 21.6 %collective-permute-start.1 = (bf16[8,8,4096]{2,1,0:T(8,128)(2,1)}, bf16[8,8,4096]{2,1,0:T(8,128)(2,1)}, u32[]{:S(2)}, u32[]{:S(2)}) collective-permute-start(bf16[8,8,4096]{2,1,0:T(8,128)(2,1)} %get-tuple-element.13), channel_id=1, source_target_pairs={{0,1},{1,2},{2,3},{3,0},{4,5},{5,6},{6,7},{7,4},{8,9},{9,10},{10,1... | collective-permute-start | bytes 1572872 | tf_op jit(solution)/shard_map/ppermute | solution.py:249
  256.9 39.7 %collective-permute-start.2 = (bf16[8,8,4096]{2,1,0:T(8,128)(2,1)}, bf16[8,8,4096]{2,1,0:T(8,128)(2,1)}, u32[]{:S(2)}, u32[]{:S(2)}) collective-permute-start(bf16[8,8,4096]{2,1,0:T(8,128)(2,1)} %get-tuple-element.15), channel_id=1, source_target_pairs={{0,2},{1,3},{2,0},{3,1},{4,6},{5,7},{6,4},{7,5},{8,10},{9,11},{10,... | collective-permute-start | bytes 1572872 | tf_op jit(solution)/shard_map/ppermute | solution.py:249
  258.9 41.9 %collective-permute-start.3 = (bf16[8,8,4096]{2,1,0:T(8,128)(2,1)S(1)}, bf16[8,8,4096]{2,1,0:T(8,128)(2,1)}, u32[]{:S(2)}, u32[]{:S(2)}) collective-permute-start(bf16[8,8,4096]{2,1,0:T(8,128)(2,1)S(1)} %get-tuple-element.14), channel_id=1, source_target_pairs={{0,3},{1,0},{2,1},{3,2},{4,7},{5,4},{6,5},{7,6},{8,11},{9,8},{10,9... | collective-permute-start | bytes 1572872 | tf_op jit(solution)/shard_map/ppermute | solution.py:249
  303.6 22.8 %copy-start.10 = (f32[128,2]{0,1:T(2,128)S(1)}, f32[128,2]{0,1:T(2,128)}, u32[]{:S(2)}) copy-start(f32[128,2]{0,1:T(2,128)} %param.33) | copy-start | bytes 3076
  303.6 15.0 %collective-permute-start.4 = (bf16[8,16,4096]{2,1,0:T(8,128)(2,1)S(1)}, bf16[8,16,4096]{2,1,0:T(8,128)(2,1)S(1)}, u32[]{:S(2)}, u32[]{:S(2)}) collective-permute-start(bf16[8,16,4096]{2,1,0:T(8,128)(2,1)S(1)} %pad_maximum_fusion.1), channel_id=1, source_target_pairs={{0,4},{4,0},{1,5},{5,1},{2,6},{6,2},{3,7},{7,3},{8,12},{12,8},{9,1... | collective-permute-start | bytes 3145736 | tf_op jit(solution)/shard_map/ppermute | solution.py:256
  321.6 22.2 %all-to-all-start.3 = ((bf16[8,16,4096]{2,0,1:T(8,128)(2,1)}), bf16[8,16,4096]{2,0,1:T(8,128)(2,1)S(1)}, u32[]{:S(2)}, u32[]{:S(2)}) async-start(bf16[8,16,4096]{2,0,1:T(8,128)(2,1)} %copy.45), calls=%async_computation.5 | async-start | bytes 2097152 | tf_op jit(solution)/shard_map/all_to_all | solution.py:258
  344.5 4.8 %copy-start.1 = (bf16[128,128]{1,0:T(8,128)(2,1)S(1)}, bf16[128,128]{1,0:T(8,128)(2,1)}, u32[]{:S(2)}) copy-start(bf16[128,128]{1,0:T(8,128)(2,1)} %param.19) | copy-start | bytes 98308
Sparse Core Ops, SparseCore 0:
  9.6 68.7 all-gather.1
  228.1 26.3 reduce-scatter.4
  257.1 61.4 reduce-scatter.2

commit v14 on v13

--- a/solution.py
+++ b/solution.py
@@ -239,7 +239,7 @@
         pieces = product.astype(jnp.bfloat16).reshape(rows.shape)
         if not by_permutes:
             return lax.psum_scatter(pieces, "exp", scatter_dimension=0, tiled=True)
-        split = rows.shape[1] // 2
+        split = rows.shape[1] * 3 // 8
         by_call = lax.psum_scatter(pieces[:, :split], "exp", scatter_dimension=0, tiled=True)
         pieces = pieces[:, split:].reshape((n_exp, capacity, rows.shape[1] - split) + rows.shape[2:])
         place = lax.axis_index("exp")

time: 357 us -> 378 us (1.059); the launches traced: 356 us -> 372 us
  local copies, waits for them, and re-layouts: 30.7 us -> 40.6 us
  waiting for transfers between devices: 135 us -> 139 us
    ppermute x3, waiting for transfers between devices: 41.3 us -> 57.5 us  [expert_rows(): lax.ppermute(outgoing, 'exp', [(i, (i + shift) % n_exp) for i in range(n_...]
    reduce_scatter x2 -> x0, waiting for transfers between devices: 14.9 us -> none  [the longest x1 14.9 us: expert_rows(): return lax.psum_scatter(pieces, 'exp', scatter_dimension=0, tiled=True)]
    unnamed x36 -> x39, local copies, waits for them, and re-layouts: 7.54 us -> 17.5 us
  transfers between devices with their start and end apart: 11 -> 11, of which waited for: 9 -> 10; matrix products, arithmetic and copies ran while one was open for 12% -> 15% of each run, Pallas kernels for 10% -> 10%
where the time goes in v14:
time: 378 us; the launch traced here: 372 us
  waiting for transfers between devices  139 us (37%)
  blocking collectives  55.5 us (15%)
  matrix products  55.4 us (15%)
  local copies, waits for them, and re-layouts  40.6 us (11%)
  Pallas kernels  36.9 us (10%)
  starting transfers between devices  16.4 us (4%)
  other arithmetic  14.7 us (4%)
  between operations  13.8 us (4%)
    ppermute x3, waiting for transfers between devices, expert_rows(): lax.ppermute(outgoing, 'exp', [(i, (i + shift) % n_exp) for i in range(n_...  57.5 us
    all_to_all x1, blocking collectives, local(): lax.all_to_all(placed, 'chip', split_axis=1, concat_axis=1, tiled=True)  55.5 us
    pallas_call x1, Pallas kernels, entering(): pl.pallas_call(functools.partial(scan_kernel, count), out_shape=(jax.Shap...  36.9 us
    dot_general x2, matrix products, expert_rows(): product = jnp.dot(activated, down_rows, preferred_element_type=jnp.float32)  32.7 us
    all_gather x1, waiting for transfers between devices, local(): lax.all_gather(out_proj, CTX, axis=1, tiled=True)  24.2 us
    unnamed x39, local copies, waits for them, and re-layouts  17.5 us
    all_to_all x1, waiting for transfers between devices, local(): lax.all_to_all(both_halves, 'chip', split_axis=1, concat_axis=1, tiled=True)  17.1 us
    all_to_all x1, waiting for transfers between devices, local(): lax.all_to_all(joined.reshape(n_exp, tok_quarter, joined.shape[1]), 'exp'...  15.9 us
  transfers between devices with their start and end apart: 11, of which 10 were waited for; matrix products, arithmetic and copies ran while one was open for 15% of the time, Pallas kernels for 10%

profile of v14, /device:TPU:0, one launch (start us, length us, event | category | flops | bytes accessed | tf_op | source)
XLA Modules:
  0.0 371.9 jit_solution(3639874186553928253)
XLA Ops:
  7.3 1.1 copy.52
  8.4 1.0 reduce_window_sum.33
  9.6 0.8 exponential_bitcast_fusion
  10.8 1.2 copy.78
  12.6 36.9 %shard_map.163 = (f32[16,128]{1,0:T(8,128)}, f32[16,8192]{1,0:T(8,128)}) custom-call(f32[16,128]{1,0:T(8,128)} %broadcast_in_dim.33.decay_ref, f32[16,8192]{1,0:T(8,128)} %bitcast.111), custom_call_target="tpu_custom_call" | custom-call | tf_op jit(solution)/shard_map/pallas_call | solution.py:93
  49.5 1.1 copy.72
  50.7 0.8 slice_reduce_fusion
  52.2 1.4 fusion.24
  54.1 24.2 %all-gather.2.cloned.1.call-done = bf16[1024,4096]{1,0:T(8,128)(2,1)} async-done(((bf16[1024,128]{1,0:T(8,128)(2,1)}), bf16[1024,4096]{1,0:T(8,128)(2,1)}) %all-gather.2.cloned.1.call-update) | async-done | bytes 8388624 | tf_op jit(solution)/shard_map/all_gather | solution.py:193
  78.3 4.7 %convolution_convert_fusion.1 = bf16[128,4096]{1,0:T(8,128)(2,1)S(1)} fusion(bf16[1024,4096]{1,0:T(8,128)(2,1)} %all-gather.2.cloned.1.call-done, f32[1024]{0:T(1024)S(1)} %copy-done.12, f32[128,1024]{1,0:T(8,128)S(1)} %copy.53, bf16[128,1024]{1,0:T(8,128)(2,1)S(1)} %copy-done.5), kind=kOutput, calls=%fused_computation.16 | convolution fusion | flops 1075314688 | bytes 10227712 | tf_op jit(solution)/shard_map/dot_general | solution.py:191
  83.2 1.1 pad_maximum_fusion
  84.2 4.2 %all-to-all-start = ((bf16[4,32,4224]{2,1,0:T(8,128)(2,1)}), bf16[4,32,4224]{2,1,0:T(8,128)(2,1)S(1)}, u32[]{:S(2)}, u32[]{:S(2)}) async-start(bf16[4,32,4224]{2,1,0:T(8,128)(2,1)} %pad_maximum_fusion), calls=%async_computation | async-start | bytes 2162688 | tf_op jit(solution)/shard_map/all_to_all | solution.py:200
  88.5 15.9 %all-to-all-done = bf16[4,32,4224]{2,1,0:T(8,128)(2,1)S(1)} async-done(((bf16[4,32,4224]{2,1,0:T(8,128)(2,1)}), bf16[4,32,4224]{2,1,0:T(8,128)(2,1)S(1)}, u32[]{:S(2)}, u32[]{:S(2)}) %all-to-all-start) | async-done | bytes 1081376 | tf_op jit(solution)/shard_map/all_to_all | solution.py:200
  105.2 1.1 broadcast_in_dim.36
  106.3 3.5 all-to-all-start.1
  111.1 13.3 %all-to-all-done.1 = bf16[4,32,4096]{2,1,0:T(8,128)(2,1)S(1)} async-done(((bf16[4,32,4096]{2,1,0:T(8,128)(2,1)}), bf16[4,32,4096]{2,1,0:T(8,128)(2,1)S(1)}, u32[]{:S(2)}, u32[]{:S(2)}) %all-to-all-start.1) | async-done | bytes 1048608 | tf_op jit(solution)/shard_map/all_to_all | solution.py:217
  124.5 3.4 broadcast_in_dim.37
  127.9 2.7 reshape.140
  130.7 1.4 convolution_convert_fusion
  132.0 2.3 copy.55
  134.3 55.5 %all_to_all.20 = bf16[32,16,4096]{2,0,1:T(8,128)(2,1)S(1)} all-to-all(bf16[32,16,4096]{2,0,1:T(8,128)(2,1)S(1)} %copy.55), channel_id=1, replica_groups=mesh['chip'=16,'core'=2,'exp'=4] {'chip'}, dimensions={1} | all-to-all | bytes 8388608 | tf_op jit(solution)/shard_map/all_to_all | solution.py:230
  189.8 2.3 copy.56
  192.2 1.9 copy-done.2
  194.2 7.1 %collective-permute-done = bf16[32,16,4096]{2,1,0:T(8,128)(2,1)S(1)} collective-permute-done((bf16[32,16,4096]{2,1,0:T(8,128)(2,1)S(1)}, bf16[32,16,4096]{2,1,0:T(8,128)(2,1)S(1)}, u32[]{:S(2)}, u32[]{:S(2)}) %collective-permute-start) | collective-permute-done | bytes 4194336 | tf_op jit(solution)/shard_map/ppermute | solution.py:231
  201.4 2.0 copy-done.11
  203.4 4.5 %fusion.4 = f32[512,896]{1,0:T(8,128)S(1)} fusion(bf16[512,4096]{1,0:T(8,128)(2,1)S(1)} %bitcast.122, bf16[1,4096,896]{2,1,0:T(8,128)(2,1)S(1)} %bitcast.121), kind=kOutput, calls=%fused_computation.5 | convolution fusion | flops 3758096384 | bytes 13369344 | tf_op jit(solution)/shard_map/dot_general | solution.py:236
  207.9 16.2 %fusion.15 = bf16[512,4096]{1,0:T(8,128)(2,1)} fusion(bf16[1,896,4096]{2,1,0:T(8,128)(2,1)} %param.31, f32[512,896]{1,0:T(8,128)S(1)} %fusion.4, bf16[512,4096]{1,0:T(8,128)(2,1)} %bitcast.123, bf16[1,4096,896]{2,1,0:T(8,128)(2,1)} %param.29), kind=kOutput, calls=%fused_computation.15 | convolution fusion | flops 7521042432 | bytes 24903680 | tf_op jit(solution)/shard_map/dot_general | solution.py:238
  224.1 1.7 slice.29
  225.9 2.1 copy.74
  228.2 9.8 %fusion.10 = f32[512,896]{1,0:T(8,128)S(1)} fusion(bf16[512,4096]{1,0:T(8,128)(2,1)} %bitcast.108, bf16[1,4096,896]{2,1,0:T(8,128)(2,1)} %param.29), kind=kOutput, calls=%fused_computation.11 | convolution fusion | flops 3758096384 | bytes 13369344 | tf_op jit(solution)/shard_map/dot_general | solution.py:235
  238.0 16.5 %fusion.12 = bf16[512,4096]{1,0:T(8,128)(2,1)} fusion(bf16[1,896,4096]{2,1,0:T(8,128)(2,1)} %param.31, f32[512,896]{1,0:T(8,128)S(1)} %fusion.10, bf16[512,4096]{1,0:T(8,128)(2,1)} %bitcast.109, bf16[1,4096,896]{2,1,0:T(8,128)(2,1)} %param.30), kind=kOutput, calls=%fused_computation.14 | convolution fusion | flops 7521042432 | bytes 24903680 | tf_op jit(solution)/shard_map/dot_general | solution.py:238
  254.5 6.5 %copy.73 = bf16[4,8,16,4096]{3,1,2,0:T(8,128)(2,1)} copy(bf16[4,8,16,4096]{3,2,1,0:T(8,128)(2,1)} %bitcast.110) | data formatting | bytes 8388608
  261.0 3.5 slice.30
  264.5 1.4 copy.77
  266.0 1.4 dynamic-slice_bitcast_fusion.2
  267.4 0.8 collective-permute-start.1
  268.1 2.0 collective-permute-start.2
  270.9 30.6 %collective-permute-done.1 = bf16[8,10,4096]{2,0,1:T(8,128)(2,1)} collective-permute-done((bf16[8,10,4096]{2,0,1:T(8,128)(2,1)}, bf16[8,10,4096]{2,0,1:T(8,128)(2,1)}, u32[]{:S(2)}, u32[]{:S(2)}) %collective-permute-start.1) | collective-permute-done | bytes 655392 | tf_op jit(solution)/shard_map/ppermute | solution.py:249
  301.5 26.4 %collective-permute-done.2 = bf16[8,10,4096]{2,0,1:T(8,128)(2,1)} collective-permute-done((bf16[8,10,4096]{2,0,1:T(8,128)(2,1)}, bf16[8,10,4096]{2,0,1:T(8,128)(2,1)}, u32[]{:S(2)}, u32[]{:S(2)}) %collective-permute-start.2) | collective-permute-done | bytes 655392 | tf_op jit(solution)/shard_map/ppermute | solution.py:249
  328.5 2.6 fusion.22
  331.1 1.3 pad_maximum_fusion.1
  332.6 2.5 collective-permute-done.4
  335.1 2.5 add_convert_fusion
  337.6 4.0 %all-to-all-start.3 = ((bf16[8,16,4096]{2,0,1:T(8,128)(2,1)}), bf16[8,16,4096]{2,0,1:T(8,128)(2,1)S(1)}, u32[]{:S(2)}, u32[]{:S(2)}) async-start(bf16[8,16,4096]{2,0,1:T(8,128)(2,1)} %add_convert_fusion), calls=%async_computation.3 | async-start | bytes 2097152 | tf_op jit(solution)/shard_map/all_to_all | solution.py:258
  342.5 17.1 %all-to-all-done.3 = bf16[8,16,4096]{2,0,1:T(8,128)(2,1)S(1)} async-done(((bf16[8,16,4096]{2,0,1:T(8,128)(2,1)}), bf16[8,16,4096]{2,0,1:T(8,128)(2,1)S(1)}, u32[]{:S(2)}, u32[]{:S(2)}) %all-to-all-start.3) | async-done | bytes 1048608 | tf_op jit(solution)/shard_map/all_to_all | solution.py:258
  360.3 0.9 gather_fusion
  361.8 1.4 multiply_reduce_fusion
  363.2 1.8 add_convert_fusion.1
  (79 shorter events, 9.5 us)
Async XLA Ops:
  6.5 3.8 %copy-start = (bf16[128,128]{1,0:T(8,128)(2,1)S(1)}, bf16[128,128]{1,0:T(8,128)(2,1)}, u32[]{:S(2)}) copy-start(bf16[128,128]{1,0:T(8,128)(2,1)} %param.19) | copy-start | bytes 98308
  6.5 45.6 %copy-start.8 = (f32[16,128]{1,0:T(8,128)S(1)}, f32[16,128]{1,0:T(8,128)}, u32[]{:S(2)}) copy-start(f32[16,128]{1,0:T(8,128)} %param.21) | copy-start | bytes 24580
  6.5 45.0 %copy-start.6 = (bf16[128,128]{1,0:T(8,128)(2,1)S(1)}, bf16[128,128]{1,0:T(8,128)(2,1)}, u32[]{:S(2)}) copy-start(bf16[128,128]{1,0:T(8,128)(2,1)} %param.20) | copy-start | bytes 98308
  6.5 45.1 %copy-start.4 = (f32[16,64,128]{2,1,0:T(8,128)S(1)}, f32[16,64,128]{2,1,0:T(8,128)}, u32[]{:S(2)}) copy-start(f32[16,64,128]{2,1,0:T(8,128)} %param.24) | copy-start | bytes 1572868
  6.5 45.6 %copy-start.13 = (f32[16]{0:T(128)S(1)}, f32[16]{0:T(128)}, u32[]{:S(2)}) copy-start(f32[16]{0:T(128)} %param.23) | copy-start | bytes 196
  6.5 71.8 %all-gather.2.cloned.1.call-start = ((), (), s32[]{:S(2)}) async-start(), calls=%async_computation.6 | async-start | bytes 8650752 | tf_op jit(solution)/shard_map/all_gather | solution.py:193
  12.6 41.2 %copy-start.5 = (bf16[128,1024]{1,0:T(8,128)(2,1)S(1)}, bf16[128,1024]{1,0:T(8,128)(2,1)}, u32[]{:S(2)}) copy-start(bf16[128,1024]{1,0:T(8,128)(2,1)} %param.18) | copy-start | bytes 786436
  49.5 28.9 %copy-start.12 = (f32[1024]{0:T(1024)S(1)}, f32[1024]{0:T(1024)}, u32[]{:S(2)}) copy-start(f32[1024]{0:T(1024)} %param.25) | copy-start | bytes 12292
  83.1 21.7 %copy-start.3 = (bf16[128,4096]{1,0:T(8,128)(2,1)S(1)}, bf16[128,4096]{1,0:T(8,128)(2,1)}, u32[]{:S(2)}) copy-start(bf16[128,4096]{1,0:T(8,128)(2,1)} %param.27) | copy-start | bytes 3145732
  83.1 22.0 %copy-start.7 = (f32[4096]{0:T(1024)S(1)}, f32[4096]{0:T(1024)}, u32[]{:S(2)}) copy-start(f32[4096]{0:T(1024)} %param.28) | copy-start | bytes 49156
  84.2 20.1 %all-to-all-start = ((bf16[4,32,4224]{2,1,0:T(8,128)(2,1)}), bf16[4,32,4224]{2,1,0:T(8,128)(2,1)S(1)}, u32[]{:S(2)}, u32[]{:S(2)}) async-start(bf16[4,32,4224]{2,1,0:T(8,128)(2,1)} %pad_maximum_fusion), calls=%async_computation | async-start | bytes 2162688 | tf_op jit(solution)/shard_map/all_to_all | solution.py:200
  88.5 21.9 %copy-start.9 = (s32[128,2]{0,1:T(2,128)S(1)}, s32[128,2]{0,1:T(2,128)}, u32[]{:S(2)}) copy-start(s32[128,2]{0,1:T(2,128)} %param.32) | copy-start | bytes 3076
  106.3 18.2 %all-to-all-start.1 = ((bf16[4,32,4096]{2,1,0:T(8,128)(2,1)}), bf16[4,32,4096]{2,1,0:T(8,128)(2,1)S(1)}, u32[]{:S(2)}, u32[]{:S(2)}) async-start(bf16[4,32,4096]{2,1,0:T(8,128)(2,1)} %broadcast_in_dim.36), calls=%async_computation.1 | async-start | bytes 2097152 | tf_op jit(solution)/shard_map/all_to_all | solution.py:217
  109.8 221.3 %reduce-scatter.9.cloned.1.call-start = ((), (), s32[]{:S(2)}) async-start(), calls=%async_computation.8 | async-start | bytes 1966080
  134.3 69.0 %slice-start = ((s8[7340032]{0:T(1024)(128)(4,1)}), s8[4194304]{0:T(1024)(128)(4,1)S(1)}, s32[]{:S(2)}) async-start(s8[7340032]{0:T(1024)(128)(4,1)} %bitcast.120), calls=%async_computation.9 | async-start | bytes 8388608
  189.8 13.5 %slice-start.1 = ((s8[7340032]{0:T(1024)(128)(4,1)}), s8[3145728]{0:T(1024)(128)(4,1)S(1)}, s32[]{:S(2)}) async-start(s8[7340032]{0:T(1024)(128)(4,1)} %bitcast.120), calls=%async_computation.10 | async-start | bytes 6291456
  192.1 1.9 copy-start.2
  194.1 7.3 %collective-permute-start = (bf16[32,16,4096]{2,1,0:T(8,128)(2,1)S(1)}, bf16[32,16,4096]{2,1,0:T(8,128)(2,1)S(1)}, u32[]{:S(2)}, u32[]{:S(2)}) collective-permute-start(bf16[32,16,4096]{2,1,0:T(8,128)(2,1)S(1)} %copy.56), channel_id=1, source_target_pairs={{0,4},{4,0},{1,5},{5,1},{2,6},{6,2},{3,7},{7,3},{8,12},{12,8},{9,1... | collective-permute-start | bytes 12582920 | tf_op jit(solution)/shard_map/ppermute | solution.py:231
  201.4 2.0 copy-start.11
  227.9 104.7 %reduce-scatter.7.cloned.1.call-start = ((), (), s32[]{:S(2)}) async-start(), calls=%async_computation.7 | async-start | bytes 5242880
  267.4 34.1 %collective-permute-start.1 = (bf16[8,10,4096]{2,0,1:T(8,128)(2,1)}, bf16[8,10,4096]{2,0,1:T(8,128)(2,1)}, u32[]{:S(2)}, u32[]{:S(2)}) collective-permute-start(bf16[8,10,4096]{2,0,1:T(8,128)(2,1)} %get-tuple-element.11), channel_id=1, source_target_pairs={{0,1},{1,2},{2,3},{3,0},{4,5},{5,6},{6,7},{7,4},{8,9},{9,10},{10,1... | collective-permute-start | bytes 1966088 | tf_op jit(solution)/shard_map/ppermute | solution.py:249
  268.1 59.7 %collective-permute-start.2 = (bf16[8,10,4096]{2,0,1:T(8,128)(2,1)}, bf16[8,10,4096]{2,0,1:T(8,128)(2,1)}, u32[]{:S(2)}, u32[]{:S(2)}) collective-permute-start(bf16[8,10,4096]{2,0,1:T(8,128)(2,1)} %get-tuple-element.13), channel_id=1, source_target_pairs={{0,2},{1,3},{2,0},{3,1},{4,6},{5,7},{6,4},{7,5},{8,10},{9,11},{10,... | collective-permute-start | bytes 1966088 | tf_op jit(solution)/shard_map/ppermute | solution.py:249
  270.2 58.3 %collective-permute-start.3 = (bf16[8,10,4096]{2,0,1:T(8,128)(2,1)}, bf16[8,10,4096]{2,0,1:T(8,128)(2,1)}, u32[]{:S(2)}, u32[]{:S(2)}) collective-permute-start(bf16[8,10,4096]{2,0,1:T(8,128)(2,1)} %get-tuple-element.12), channel_id=1, source_target_pairs={{0,3},{1,0},{2,1},{3,2},{4,7},{5,4},{6,5},{7,6},{8,11},{9,8},{10,9... | collective-permute-start | bytes 1966088 | tf_op jit(solution)/shard_map/ppermute | solution.py:249
  331.1 11.1 %copy-start.10 = (f32[128,2]{0,1:T(2,128)S(1)}, f32[128,2]{0,1:T(2,128)}, u32[]{:S(2)}) copy-start(f32[128,2]{0,1:T(2,128)} %param.33) | copy-start | bytes 3076
  332.4 2.7 collective-permute-start.4
  337.6 22.1 %all-to-all-start.3 = ((bf16[8,16,4096]{2,0,1:T(8,128)(2,1)}), bf16[8,16,4096]{2,0,1:T(8,128)(2,1)S(1)}, u32[]{:S(2)}, u32[]{:S(2)}) async-start(bf16[8,16,4096]{2,0,1:T(8,128)(2,1)} %add_convert_fusion), calls=%async_computation.3 | async-start | bytes 2097152 | tf_op jit(solution)/shard_map/all_to_all | solution.py:258
  360.3 4.8 %copy-start.1 = (bf16[128,128]{1,0:T(8,128)(2,1)S(1)}, bf16[128,128]{1,0:T(8,128)(2,1)}, u32[]{:S(2)}) copy-start(bf16[128,128]{1,0:T(8,128)(2,1)} %param.19) | copy-start | bytes 98308
Sparse Core Ops, SparseCore 0:
  9.6 68.7 all-gather.1
  228.1 22.3 reduce-scatter.8
  261.1 71.4 reduce-scatter.6
